TPU v7x, 256 devices: a whole 4x4x8 slice. The times are simulated.
256 devices in a mesh: dom: 32 (over x_lo, z, core), kv: 8 (over y, x_hi).
Axes of the slice: x: 4 (x_hi: 2, x_lo: 2; x = x_hi * 2 + x_lo), y: 4, z: 8, core: 2. Of those that a mesh axis runs over, the one named last changes fastest.
Arguments:
- positions: float32 [3, 65536], P(None, ('dom', 'kv')), may hold values from 0 to 60
- features: bfloat16 [65536, 128], P(('dom', 'kv')), may hold values from -6 to 6
- nbr_index: int32 [65536, 64], P(('dom', 'kv')), may hold values from 0 to 4095
- nbr_count: int32 [65536], P(('dom', 'kv')), may hold values from 16 to 64
- nbr_dist: float32 [65536, 64], P(('dom', 'kv')), may hold values from 0.8 to 5
- halo_lists: int32 [32, 2, 1024], P('dom'), may hold values from 0 to 2047
- wave_vectors: float32 [3, 2048], replicated, may hold values from -1.2566371 to 1.2566371, as said below
- w_charge_first: bfloat16 [128, 16], replicated, may hold values from -0.5 to 0.5
- w_long_first: float32 [16, 128], replicated, may hold values from -1.5 to 1.5
- w_value: bfloat16 [128, 128], replicated, may hold values from -0.5 to 0.5
- w_filter: float32 [16, 128], replicated, may hold values from -1.5 to 1.5
- w_charge_second: bfloat16 [128, 16], replicated, may hold values from -0.5 to 0.5
- w_long_second: float32 [16, 128], replicated, may hold values from -1.5 to 1.5
Outputs:
- features_out: bfloat16 [65536, 128], P(('dom', 'kv'))
- forces: float32 [3, 65536], P(None, ('dom', 'kv'))
Inputs may be any that keep to these rules, and one draw needn't show every extreme that they name: `nbr_index`: rows of the atom's own domain table. `nbr_count`: slots at or past the count are padding. `halo_lists`: rows among the domain's own 2048 atoms; repeats may occur. `wave_vectors`: the columns are 2 pi n / 60 for 2048 distinct nonzero integer vectors n of smallest length, no two equal or opposite, in no particular order.
All inputs are finite; a program needn't handle non-finite values.
Results may differ from a plain program's by a relative error of at most 0.0054.
Values may be sent and summed in bfloat16 or wider, within the bound.
No kernel may reach another device: no remote copies, remote signals or barrier semaphores. Data moves between devices by JAX's collectives and lax.ppermute only.
A program may use at most 64 MiB of HBM per device.

v0:
```python
import math

import jax
import jax.numpy as jnp
from jax import lax
from jax.sharding import PartitionSpec as P

HIGHEST_PRECISION = lax.Precision.HIGHEST
LONG_SCALE = 2.0


def passed_along(block, axis, distance):
    devices = range(lax.axis_size(axis))
    route = [((i - distance) % len(devices), i) for i in devices]
    return lax.ppermute(block, axis, route)


def wave_weight(wavevec):
    sq_norm = wavevec[0] * wavevec[0] + wavevec[1] * wavevec[1] + wavevec[2] * wavevec[2]
    return jnp.exp(-0.5 * sq_norm) / (sq_norm + 1.0)


def phase_tables(wavevec, coords):
    phase_angle = (
        wavevec[0][:, None] * coords[0][None, :]
        + wavevec[1][:, None] * coords[1][None, :]
        + wavevec[2][:, None] * coords[2][None, :]
    )
    return (jnp.cos(phase_angle), jnp.sin(phase_angle))


def partial_structure(wavevec, coords, charge):
    cos_table, sin_table = phase_tables(wavevec, coords)
    return (
        jnp.dot(cos_table, charge, precision=HIGHEST_PRECISION, preferred_element_type=jnp.float32),
        jnp.dot(sin_table, charge, precision=HIGHEST_PRECISION, preferred_element_type=jnp.float32),
    )


def partial_project(wavevec, coords, charge, cos_part, sin_part):
    cos_table, sin_table = phase_tables(wavevec, coords)
    weight = wave_weight(wavevec)[:, None]
    cos_weighted = weight * cos_part
    sin_weighted = weight * sin_part
    contract_dims = (((0,), (0,)), ((), ()))
    potential = lax.dot_general(
        cos_table,
        cos_weighted,
        contract_dims,
        precision=HIGHEST_PRECISION,
        preferred_element_type=jnp.float32,
    )
    potential = potential + lax.dot_general(
        sin_table,
        sin_weighted,
        contract_dims,
        precision=HIGHEST_PRECISION,
        preferred_element_type=jnp.float32,
    )
    along_cos = jnp.dot(
        cos_weighted, charge.T, precision=HIGHEST_PRECISION, preferred_element_type=jnp.float32
    )
    along_sin = jnp.dot(
        sin_weighted, charge.T, precision=HIGHEST_PRECISION, preferred_element_type=jnp.float32
    )
    mixed = sin_table * along_cos - cos_table * along_sin
    force = jnp.dot(wavevec, mixed, precision=HIGHEST_PRECISION, preferred_element_type=jnp.float32)
    return (potential, force)


def sliced_range(pos_dom, charge_dom, wave_vectors, total_atoms, atom_dev):
    kv_count = lax.axis_size("kv")
    per_device = wave_vectors.shape[1] // kv_count
    my_waves = lax.dynamic_slice_in_dim(
        wave_vectors, lax.axis_index("kv") * per_device, per_device, 1
    )
    dom_span = pos_dom.shape[1]
    channels = charge_dom.shape[1]
    atom_block = min(512, dom_span)
    block_count = dom_span // atom_block
    coord_blocks = pos_dom.reshape(3, block_count, atom_block).transpose(1, 0, 2)
    charge_blocks = charge_dom.reshape(block_count, atom_block, channels)

    def add_sums(running, member):
        add_cos, add_sin = partial_structure(my_waves, member[0], member[1])
        return ((running[0] + add_cos, running[1] + add_sin), None)

    zero_part = jnp.zeros((per_device, channels), jnp.float32)
    (cos_part, sin_part), _ = lax.scan(
        add_sums, (zero_part, zero_part), (coord_blocks, charge_blocks)
    )
    cos_part, sin_part = lax.psum((cos_part, sin_part), "dom")
    inv_root = 1.0 / math.sqrt(total_atoms)
    cos_part = cos_part * inv_root
    sin_part = sin_part * inv_root
    prefactor = LONG_SCALE / math.sqrt(wave_vectors.shape[1])
    pieces = atom_dev * lax.axis_size("kv") // atom_dev
    coords = pos_dom.reshape(3, pieces, atom_dev).transpose(1, 0, 2)
    charges = charge_dom.reshape(pieces, atom_dev, channels)

    def one_piece(member):
        potential, force = partial_project(my_waves, member[0], member[1], cos_part, sin_part)
        return jnp.concatenate([potential, force.T], axis=1) * prefactor

    summed = lax.psum_scatter(
        lax.map(one_piece, (coords, charges)).reshape(atom_dev * lax.axis_size("kv"), channels + 3),
        "kv",
        scatter_dimension=0,
        tiled=True,
    )
    return (summed[:, :channels], summed[:, channels:].T)


def basis_of(distance, live_count, basis_count):
    centers = 0.5 + 4.5 / (basis_count - 1) * jnp.arange(basis_count, dtype=jnp.int32).astype(
        jnp.float32
    )
    sharpness = ((basis_count - 1) / 4.5) ** 2
    envelope = 0.5 * (jnp.cos(math.pi * distance / 5.0) + 1.0)
    in_list = (
        jnp.arange(distance.shape[1], dtype=jnp.int32)[None, :] < live_count[:, None]
    ).astype(jnp.float32)
    radial = jnp.exp(-sharpness * (distance[..., None] - centers) ** 2)
    return (radial * (envelope * in_list)[..., None]).astype(jnp.bfloat16)


def short_range(hidden, w_value, w_filter, nbr_index, nbr_count, nbr_dist, halo_lists):
    values = jnp.dot(hidden, w_value, preferred_element_type=jnp.float32).astype(jnp.bfloat16)
    v_dom = lax.all_gather(values, "kv", axis=0, tiled=True)
    halo_rows = halo_lists[0]
    from_below = passed_along(v_dom[halo_rows[0]], "dom", 1)
    from_above = passed_along(v_dom[halo_rows[1]], "dom", -1)
    value_table = jnp.concatenate([v_dom, from_below, from_above], axis=0)
    atom_dev = hidden.shape[0]
    neigh_slots = nbr_index.shape[1]
    atom_block = min(64, atom_dev)
    block_count = atom_dev // atom_block

    def one_block(member):
        index_rows, count_rows, dist_rows = member
        picked = value_table[index_rows]
        basis = basis_of(dist_rows, count_rows, w_filter.shape[0])
        contracted = jnp.einsum("ajr,ajf->arf", basis, picked, preferred_element_type=jnp.float32)
        return jnp.einsum("arf,rf->af", contracted, w_filter, precision=HIGHEST_PRECISION)

    message = lax.map(
        one_block,
        (
            nbr_index.reshape(block_count, atom_block, neigh_slots),
            nbr_count.reshape(block_count, atom_block),
            nbr_dist.reshape(block_count, atom_block, neigh_slots),
        ),
    ).reshape(atom_dev, -1)
    return (hidden.astype(jnp.float32) + jax.nn.silu(message)).astype(jnp.bfloat16)


def local(
    positions,
    features,
    nbr_index,
    nbr_count,
    nbr_dist,
    halo_lists,
    wave_vectors,
    w_charge_first,
    w_long_first,
    w_value,
    w_filter,
    w_charge_second,
    w_long_second,
):
    atom_dev = features.shape[0]
    total_atoms = atom_dev * lax.axis_size("dom") * lax.axis_size("kv")
    charge_first = jnp.dot(features, w_charge_first, preferred_element_type=jnp.float32)
    pos_dom, charge_dom = (
        lax.all_gather(positions, "kv", axis=1, tiled=True),
        lax.all_gather(charge_first, "kv", axis=0, tiled=True),
    )
    pot_first, force_first = sliced_range(pos_dom, charge_dom, wave_vectors, total_atoms, atom_dev)
    lifted = jnp.dot(
        pot_first, w_long_first, precision=HIGHEST_PRECISION, preferred_element_type=jnp.float32
    )
    hidden_first = (features.astype(jnp.float32) + jax.nn.silu(lifted)).astype(jnp.bfloat16)
    hidden_second = short_range(
        hidden_first, w_value, w_filter, nbr_index, nbr_count, nbr_dist, halo_lists
    )
    charge_second = jnp.dot(hidden_second, w_charge_second, preferred_element_type=jnp.float32)
    charge_dom = lax.all_gather(charge_second, "kv", axis=0, tiled=True)
    pot_second, force_second = sliced_range(
        pos_dom, charge_dom, wave_vectors, total_atoms, atom_dev
    )
    lifted = jnp.dot(
        pot_second, w_long_second, precision=HIGHEST_PRECISION, preferred_element_type=jnp.float32
    )
    features_out = (hidden_second.astype(jnp.float32) + jax.nn.silu(lifted)).astype(jnp.bfloat16)
    return (features_out, force_first + force_second)


def solution(mesh):
    return jax.shard_map(
        local,
        mesh=mesh,
        in_specs=(
            P(None, ("dom", "kv")),
            P(("dom", "kv"), None),
            P(("dom", "kv"), None),
            P(("dom", "kv")),
            P(("dom", "kv"), None),
            P("dom", None, None),
            P(),
            P(),
            P(),
            P(),
            P(),
            P(),
            P(),
        ),
        out_specs=(P(("dom", "kv"), None), P(None, ("dom", "kv"))),
        check_vma=False,
    )
```

profile of v0, /device:TPU:1, one launch (start us, length us, event | category | flops | bytes accessed | tf_op | source)
XLA Modules:
  0.0 707.3 jit_solution(5735712428069415658)
XLA Ops:
  7.3 29.2 %all_gather.12 = f32[3,2048]{1,0:T(4,128)S(1)} all-gather(f32[3,256]{1,0:T(4,128)} %param.23), channel_id=1, replica_groups=mesh['dom'=32,'kv'=8] {'kv'}, dimensions={1}, use_global_device_ids=true | all-gather | bytes 27648 | tf_op jit(solution)/shard_map/all_gather | solution.py:176
  37.5 28.5 %all_gather.13 = f32[2048,16]{0,1:T(8,128)S(1)} all-gather(f32[256,16]{0,1:T(8,128)S(1)} %fusion.105), channel_id=1, replica_groups=mesh['dom'=32,'kv'=8] {'kv'}, dimensions={0}, use_global_device_ids=true | all-gather | bytes 147456 | tf_op jit(solution)/shard_map/all_gather | solution.py:177
  66.8 19.2 %while.65 = (s32[]{:T(128)}, f32[256,16]{0,1:T(8,128)S(1)}, f32[256,16]{0,1:T(8,128)S(1)}, f32[3,256]{1,0:T(4,128)S(1)}, f32[4,3,512]{2,1,0:T(4,128)S(1)}, /*ind...) while((s32[]{:T(128)}, f32[256,16]{0,1:T(8,128)S(1)}, f32[256,16]{0,1:T(8,128)S(1)}, ...), condition=%wide.region_1.2_spmd.clone, body=%wide.region_0.1_spmd.clone.sunk | while | flops 51658756 | bytes 233624 | solution.py:89
  66.8 2.4 convolution_add_fusion.11
  69.2 2.4 convolution_add_fusion.10
  71.7 2.4 convolution_add_fusion.11
  74.0 2.4 convolution_add_fusion.10
  76.5 2.4 convolution_add_fusion.11
  78.8 2.4 convolution_add_fusion.10
  81.3 2.4 convolution_add_fusion.11
  83.6 2.4 convolution_add_fusion.10
  86.1 115.9 %all-reduce.1 = (f32[256,16]{0,1:T(8,128)S(1)}, f32[256,16]{0,1:T(8,128)S(1)}) all-reduce(f32[256,16]{0,1:T(8,128)S(1)} %get-tuple-element.339, f32[256,16]{0,1:T(8,128)S(1)} %get-tuple-element.340), channel_id=1, replica_groups=mesh['dom'=32,'kv'=8] {'dom'}, use_global_device_ids=true, to_apply=%region_2.3 | all-reduce | flops 8192 | bytes 65536 | tf_op jit(solution)/shard_map/psum | solution.py:92
  202.8 43.6 %while.62 = (s32[]{:T(128)}, f32[8,256,19]{1,0,2:T(8,128)S(1)}, f32[3,256]{1,0:T(4,128)S(1)}, f32[8,3,256]{2,1,0:T(4,128)S(1)}, f32[256,1]{0,1:T(1,128)S(1)}, /*...) while((s32[]{:T(128)}, f32[8,256,19]{1,0,2:T(8,128)S(1)}, ...), condition=%wide.region_5.6_spmd, body=%wide.region_4.5_spmd.sunk | while | flops 54229252 | bytes 1394849 | solution.py:106
  204.2 1.3 fusion.162
  208.4 1.3 convolution_multiply_fusion.6
  209.6 1.3 fusion.162
  213.8 1.3 convolution_multiply_fusion.6
  215.1 1.3 fusion.162
  220.5 1.3 fusion.162
  224.7 1.3 convolution_multiply_fusion.6
  226.0 1.3 fusion.162
  231.4 1.3 fusion.162
  235.6 1.3 convolution_multiply_fusion.6
  236.9 1.3 fusion.162
  242.3 1.3 fusion.162
  247.3 73.5 %reduce-scatter.3.cloned.1.call-done = f32[256,19]{0,1:T(8,128)} async-done(((f32[2048,19]{0,1:T(8,128)}), f32[256,19]{0,1:T(8,128)}) %reduce-scatter.3.cloned.1.call-update) | async-done | bytes 19472 | tf_op jit(solution)/shard_map/reduce_scatter | solution.py:105
  322.1 30.4 %all_gather.14 = bf16[2048,128]{1,0:T(8,128)(2,1)S(1)} all-gather(bf16[256,128]{1,0:T(8,128)(2,1)S(1)} %convolution_convert_fusion), channel_id=1, replica_groups=mesh['dom'=32,'kv'=8] {'kv'}, dimensions={0}, use_global_device_ids=true | all-gather | bytes 589824 | tf_op jit(solution)/shard_map/all_gather | solution.py:129
  352.5 3.2 gather_fusion.1
  355.7 9.8 %collective-permute-start = (bf16[1024,128]{1,0:T(8,128)(2,1)S(1)}, bf16[1024,128]{1,0:T(8,128)(2,1)S(1)}, u32[]{:S(2)}, u32[]{:S(2)}) collective-permute-start(bf16[1024,128]{1,0:T(8,128)(2,1)S(1)} %gather_fusion.1), channel_id=1, source_target_pairs={{248,0},{0,8},{8,16},{16,24},{24,32},{32,40},{40,48},{48,56},{56,6... | collective-permute-start | bytes 786440 | tf_op jit(solution)/shard_map/ppermute | solution.py:15
  365.5 3.2 gather_fusion.2
  369.1 5.4 collective-permute-done.1
  374.7 51.7 %while.63 = (s32[]{:T(128)}, f32[4,64,128]{2,1,0:T(8,128)S(1)}, f32[4,64,64]{2,1,0:T(8,128)S(1)}, s32[4,64]{1,0:T(4,128)S(1)}, s32[4,64,64]{2,1,0:T(8,128)S(1)},...) while((s32[]{:T(128)}, f32[4,64,128]{2,1,0:T(8,128)S(1)}, ...), condition=%wide.region_8.9_spmd, body=%wide.region_7.8_spmd.sunk | while | flops 17395760 | bytes 3449829 | solution.py:146
  374.9 12.1 %gather_fusion = bf16[4096,128]{1,0:T(8,128)(2,1)S(1)} fusion(bf16[4096,128]{1,0:T(8,128)(2,1)S(1)} %get-tuple-element.930, s32[4096]{0:T(1024)S(1)} %broadcast_clamp_fusion.4), kind=kCustom, calls=%fused_computation.clone.1 | custom fusion | bytes 2113536 | tf_op jit(solution)/shard_map/while/body/eval_jaxpr/gather | solution.py:141
  387.9 12.1 %gather_fusion = bf16[4096,128]{1,0:T(8,128)(2,1)S(1)} fusion(bf16[4096,128]{1,0:T(8,128)(2,1)S(1)} %get-tuple-element.930, s32[4096]{0:T(1024)S(1)} %broadcast_clamp_fusion.4), kind=kCustom, calls=%fused_computation.clone.1 | custom fusion | bytes 2113536 | tf_op jit(solution)/shard_map/while/body/eval_jaxpr/gather | solution.py:141
  400.8 12.1 %gather_fusion = bf16[4096,128]{1,0:T(8,128)(2,1)S(1)} fusion(bf16[4096,128]{1,0:T(8,128)(2,1)S(1)} %get-tuple-element.930, s32[4096]{0:T(1024)S(1)} %broadcast_clamp_fusion.4), kind=kCustom, calls=%fused_computation.clone.1 | custom fusion | bytes 2113536 | tf_op jit(solution)/shard_map/while/body/eval_jaxpr/gather | solution.py:141
  413.7 12.1 %gather_fusion = bf16[4096,128]{1,0:T(8,128)(2,1)S(1)} fusion(bf16[4096,128]{1,0:T(8,128)(2,1)S(1)} %get-tuple-element.930, s32[4096]{0:T(1024)S(1)} %broadcast_clamp_fusion.4), kind=kCustom, calls=%fused_computation.clone.1 | custom fusion | bytes 2113536 | tf_op jit(solution)/shard_map/while/body/eval_jaxpr/gather | solution.py:141
  426.6 28.3 %all_gather.15 = f32[2048,16]{0,1:T(8,128)S(1)} all-gather(f32[256,16]{0,1:T(8,128)S(1)} %fusion.106), channel_id=1, replica_groups=mesh['dom'=32,'kv'=8] {'kv'}, dimensions={0}, use_global_device_ids=true | all-gather | bytes 147456 | tf_op jit(solution)/shard_map/all_gather | solution.py:188
  455.0 19.2 %while.66 = (s32[]{:T(128)}, f32[256,16]{0,1:T(8,128)S(1)}, f32[256,16]{0,1:T(8,128)S(1)}, f32[3,256]{1,0:T(4,128)S(1)}, f32[4,3,512]{2,1,0:T(4,128)S(1)}, /*ind...) while((s32[]{:T(128)}, f32[256,16]{0,1:T(8,128)S(1)}, ...), condition=%wide.region_10.11_spmd.clone, body=%wide.region_9.10_spmd.clone.sunk | while | flops 51658756 | bytes 233624 | solution.py:89
  455.1 2.4 convolution_add_fusion.13
  457.4 2.4 convolution_add_fusion.12
  459.9 2.4 convolution_add_fusion.13
  462.2 2.4 convolution_add_fusion.12
  464.7 2.4 convolution_add_fusion.13
  467.1 2.4 convolution_add_fusion.12
  469.5 2.4 convolution_add_fusion.13
  471.9 2.4 convolution_add_fusion.12
  474.2 107.0 %all-reduce = (f32[256,16]{0,1:T(8,128)S(1)}, f32[256,16]{0,1:T(8,128)S(1)}) all-reduce(f32[256,16]{0,1:T(8,128)S(1)} %get-tuple-element.343, f32[256,16]{0,1:T(8,128)S(1)} %get-tuple-element.344), channel_id=1, replica_groups=mesh['dom'=32,'kv'=8] {'dom'}, use_global_device_ids=true, to_apply=%region_11.12 | all-reduce | flops 8192 | bytes 65536 | tf_op jit(solution)/shard_map/psum | solution.py:92
  581.3 43.6 %while.64 = (s32[]{:T(128)}, f32[8,256,19]{1,0,2:T(8,128)S(1)}, f32[3,256]{1,0:T(4,128)S(1)}, f32[8,3,256]{2,1,0:T(4,128)S(1)}, f32[256,1]{0,1:T(1,128)S(1)}, /*...) while((s32[]{:T(128)}, f32[8,256,19]{1,0,2:T(8,128)S(1)}, ...), condition=%wide.region_14.15_spmd, body=%wide.region_13.14_spmd.sunk | while | flops 54229252 | bytes 1394849 | solution.py:106
  582.7 1.3 fusion.177
  586.8 1.3 convolution_multiply_fusion.7
  588.1 1.3 fusion.177
  592.3 1.3 convolution_multiply_fusion.7
  593.6 1.3 fusion.177
  597.7 1.3 convolution_multiply_fusion.7
  599.0 1.3 fusion.177
  603.2 1.3 convolution_multiply_fusion.7
  604.5 1.3 fusion.177
  608.6 1.3 convolution_multiply_fusion.7
  609.9 1.3 fusion.177
  615.4 1.3 fusion.177
  620.8 1.3 fusion.177
  625.7 71.7 %reduce-scatter.5.cloned.1.call-done = f32[256,19]{0,1:T(8,128)} async-done(((f32[2048,19]{0,1:T(8,128)}), f32[256,19]{0,1:T(8,128)}) %reduce-scatter.5.cloned.1.call-update) | async-done | bytes 19472 | tf_op jit(solution)/shard_map/reduce_scatter | solution.py:105
  697.4 1.3 fusion.97
  698.7 1.8 add_convert_fusion
  (281 shorter events, 63.9 us)
Async XLA Ops:
  7.2 314.8 %copy-start = (bf16[128,128]{1,0:T(8,128)(2,1)S(1)}, bf16[128,128]{1,0:T(8,128)(2,1)}, u32[]{:S(2)}) copy-start(bf16[128,128]{1,0:T(8,128)(2,1)} %param.32) | copy-start | bytes 98308
  7.2 313.6 %reduce-scatter.3.cloned.1.call-start = ((), (), s32[]{:S(2)}) async-start(), calls=%async_computation.2 | async-start | bytes 221184 | tf_op jit(solution)/shard_map/reduce_scatter | solution.py:105
  202.8 44.5 %copy-start.4 = (s32[1,2,1024]{2,1,0:T(2,128)S(1)}, s32[1,2,1024]{2,1,0:T(2,128)}, u32[]{:S(2)}) copy-start(s32[1,2,1024]{2,1,0:T(2,128)} %param.28) | copy-start | bytes 24580
  202.8 118.0 %copy-start.3 = (bf16[256,128]{1,0:T(8,128)(2,1)S(1)}, bf16[256,128]{1,0:T(8,128)(2,1)}, u32[]{:S(2)}) copy-start(bf16[256,128]{1,0:T(8,128)(2,1)} %param.24) | copy-start | bytes 196612
  202.8 118.0 %copy-start.7 = (f32[16,128]{1,0:T(8,128)S(1)}, f32[16,128]{1,0:T(8,128)}, u32[]{:S(2)}) copy-start(f32[16,128]{1,0:T(8,128)} %param.31) | copy-start | bytes 24580
  247.2 450.2 %reduce-scatter.5.cloned.1.call-start = ((), (), s32[]{:S(2)}) async-start(), calls=%async_computation.3 | async-start | bytes 221184 | tf_op jit(solution)/shard_map/reduce_scatter | solution.py:105
  355.7 13.1 %copy-start.1 = (f32[256,64]{0,1:T(8,128)S(1)}, f32[256,64]{0,1:T(8,128)}, u32[]{:S(2)}) copy-start(f32[256,64]{0,1:T(8,128)} %param.27) | copy-start | bytes 196612
  355.7 13.2 %copy-start.2 = (s32[256,64]{0,1:T(8,128)S(1)}, s32[256,64]{0,1:T(8,128)}, u32[]{:S(2)}) copy-start(s32[256,64]{0,1:T(8,128)} %param.25) | copy-start | bytes 196612
  355.7 13.3 %copy-start.6 = (s32[256]{0:T(256)S(1)}, s32[256]{0:T(256)}, u32[]{:S(2)}) copy-start(s32[256]{0:T(256)} %param.26) | copy-start | bytes 3076
  355.7 13.4 %collective-permute-start = (bf16[1024,128]{1,0:T(8,128)(2,1)S(1)}, bf16[1024,128]{1,0:T(8,128)(2,1)S(1)}, u32[]{:S(2)}, u32[]{:S(2)}) collective-permute-start(bf16[1024,128]{1,0:T(8,128)(2,1)S(1)} %gather_fusion.1), channel_id=1, source_target_pairs={{248,0},{0,8},{8,16},{16,24},{24,32},{32,40},{40,48},{48,56},{56,6... | collective-permute-start | bytes 786440 | tf_op jit(solution)/shard_map/ppermute | solution.py:15
  368.7 5.9 collective-permute-start.1
  369.1 5.5 copy-start.8
  374.7 51.8 %copy-start.5 = (bf16[128,16]{0,1:T(8,128)(2,1)S(1)}, bf16[128,16]{0,1:T(8,128)(2,1)}, u32[]{:S(2)}) copy-start(bf16[128,16]{0,1:T(8,128)(2,1)} %param.34) | copy-start | bytes 12292
  581.3 117.4 %copy-start.9 = (f32[16,128]{1,0:T(8,128)S(1)}, f32[16,128]{1,0:T(8,128)}, u32[]{:S(2)}) copy-start(f32[16,128]{1,0:T(8,128)} %param.35) | copy-start | bytes 24580
Sparse Core Ops, SparseCore 0:
  247.3 73.4 reduce-scatter.2
  625.8 71.5 reduce-scatter.4
where the time goes:
time: 709 us; the launch traced here: 707 us
  blocking collectives  339 us (48%)
  waiting for transfers between devices  151 us (21%)
  matrix products  126 us (18%)
  local copies, waits for them, and re-layouts  61 us (9%)
  between operations  14.4 us (2%)
  starting transfers between devices  9.91 us (1%)
    psum x2, blocking collectives, sliced_range(): cos_part, sin_part = lax.psum((cos_part, sin_part), 'dom')  223 us
    reduce_scatter x2, waiting for transfers between devices, sliced_range(): lax.psum_scatter(lax.map(one_piece, (coords, charges)).reshape(atom_dev *...  145 us
    gather x4, local copies, waits for them, and re-layouts, one_block(): picked = value_table[index_rows]  48.5 us
    all_gather x1, blocking collectives, short_range(): v_dom = lax.all_gather(values, 'kv', axis=0, tiled=True)  30.4 us
    all_gather x1, blocking collectives, local(): lax.all_gather(positions, 'kv', axis=1, tiled=True)  29.2 us
    all_gather x1, blocking collectives, local(): lax.all_gather(charge_first, 'kv', axis=0, tiled=True)  28.5 us
    all_gather x1, blocking collectives, local(): charge_dom = lax.all_gather(charge_second, 'kv', axis=0, tiled=True)  28.3 us
    dot_general x16, matrix products, partial_project(): jnp.dot(sin_weighted, charge.T, precision=HIGHEST_PRECISION, preferred_el...  20.2 us
  transfers between devices with their start and end apart: 4, of which 3 were waited for; matrix products, arithmetic and copies ran while one was open for 0% of the time, Pallas kernels for 0%

commit v1 on v0

v1 whole, which is shorter than its diff:
```python
import math

import jax
import jax.numpy as jnp
from jax import lax
from jax.experimental import pallas as pl
from jax.experimental.pallas import tpu as pltpu
from jax.sharding import PartitionSpec as P

F32 = jnp.float32
BF16 = jnp.bfloat16
HIGHEST = lax.Precision.HIGHEST
LONG_SCALE = 2.0
CELL = 60.0
EVERY = ("dom", "kv")

COS_COEF = (
    1.0,
    -19.73920440673828,
    64.93911743164062,
    -85.45014190673828,
    60.16762924194336,
    -25.967599868774414,
    6.528658390045166,
)
SIN_COEF = (
    6.2831854820251465,
    -41.34170150756836,
    81.60513305664062,
    -76.70301818847656,
    42.02592849731445,
    -14.899847030639648,
    3.2381374835968018,
)

NN = (((1,), (0,)), ((), ()))
NT = (((1,), (1,)), ((), ()))
TN = (((0,), (0,)), ((), ()))


def horner(coefs, v):
    total = v * coefs[-1] + coefs[-2]
    for coef in coefs[-3::-1]:
        total = total * v + coef
    return total


def dot(a, b, dims=NN, precision=None):
    return lax.dot_general(a, b, dims, precision=precision, preferred_element_type=F32)


def silu(x):
    return x / (1.0 + jnp.exp(-x))


def wave_weight(wave):
    sq_norm = wave[0:1] * wave[0:1] + wave[1:2] * wave[1:2] + wave[2:3] * wave[2:3]
    return jnp.exp(-0.5 * sq_norm) / (sq_norm + 1.0)


def split_rows(x):
    high = x.astype(BF16)
    return jnp.concatenate([high, (x - high.astype(F32)).astype(BF16)], axis=0)


def structure_part(charge_t, cos_ref, sin_ref, wave_ref, part_ref, scale):
    chan = charge_t.shape[0]
    waves = cos_ref.shape[1]
    rows = split_rows(charge_t)
    cos_sum = dot(rows, cos_ref[...])
    sin_sum = dot(rows, sin_ref[...])
    weight = wave_weight(wave_ref[...]) * scale
    cos_sum = (cos_sum[:chan] + cos_sum[chan:]) * weight
    sin_sum = (sin_sum[:chan] + sin_sum[chan:]) * weight
    for t in range(waves // 128):
        lanes = slice(t * 128, (t + 1) * 128)
        part_ref[t * 2 * chan : t * 2 * chan + chan, :] = cos_sum[:, lanes].astype(BF16)
        part_ref[t * 2 * chan + chan : (t + 1) * 2 * chan, :] = sin_sum[:, lanes].astype(BF16)


def table_kernel(pos_ref, feat_ref, wc_ref, wave_ref, cos_ref, sin_ref, part_ref, turns, pad, *, scale):
    atoms, waves = cos_ref.shape
    pad[...] = jnp.zeros_like(pad)
    pad[0:3, :] = pos_ref[...] * (1.0 / CELL)
    columns = jnp.transpose(pad[...])
    for c in range(3):
        turns[c] = jnp.broadcast_to(columns[:, c : c + 1], (atoms, 128))
    rows = 64

    def one_tile(t, carry):
        lanes = pl.ds(pl.multiple_of(t * 128, 128), 128)
        whole = jnp.round(wave_ref[:, lanes] * (CELL / (2.0 * math.pi)))
        for b in range(atoms // rows):
            at = slice(b * rows, (b + 1) * rows)
            u = (
                turns[0, at, :] * whole[0:1]
                + turns[1, at, :] * whole[1:2]
                + turns[2, at, :] * whole[2:3]
            )
            u = u - jnp.round(u)
            v = u * u
            cos_ref[at, lanes] = horner(COS_COEF, v).astype(BF16)
            sin_ref[at, lanes] = (u * horner(SIN_COEF, v)).astype(BF16)
        return carry

    lax.fori_loop(0, waves // 128, one_tile, 0)
    charge_t = dot(wc_ref[...], feat_ref[...], (((0,), (1,)), ((), ())))
    structure_part(charge_t, cos_ref, sin_ref, wave_ref, part_ref, scale)


def fold_kernel(in_ref, out_ref):
    rows = in_ref.shape[0]
    total = jnp.sum(in_ref[...].astype(F32).reshape(rows // 8, 8, 128), axis=0)
    total = total + pltpu.roll(total, 4, 0)
    total = total + pltpu.roll(total, 2, 0)
    out_ref[...] = jnp.broadcast_to(total[None], (rows // 8, 8, 128)).reshape(rows, 128).astype(BF16)


def project(sums_ref, cos_ref, sin_ref, wave_ref, charge_t, with_cos, with_sin):
    chan = charge_t.shape[0]
    waves = cos_ref.shape[1]
    for t in range(waves // 128):
        lanes = slice(t * 128, (t + 1) * 128)
        wave = wave_ref[:, lanes]
        cos_w = sums_ref[t * 2 * chan : t * 2 * chan + chan, :].astype(F32)
        sin_w = sums_ref[t * 2 * chan + chan : (t + 1) * 2 * chan, :].astype(F32)
        with_cos[0:chan, lanes] = cos_w.astype(BF16)
        with_sin[0:chan, lanes] = sin_w.astype(BF16)
        for c in range(3):
            at = slice((c + 1) * chan, (c + 2) * chan)
            with_cos[at, lanes] = (-wave[c : c + 1] * sin_w).astype(BF16)
            with_sin[at, lanes] = (wave[c : c + 1] * cos_w).astype(BF16)
    both = dot(with_cos[...], cos_ref[...], NT) + dot(with_sin[...], sin_ref[...], NT)
    potential_t = both[:chan]
    force = [
        jnp.sum(charge_t * both[(c + 1) * chan : (c + 2) * chan], axis=0, keepdims=True)
        for c in range(3)
    ]
    return potential_t, force


def first_project_kernel(
    sums_ref, cos_ref, sin_ref, wave_ref, feat_ref, wc_ref, wl_ref, wv_ref,
    hidden_ref, values_ref, force_ref, with_cos, with_sin,
):
    charge_t = dot(wc_ref[...], feat_ref[...], (((0,), (1,)), ((), ())))
    potential_t, force = project(sums_ref, cos_ref, sin_ref, wave_ref, charge_t, with_cos, with_sin)
    for c in range(3):
        force_ref[c : c + 1, :] = force[c]
    lifted = dot(potential_t, wl_ref[...], TN, HIGHEST)
    hidden = (feat_ref[...].astype(F32) + silu(lifted)).astype(BF16)
    hidden_ref[...] = hidden
    values = dot(hidden, wv_ref[...]).astype(BF16)
    atoms = values.shape[0]
    for j in range(values_ref.shape[0] // atoms):
        values_ref[j * atoms : (j + 1) * atoms, :] = values


def last_project_kernel(
    sums_ref, cos_ref, sin_ref, wave_ref, hidden_ref, wc_ref, wl_ref, force_in,
    feat_out, force_out, with_cos, with_sin,
):
    charge_t = dot(wc_ref[...], hidden_ref[...], (((0,), (1,)), ((), ())))
    potential_t, force = project(sums_ref, cos_ref, sin_ref, wave_ref, charge_t, with_cos, with_sin)
    for c in range(3):
        force_out[c : c + 1, :] = force_in[c : c + 1, :] + force[c]
    lifted = dot(potential_t, wl_ref[...], TN, HIGHEST)
    feat_out[...] = (hidden_ref[...].astype(F32) + silu(lifted)).astype(BF16)


def halo_kernel(list_ref, values_ref, below_ref, above_ref, table, picked):
    table[...] = values_ref[...].astype(F32)
    count = below_ref.shape[0]
    for side, out_ref in ((0, below_ref), (1, above_ref)):

        def some_rows(b, carry, side=side):
            for j in range(16):
                picked[pl.ds(b * 16 + j, 1), :] = table[pl.ds(list_ref[side, b * 16 + j], 1), :]
            return carry

        lax.fori_loop(0, count // 16, some_rows, 0)
        out_ref[...] = picked[...].astype(BF16)


def weight_kernel(count_ref, dist_ref, wf_ref, out_ref, taper, wide):
    step = pl.program_id(0)
    rows = dist_ref.shape[0]
    basis = wf_ref.shape[0]
    sharpness = ((basis - 1) / 4.5) ** 2
    centers = 0.5 + 4.5 / (basis - 1) * lax.broadcasted_iota(jnp.int32, (basis, 128), 0).astype(F32)
    scaled = dist_ref[...] * 0.1
    taper[...] = 0.5 * (horner(COS_COEF, scaled * scaled) + 1.0)
    wf_high = wf_ref[...].astype(BF16)
    wide[0:basis, :] = wf_high
    wide[basis : 2 * basis, :] = (wf_ref[...] - wf_high.astype(F32)).astype(BF16)
    lane = lax.broadcasted_iota(jnp.int32, (1, 128), 1)

    for j in range(rows):
        atom = (step * rows + j) * 2
        live = jnp.where(lane < 64, count_ref[atom], count_ref[atom + 1] + 64)
        away = jnp.broadcast_to(dist_ref[j : j + 1, :], (basis, 128)) - centers
        height = jnp.where(lane < live, taper[j : j + 1, :], 0.0)
        radial = (jnp.exp(-sharpness * (away * away)) * height).astype(BF16)
        both = jnp.concatenate([radial, radial], axis=0)
        out_ref[j * 128 : (j + 1) * 128, :] = dot(both, wide[...], TN)


def neighbour_kernel(
    index_ref, weight_ref, values_ref, below_ref, above_ref, hidden_ref, wc_ref, cos_ref, sin_ref, wave_ref,
    hidden_out, part_ref, table, message, *, scale,
):
    step = pl.program_id(0)
    own = values_ref.shape[0]
    halo = below_ref.shape[0]
    slots = index_ref.shape[1]
    atoms = weight_ref.shape[0] // slots

    @pl.when(step == 0)
    def _():
        table[0:own, :] = values_ref[...].astype(F32)
        table[own : own + halo, :] = below_ref[...].astype(F32)
        table[own + halo : own + 2 * halo, :] = above_ref[...].astype(F32)

    sub = lax.broadcasted_iota(jnp.int32, (8, 128), 0)

    def one_atom(a, carry):
        atom = step * atoms + a
        total = jnp.zeros((8, 128), F32)
        for s in range(0, slots, 8):
            rows = table[pl.ds(index_ref[atom, s], 8, stride=0), :]
            for j in range(1, 8):
                rows = jnp.where(sub == j, table[pl.ds(index_ref[atom, s + j], 8, stride=0), :], rows)
            at = pl.ds(pl.multiple_of(a * slots + s, 8), 8)
            total = total + rows * weight_ref[at, :]
        message[pl.ds(atom, 1), :] = jnp.sum(total, axis=0, keepdims=True)
        return carry

    lax.fori_loop(0, atoms, one_atom, 0)

    @pl.when(step == pl.num_programs(0) - 1)
    def _():
        hidden = (hidden_ref[...].astype(F32) + silu(message[...])).astype(BF16)
        hidden_out[...] = hidden
        charge_t = dot(wc_ref[...], hidden, (((0,), (1,)), ((), ())))
        structure_part(charge_t, cos_ref, sin_ref, wave_ref, part_ref, scale)


def shape(dims, kind):
    return jax.ShapeDtypeStruct(dims, kind)


def everything(part, name):
    sums = lax.all_to_all(part, EVERY, 0, 0, tiled=True)
    folded = pl.pallas_call(fold_kernel, out_shape=shape(part.shape, BF16), name=name)(sums)
    return lax.all_to_all(folded, EVERY, 0, 0, tiled=True)


def local(
    positions, features, nbr_index, nbr_count, nbr_dist, halo_lists, wave_vectors,
    w_charge_first, w_long_first, w_value, w_filter, w_charge_second, w_long_second,
):
    atoms, hid = features.shape
    chan = w_charge_first.shape[1]
    waves = wave_vectors.shape[1]
    slots = nbr_index.shape[1]
    kv = lax.axis_size("kv")
    doms = lax.axis_size("dom")
    total_atoms = atoms * doms * kv
    scale = LONG_SCALE / math.sqrt(waves) / math.sqrt(total_atoms)
    part_rows = 2 * chan * waves // 128
    halo = halo_lists.shape[2]
    smem = pl.BlockSpec(memory_space=pltpu.SMEM)

    cos_table, sin_table, part = pl.pallas_call(
        lambda *refs: table_kernel(*refs, scale=scale),
        out_shape=(shape((atoms, waves), BF16), shape((atoms, waves), BF16), shape((part_rows, 128), BF16)),
        scratch_shapes=[pltpu.VMEM((3, atoms, 128), F32), pltpu.VMEM((8, atoms), F32)],
        name="tables",
    )(positions, features, w_charge_first, wave_vectors)
    sums = everything(part, "fold_first")
    hidden_first, values, force_first = pl.pallas_call(
        first_project_kernel,
        out_shape=(shape((atoms, hid), BF16), shape((kv * atoms, hid), BF16), shape((3, atoms), F32)),
        scratch_shapes=[pltpu.VMEM((4 * chan, waves), BF16)] * 2,
        name="project_first",
    )(sums, cos_table, sin_table, wave_vectors, features, w_charge_first, w_long_first, w_value)

    v_dom = lax.all_to_all(values, "kv", 0, 0, tiled=True)
    to_next, to_previous = pl.pallas_call(
        halo_kernel,
        in_specs=[smem, pl.BlockSpec(memory_space=pltpu.VMEM)],
        out_shape=(shape((halo, hid), BF16), shape((halo, hid), BF16)),
        scratch_shapes=[pltpu.VMEM((kv * atoms, hid), F32), pltpu.VMEM((halo, hid), F32)],
        name="halo_rows",
    )(halo_lists[0], v_dom)
    from_below = lax.ppermute(to_next, "dom", [(i, (i + 1) % doms) for i in range(doms)])
    from_above = lax.ppermute(to_previous, "dom", [(i, (i - 1) % doms) for i in range(doms)])

    steps = 8
    pair_rows = atoms * slots // 128
    weights = pl.pallas_call(
        weight_kernel,
        grid=(steps,),
        in_specs=[
            smem,
            pl.BlockSpec((pair_rows // steps, 128), lambda i: (i, 0)),
            pl.BlockSpec(w_filter.shape, lambda i: (0, 0)),
        ],
        out_specs=pl.BlockSpec((atoms * slots // steps, hid), lambda i: (i, 0)),
        out_shape=shape((atoms * slots, hid), F32),
        scratch_shapes=[
            pltpu.VMEM((pair_rows // steps, 128), F32),
            pltpu.VMEM((2 * w_filter.shape[0], hid), BF16),
        ],
        cost_estimate=pl.CostEstimate(flops=2 * atoms * slots * hid * 32, bytes_accessed=atoms * slots * hid * 4, transcendentals=atoms * slots * 16),
        name="slot_weights",
    )(nbr_count, nbr_dist.reshape(pair_rows, 128), w_filter)

    whole = lambda a: pl.BlockSpec(a, lambda i: (0, 0))
    hidden_second, part = pl.pallas_call(
        lambda *refs: neighbour_kernel(*refs, scale=scale),
        grid=(steps,),
        in_specs=[
            smem,
            pl.BlockSpec((atoms * slots // steps, hid), lambda i: (i, 0)),
            whole((kv * atoms, hid)),
            whole((halo, hid)),
            whole((halo, hid)),
            whole((atoms, hid)),
            whole((hid, chan)),
            whole((atoms, waves)),
            whole((atoms, waves)),
            whole((3, waves)),
        ],
        out_specs=(whole((atoms, hid)), whole((part_rows, 128))),
        out_shape=(shape((atoms, hid), BF16), shape((part_rows, 128), BF16)),
        scratch_shapes=[pltpu.VMEM((kv * atoms + 2 * halo, hid), F32), pltpu.VMEM((atoms, hid), F32)],
        name="neighbours",
    )(
        nbr_index, weights, v_dom, from_below, from_above, hidden_first,
        w_charge_second, cos_table, sin_table, wave_vectors,
    )
    sums = everything(part, "fold_second")
    return pl.pallas_call(
        last_project_kernel,
        out_shape=(shape((atoms, hid), BF16), shape((3, atoms), F32)),
        scratch_shapes=[pltpu.VMEM((4 * chan, waves), BF16)] * 2,
        name="project_second",
    )(sums, cos_table, sin_table, wave_vectors, hidden_second, w_charge_second, w_long_second, force_first)


def solution(mesh):
    return jax.shard_map(
        local,
        mesh=mesh,
        in_specs=(
            P(None, EVERY), P(EVERY, None), P(EVERY, None), P(EVERY), P(EVERY, None), P("dom", None, None),
            P(), P(), P(), P(), P(), P(), P(),
        ),
        out_specs=(P(EVERY, None), P(None, EVERY)),
        check_vma=False,
    )
```

time: 709 us -> 170 us (0.24)
  blocking collectives: 339 us -> 106 us
  waiting for transfers between devices: 151 us -> 0.01 us
  matrix products: 126 us -> 0 us
  local copies, waits for them, and re-layouts: 61 us -> 6.81 us
  Pallas kernels: 0 us -> 53.7 us
  between operations: 14.4 us -> 0.66 us
  starting transfers between devices: 9.91 us -> 2.61 us
    psum x2 -> x0, blocking collectives: 223 us -> none  [sliced_range(): cos_part, sin_part = lax.psum((cos_part, sin_part), 'dom')]
    reduce_scatter x2 -> x0, waiting for transfers between devices: 145 us -> none  [sliced_range(): lax.psum_scatter(lax.map(one_piece, (coords, charges)).reshape(atom_dev *...]
    dot_general x105 -> x0, matrix products: 126 us -> none  [the longest x16 20.2 us: partial_project(): jnp.dot(sin_weighted, charge.T, precision=HIGHEST_PRECISION, preferred_el...]
    all_gather x4 -> x0, blocking collectives: 116 us -> none  [the longest x1 30.4 us: short_range(): v_dom = lax.all_gather(values, 'kv', axis=0, tiled=True)]
    all_to_all x0 -> x5, blocking collectives: none -> 106 us  [the longest x2 51 us: everything(): sums = lax.all_to_all(part, EVERY, 0, 0, tiled=True)]
    gather x6 -> x0, local copies, waits for them, and re-layouts: 54.9 us -> none  [the longest x4 48.5 us: one_block(): picked = value_table[index_rows]]
    pallas_call x0 -> x8, Pallas kernels: none -> 53.7 us  [the longest x1 24.3 us: local(): pl.pallas_call(lambda *refs: neighbour_kernel(*refs, scale=scale), grid=(...]
    ppermute x2, starting transfers between devices: 9.83 us -> 2.61 us  [the longest x1 2.6 us: local(): lax.ppermute(to_next, 'dom', [(i, (i + 1) % doms) for i in range(doms)])]
  transfers between devices with their start and end apart: 4 -> 2, of which waited for: 3 -> 0; matrix products, arithmetic and copies ran while one was open for 0% -> 3% of each run, Pallas kernels for 0% -> 4%
where the time goes in v1:
time: 170 us; the launch traced here: 169 us
  blocking collectives  106 us (62%)
  Pallas kernels  53.7 us (32%)
  local copies, waits for them, and re-layouts  6.81 us (4%)
  starting transfers between devices  2.61 us (2%)
    all_to_all x2, blocking collectives, everything(): sums = lax.all_to_all(part, EVERY, 0, 0, tiled=True)  51 us
    all_to_all x2, blocking collectives, everything(): return lax.all_to_all(folded, EVERY, 0, 0, tiled=True)  39.8 us
    pallas_call x1, Pallas kernels, local(): pl.pallas_call(lambda *refs: neighbour_kernel(*refs, scale=scale), grid=(...  24.3 us
    all_to_all x1, blocking collectives, local(): v_dom = lax.all_to_all(values, 'kv', 0, 0, tiled=True)  14.9 us
    pallas_call x1, Pallas kernels, local(): pl.pallas_call(weight_kernel, grid=(steps,), in_specs=[smem, pl.BlockSpec...  6.98 us
    pallas_call x1, Pallas kernels, local(): pl.pallas_call(halo_kernel, in_specs=[smem, pl.BlockSpec(memory_space=plt...  6.63 us
    unnamed x8, local copies, waits for them, and re-layouts  6.09 us
    pallas_call x1, Pallas kernels, local(): pl.pallas_call(lambda *refs: table_kernel(*refs, scale=scale), out_shape=...  5.15 us
  transfers between devices with their start and end apart: 2, of which 0 were waited for; matrix products, arithmetic and copies ran while one was open for 3% of the time, Pallas kernels for 4%

profile of v1, /device:TPU:1, one launch (start us, length us, event | category | flops | bytes accessed | tf_op | source)
XLA Modules:
  0.0 169.4 jit_solution(8882037131992676566)
XLA Ops:
  0.6 1.4 copy.22.refs_2_.wc_ref
  2.0 5.1 %tables.1 = (bf16[256,2048]{1,0:T(8,128)(2,1)}, bf16[256,2048]{1,0:T(8,128)(2,1)}, bf16[512,128]{1,0:T(8,128)(2,1)}) custom-call(f32[3,256]{1,0:T(4,128)} %refs_0_.2, bf16[256,128]{1,0:T(8,128)(2,1)} %feat_ref.1, bf16[128,16]{1,0:T(8,128)(2,1)} %copy.22.refs_2_.wc_ref, f32[3,2048]{1,0:T(4,128)} %wave_ref.3), custom_call_target="tpu_custom_call" | custom-call | tf_op jit(solution)/shard_map/tables/pallas_call | solution.py:274
  7.2 28.6 %all_to_all.55 = bf16[256,2,128]{2,1,0:T(2,128)(2,1)} all-to-all(bf16[256,2,128]{2,1,0:T(2,128)(2,1)} %bitcast.21), channel_id=1, replica_groups=mesh['dom'=32,'kv'=8] {'dom','kv'}, dimensions={0} | all-to-all | bytes 262144 | tf_op jit(solution)/shard_map/all_to_all | solution.py:253
  35.8 1.6 fold_first.1
  37.4 19.9 %all_to_all.56 = bf16[256,2,128]{2,1,0:T(2,128)(2,1)} all-to-all(bf16[256,2,128]{2,1,0:T(2,128)(2,1)} %bitcast.17), channel_id=1, replica_groups=mesh['dom'=32,'kv'=8] {'dom','kv'}, dimensions={0} | all-to-all | bytes 262144 | tf_op jit(solution)/shard_map/all_to_all | solution.py:255
  57.3 3.8 %project_first.1 = (bf16[256,128]{1,0:T(8,128)(2,1)}, bf16[2048,128]{1,0:T(8,128)(2,1)}, f32[3,256]{1,0:T(4,128)}) custom-call(bf16[512,128]{1,0:T(8,128)(2,1)} %bitcast.14, bf16[256,2048]{1,0:T(8,128)(2,1)} %get-tuple-element.13.cos_ref.refs_7_, bf16[256,2048]{1,0:T(8,128)(2,1)} %get-tuple-element.14.sin_ref.refs_8_, f32[3,2048]{1,0:T(4,128)} %wave_ref.3, ...), custom_call_target="tpu_custom_call" | custom-call | tf_op jit(solution)/shard_map/project_first/pallas_call | solution.py:281
  61.1 14.9 %all_to_all.57 = bf16[8,256,128]{2,1,0:T(8,128)(2,1)} all-to-all(bf16[8,256,128]{2,1,0:T(8,128)(2,1)} %bitcast.15), channel_id=1, replica_groups=mesh['dom'=32,'kv'=8] {'kv'}, dimensions={0} | all-to-all | bytes 1048576 | tf_op jit(solution)/shard_map/all_to_all | solution.py:288
  76.0 6.6 %halo_rows.1 = (bf16[1024,128]{1,0:T(8,128)(2,1)}, bf16[1024,128]{1,0:T(8,128)(2,1)}) custom-call(s32[2,1024]{1,0:T(2,128)} %bitcast.22, bf16[2048,128]{1,0:T(8,128)(2,1)} %bitcast.11), custom_call_target="tpu_custom_call" | custom-call | tf_op jit(solution)/shard_map/halo_rows/pallas_call | solution.py:289
  82.6 2.6 %collective-permute-start = (bf16[1024,128]{1,0:T(8,128)(2,1)}, bf16[1024,128]{1,0:T(8,128)(2,1)S(1)}, u32[]{:S(2)}, u32[]{:S(2)}) collective-permute-start(bf16[1024,128]{1,0:T(8,128)(2,1)} %get-tuple-element.16), channel_id=1, source_target_pairs={{0,8},{8,16},{16,24},{24,32},{32,40},{40,48},{48,56},{56,64},{64,7... | collective-permute-start | bytes 786440 | tf_op jit(solution)/shard_map/ppermute | solution.py:296
  85.2 0.0 collective-permute-start.1
  85.2 1.4 copy.25.refs_6_.wc_ref
  86.6 1.6 copy.24.refs_0_
  88.2 0.9 copy.21
  89.1 0.7 reshape.17.dist_ref
  89.8 7.0 %slot_weights.1.refs_1_ = f32[16384,128]{1,0:T(8,128)} custom-call(s32[256]{0:T(256)} %count_ref.1, f32[128,128]{1,0:T(8,128)} %reshape.17.dist_ref, f32[16,128]{1,0:T(8,128)} %wf_ref.1), custom_call_target="tpu_custom_call" | custom-call | flops 134217728 | bytes 8388608 | tf_op jit(solution)/shard_map/slot_weights/pallas_call | solution.py:301
  96.8 0.0 collective-permute-done.refs_3_
  96.8 0.0 copy-start
  96.8 0.0 collective-permute-done.1.refs_4_
  96.8 0.0 copy-start.1
  96.8 0.7 copy-done
  97.5 0.1 copy-done.1
  97.6 24.3 %neighbours.1 = (bf16[256,128]{1,0:T(8,128)(2,1)}, bf16[512,128]{1,0:T(8,128)(2,1)}) custom-call(s32[256,64]{1,0:T(8,128)} %copy.24.refs_0_, f32[16384,128]{1,0:T(8,128)} %slot_weights.1.refs_1_, bf16[2048,128]{1,0:T(8,128)(2,1)} %bitcast.12, bf16[1024,128]{1,0:T(8,128)(2,1)} %copy-done, bf16[1024,128]{1,0:T(8,128)(2,1)} %copy-done.1, ...), custom_call_target="tpu_custom_call" | custom-call | tf_op jit(solution)/shard_map/neighbours/pallas_call | solution.py:320
  121.9 22.4 %all_to_all.58 = bf16[256,2,128]{2,1,0:T(2,128)(2,1)} all-to-all(bf16[256,2,128]{2,1,0:T(2,128)(2,1)} %bitcast.20), channel_id=1, replica_groups=mesh['dom'=32,'kv'=8] {'dom','kv'}, dimensions={0} | all-to-all | bytes 262144 | tf_op jit(solution)/shard_map/all_to_all | solution.py:253
  144.3 1.6 fold_second.1
  146.0 19.9 %all_to_all.59 = bf16[256,2,128]{2,1,0:T(2,128)(2,1)} all-to-all(bf16[256,2,128]{2,1,0:T(2,128)(2,1)} %bitcast.19), channel_id=1, replica_groups=mesh['dom'=32,'kv'=8] {'dom','kv'}, dimensions={0} | all-to-all | bytes 262144 | tf_op jit(solution)/shard_map/all_to_all | solution.py:255
  165.9 3.6 %project_second.1 = (bf16[256,128]{1,0:T(8,128)(2,1)}, f32[3,256]{1,0:T(4,128)}) custom-call(bf16[512,128]{1,0:T(8,128)(2,1)} %bitcast.13, bf16[256,2048]{1,0:T(8,128)(2,1)} %get-tuple-element.13.cos_ref.refs_7_, bf16[256,2048]{1,0:T(8,128)(2,1)} %get-tuple-element.14.sin_ref.refs_8_, f32[3,2048]{1,0:T(4,128)} %wave_ref.3, ...), custom_call_target="tpu_custom_call" | custom-call | tf_op jit(solution)/shard_map/project_second/pallas_call | solution.py:344
Async XLA Ops:
  82.6 14.2 %collective-permute-start = (bf16[1024,128]{1,0:T(8,128)(2,1)}, bf16[1024,128]{1,0:T(8,128)(2,1)S(1)}, u32[]{:S(2)}, u32[]{:S(2)}) collective-permute-start(bf16[1024,128]{1,0:T(8,128)(2,1)} %get-tuple-element.16), channel_id=1, source_target_pairs={{0,8},{8,16},{16,24},{24,32},{32,40},{40,48},{48,56},{56,64},{64,7... | collective-permute-start | bytes 786440 | tf_op jit(solution)/shard_map/ppermute | solution.py:296
  85.2 11.6 %collective-permute-start.1 = (bf16[1024,128]{1,0:T(8,128)(2,1)}, bf16[1024,128]{1,0:T(8,128)(2,1)S(1)}, u32[]{:S(2)}, u32[]{:S(2)}) collective-permute-start(bf16[1024,128]{1,0:T(8,128)(2,1)} %get-tuple-element.17), channel_id=1, source_target_pairs={{0,248},{8,0},{16,8},{24,16},{32,24},{40,32},{48,40},{56,48},{64,5... | collective-permute-start | bytes 786440 | tf_op jit(solution)/shard_map/ppermute | solution.py:297
  96.8 0.7 copy-start
  96.8 0.8 copy-start.1

commit v2 on v1

--- a/solution.py
+++ b/solution.py
@@ -104,7 +104,7 @@
         return carry
 
     lax.fori_loop(0, waves // 128, one_tile, 0)
-    charge_t = dot(wc_ref[...], feat_ref[...], (((0,), (1,)), ((), ())))
+    charge_t = dot(wc_ref[...], feat_ref[...], NT)
     structure_part(charge_t, cos_ref, sin_ref, wave_ref, part_ref, scale)
 
 
@@ -143,7 +143,7 @@
     sums_ref, cos_ref, sin_ref, wave_ref, feat_ref, wc_ref, wl_ref, wv_ref,
     hidden_ref, values_ref, force_ref, with_cos, with_sin,
 ):
-    charge_t = dot(wc_ref[...], feat_ref[...], (((0,), (1,)), ((), ())))
+    charge_t = dot(wc_ref[...], feat_ref[...], NT)
     potential_t, force = project(sums_ref, cos_ref, sin_ref, wave_ref, charge_t, with_cos, with_sin)
     for c in range(3):
         force_ref[c : c + 1, :] = force[c]
@@ -160,7 +160,7 @@
     sums_ref, cos_ref, sin_ref, wave_ref, hidden_ref, wc_ref, wl_ref, force_in,
     feat_out, force_out, with_cos, with_sin,
 ):
-    charge_t = dot(wc_ref[...], hidden_ref[...], (((0,), (1,)), ((), ())))
+    charge_t = dot(wc_ref[...], hidden_ref[...], NT)
     potential_t, force = project(sums_ref, cos_ref, sin_ref, wave_ref, charge_t, with_cos, with_sin)
     for c in range(3):
         force_out[c : c + 1, :] = force_in[c : c + 1, :] + force[c]
@@ -168,52 +168,82 @@
     feat_out[...] = (hidden_ref[...].astype(F32) + silu(lifted)).astype(BF16)
 
 
-def halo_kernel(list_ref, values_ref, below_ref, above_ref, table, picked):
+def row_tile(table, rows, bits):
+    tiles = [table[pl.ds(row, 8, stride=0), :] for row in rows]
+    for bit in bits:
+        tiles = [jnp.where(bit, odd, even) for even, odd in zip(tiles[::2], tiles[1::2])]
+    return tiles[0]
+
+
+def sublane_bits():
+    sub = lax.broadcasted_iota(jnp.int32, (8, 128), 0)
+    return [(sub & bit) != 0 for bit in (1, 2, 4)]
+
+
+def halo_kernel(*refs):
+    lists, (values_ref, below_ref, above_ref, table, picked) = refs[:-5], refs[-5:]
     table[...] = values_ref[...].astype(F32)
-    count = below_ref.shape[0]
-    for side, out_ref in ((0, below_ref), (1, above_ref)):
-
-        def some_rows(b, carry, side=side):
-            for j in range(16):
-                picked[pl.ds(b * 16 + j, 1), :] = table[pl.ds(list_ref[side, b * 16 + j], 1), :]
-            return carry
-
-        lax.fori_loop(0, count // 16, some_rows, 0)
-        out_ref[...] = picked[...].astype(BF16)
-
-
-def weight_kernel(count_ref, dist_ref, wf_ref, out_ref, taper, wide):
+    bits = sublane_bits()
+
+    def some_rows(g, carry):
+        first = g * 8
+        at = [[first + j for j in range(8)] for side in (0, 1)]
+        for b, list_ref in enumerate(lists):
+            for side in (0, 1):
+                rows = [list_ref[side, lane] for lane in at[side]]
+                picked[side, pl.ds(pl.multiple_of(b * 128 + first, 8), 8), :] = row_tile(table, rows, bits)
+        return carry
+
+    lax.fori_loop(0, 16, some_rows, 0)
+    below_ref[...] = picked[0].astype(BF16)
+    above_ref[...] = picked[1].astype(BF16)
+
+
+def weight_kernel(count_ref, dist_ref, wf_ref, out_ref, turned, near, taper, wide):
     step = pl.program_id(0)
-    rows = dist_ref.shape[0]
+    slots, atoms = dist_ref.shape
     basis = wf_ref.shape[0]
+    pairs = out_ref.shape[0] // 2
     sharpness = ((basis - 1) / 4.5) ** 2
-    centers = 0.5 + 4.5 / (basis - 1) * lax.broadcasted_iota(jnp.int32, (basis, 128), 0).astype(F32)
-    scaled = dist_ref[...] * 0.1
-    taper[...] = 0.5 * (horner(COS_COEF, scaled * scaled) + 1.0)
-    wf_high = wf_ref[...].astype(BF16)
-    wide[0:basis, :] = wf_high
-    wide[basis : 2 * basis, :] = (wf_ref[...] - wf_high.astype(F32)).astype(BF16)
-    lane = lax.broadcasted_iota(jnp.int32, (1, 128), 1)
-
-    for j in range(rows):
-        atom = (step * rows + j) * 2
-        live = jnp.where(lane < 64, count_ref[atom], count_ref[atom + 1] + 64)
-        away = jnp.broadcast_to(dist_ref[j : j + 1, :], (basis, 128)) - centers
-        height = jnp.where(lane < live, taper[j : j + 1, :], 0.0)
-        radial = (jnp.exp(-sharpness * (away * away)) * height).astype(BF16)
-        both = jnp.concatenate([radial, radial], axis=0)
-        out_ref[j * 128 : (j + 1) * 128, :] = dot(both, wide[...], TN)
-
-
-def neighbour_kernel(
-    index_ref, weight_ref, values_ref, below_ref, above_ref, hidden_ref, wc_ref, cos_ref, sin_ref, wave_ref,
-    hidden_out, part_ref, table, message, *, scale,
-):
+
+    def paired(block):
+        turned[...] = jnp.transpose(block)
+        return jnp.concatenate(
+            [turned[pl.ds(0, atoms // 2, stride=2), :], turned[pl.ds(1, atoms // 2, stride=2), :]], axis=1
+        )
+
+    @pl.when(step == 0)
+    def _():
+        dist = dist_ref[...]
+        scaled = dist * 0.1
+        height = 0.5 * (horner(COS_COEF, scaled * scaled) + 1.0)
+        slot = lax.broadcasted_iota(jnp.int32, (slots, atoms), 0)
+        near[...] = paired(dist)
+        taper[...] = paired(jnp.where(slot < count_ref[...], height, 0.0))
+        wf_high = wf_ref[...].astype(BF16)
+        wide[0:basis, :] = wf_high
+        wide[basis : 2 * basis, :] = (wf_ref[...] - wf_high.astype(F32)).astype(BF16)
+
+    centers = 0.5 + 4.5 / (basis - 1) * lax.broadcasted_iota(jnp.int32, (basis, 2 * slots), 0).astype(F32)
+    for p in range(pairs):
+        row = pl.ds(step * pairs + p, 1)
+        away = near[row, :] - centers
+        radial = (jnp.exp(-sharpness * (away * away)) * taper[row, :]).astype(BF16)
+        both = dot(jnp.concatenate([radial, radial], axis=0), wide[...], TN)
+        out_ref[2 * p] = both[:slots]
+        out_ref[2 * p + 1] = both[slots:]
+
+
+def neighbour_kernel(*refs, scale):
+    index_refs = refs[:-13]
+    (
+        weight_ref, values_ref, below_ref, above_ref, hidden_ref, wc_ref, cos_ref, sin_ref, wave_ref,
+        hidden_out, part_ref, table, sums,
+    ) = refs[-13:]
     step = pl.program_id(0)
     own = values_ref.shape[0]
     halo = below_ref.shape[0]
-    slots = index_ref.shape[1]
-    atoms = weight_ref.shape[0] // slots
+    halves, atoms, slots, _ = weight_ref.shape
 
     @pl.when(step == 0)
     def _():
@@ -221,27 +251,29 @@
         table[own : own + halo, :] = below_ref[...].astype(F32)
         table[own + halo : own + 2 * halo, :] = above_ref[...].astype(F32)
 
-    sub = lax.broadcasted_iota(jnp.int32, (8, 128), 0)
-
-    def one_atom(a, carry):
-        atom = step * atoms + a
-        total = jnp.zeros((8, 128), F32)
-        for s in range(0, slots, 8):
-            rows = table[pl.ds(index_ref[atom, s], 8, stride=0), :]
-            for j in range(1, 8):
-                rows = jnp.where(sub == j, table[pl.ds(index_ref[atom, s + j], 8, stride=0), :], rows)
-            at = pl.ds(pl.multiple_of(a * slots + s, 8), 8)
-            total = total + rows * weight_ref[at, :]
-        message[pl.ds(atom, 1), :] = jnp.sum(total, axis=0, keepdims=True)
-        return carry
-
-    lax.fori_loop(0, atoms, one_atom, 0)
+    bits = sublane_bits()
+    for half in range(halves):
+
+        def one_atom(a, carry, half=half):
+            lane = step * atoms + a
+            total = jnp.zeros((8, 128), F32)
+            for b in range(slots // 8):
+                rows = [index_refs[b * halves + half][s, lane] for s in range(8)]
+                total = total + row_tile(table, rows, bits) * weight_ref[half, a, 8 * b : 8 * b + 8, :]
+            sums[pl.ds(pl.multiple_of((half * 128 + lane) * 8, 8), 8), :] = total
+            return carry
+
+        lax.fori_loop(0, atoms, one_atom, 0)
 
     @pl.when(step == pl.num_programs(0) - 1)
     def _():
-        hidden = (hidden_ref[...].astype(F32) + silu(message[...])).astype(BF16)
+        count = hidden_ref.shape[0]
+        message = sums[pl.ds(0, count, stride=8), :]
+        for k in range(1, 8):
+            message = message + sums[pl.ds(k, count, stride=8), :]
+        hidden = (hidden_ref[...].astype(F32) + silu(message)).astype(BF16)
         hidden_out[...] = hidden
-        charge_t = dot(wc_ref[...], hidden, (((0,), (1,)), ((), ())))
+        charge_t = dot(wc_ref[...], hidden, NT)
         structure_part(charge_t, cos_ref, sin_ref, wave_ref, part_ref, scale)
 
 
@@ -269,7 +301,11 @@
     scale = LONG_SCALE / math.sqrt(waves) / math.sqrt(total_atoms)
     part_rows = 2 * chan * waves // 128
     halo = halo_lists.shape[2]
-    smem = pl.BlockSpec(memory_space=pltpu.SMEM)
+    w_charge_first = w_charge_first.T
+    w_charge_second = w_charge_second.T
+    lists = halo_lists[0]
+    index_t = nbr_index.T
+    dist_t = nbr_dist.T
 
     cos_table, sin_table, part = pl.pallas_call(
         lambda *refs: table_kernel(*refs, scale=scale),
@@ -288,57 +324,69 @@
     v_dom = lax.all_to_all(values, "kv", 0, 0, tiled=True)
     to_next, to_previous = pl.pallas_call(
         halo_kernel,
-        in_specs=[smem, pl.BlockSpec(memory_space=pltpu.VMEM)],
+        grid=(1,),
+        in_specs=[
+            pl.BlockSpec((2, 128), lambda i, b=b: (0, b), memory_space=pltpu.SMEM) for b in range(halo // 128)
+        ] + [pl.BlockSpec((kv * atoms, hid), lambda i: (0, 0))],
+        out_specs=(pl.BlockSpec((halo, hid), lambda i: (0, 0)), pl.BlockSpec((halo, hid), lambda i: (0, 0))),
         out_shape=(shape((halo, hid), BF16), shape((halo, hid), BF16)),
-        scratch_shapes=[pltpu.VMEM((kv * atoms, hid), F32), pltpu.VMEM((halo, hid), F32)],
+        scratch_shapes=[pltpu.VMEM((kv * atoms, hid), F32), pltpu.VMEM((2, halo, hid), F32)],
         name="halo_rows",
-    )(halo_lists[0], v_dom)
+    )(*[lists] * (halo // 128), v_dom)
     from_below = lax.ppermute(to_next, "dom", [(i, (i + 1) % doms) for i in range(doms)])
     from_above = lax.ppermute(to_previous, "dom", [(i, (i - 1) % doms) for i in range(doms)])
 
     steps = 8
-    pair_rows = atoms * slots // 128
+    halves = atoms // 128
+    whole = lambda dims: pl.BlockSpec(dims, lambda i: (0, 0))
     weights = pl.pallas_call(
         weight_kernel,
         grid=(steps,),
         in_specs=[
-            smem,
-            pl.BlockSpec((pair_rows // steps, 128), lambda i: (i, 0)),
-            pl.BlockSpec(w_filter.shape, lambda i: (0, 0)),
+            whole((1, atoms)),
+            whole((slots, atoms)),
+            whole(w_filter.shape),
         ],
-        out_specs=pl.BlockSpec((atoms * slots // steps, hid), lambda i: (i, 0)),
-        out_shape=shape((atoms * slots, hid), F32),
+        out_specs=pl.BlockSpec((atoms // steps, slots, hid), lambda i: (i, 0, 0)),
+        out_shape=shape((atoms, slots, hid), F32),
         scratch_shapes=[
-            pltpu.VMEM((pair_rows // steps, 128), F32),
+            pltpu.VMEM((atoms, slots), F32),
+            pltpu.VMEM((atoms // 2, 2 * slots), F32),
+            pltpu.VMEM((atoms // 2, 2 * slots), F32),
             pltpu.VMEM((2 * w_filter.shape[0], hid), BF16),
         ],
-        cost_estimate=pl.CostEstimate(flops=2 * atoms * slots * hid * 32, bytes_accessed=atoms * slots * hid * 4, transcendentals=atoms * slots * 16),
+        cost_estimate=pl.CostEstimate(
+            flops=2 * atoms * slots * hid * 32,
+            bytes_accessed=atoms * slots * hid * 4,
+            transcendentals=atoms * slots * 16,
+        ),
         name="slot_weights",
-    )(nbr_count, nbr_dist.reshape(pair_rows, 128), w_filter)
-
-    whole = lambda a: pl.BlockSpec(a, lambda i: (0, 0))
+    )(nbr_count.reshape(1, atoms), dist_t, w_filter)
+
+    blocks = [(b, h) for b in range(slots // 8) for h in range(halves)]
     hidden_second, part = pl.pallas_call(
         lambda *refs: neighbour_kernel(*refs, scale=scale),
         grid=(steps,),
         in_specs=[
-            smem,
-            pl.BlockSpec((atoms * slots // steps, hid), lambda i: (i, 0)),
+            pl.BlockSpec((8, 128), lambda i, at=at: at, memory_space=pltpu.SMEM) for at in blocks
+        ] + [
+            pl.BlockSpec((halves, 128 // steps, slots, hid), lambda i: (0, i, 0, 0)),
             whole((kv * atoms, hid)),
             whole((halo, hid)),
             whole((halo, hid)),
             whole((atoms, hid)),
-            whole((hid, chan)),
+            whole((chan, hid)),
             whole((atoms, waves)),
             whole((atoms, waves)),
             whole((3, waves)),
         ],
         out_specs=(whole((atoms, hid)), whole((part_rows, 128))),
         out_shape=(shape((atoms, hid), BF16), shape((part_rows, 128), BF16)),
-        scratch_shapes=[pltpu.VMEM((kv * atoms + 2 * halo, hid), F32), pltpu.VMEM((atoms, hid), F32)],
+        scratch_shapes=[pltpu.VMEM((kv * atoms + 2 * halo, hid), F32), pltpu.VMEM((8 * atoms, hid), F32)],
         name="neighbours",
     )(
-        nbr_index, weights, v_dom, from_below, from_above, hidden_first,
-        w_charge_second, cos_table, sin_table, wave_vectors,
+        *[index_t] * len(blocks), weights.reshape(halves, 128, slots, hid), v_dom, from_below, from_above,
+        hidden_first, w_charge_second, cos_table, sin_table, wave_vectors,
     )
     sums = everything(part, "fold_second")
     return pl.pallas_call(

time: 170 us -> 159 us (0.935)
  local copies, waits for them, and re-layouts: 6.81 us -> 0.79 us
  Pallas kernels: 53.7 us -> 48.5 us
    unnamed x8 -> x4, local copies, waits for them, and re-layouts: 6.09 us -> 0.79 us
    pallas_call x2, Pallas kernels: 13.6 us -> 10.4 us  [the longest x1 6.88 us: local(): pl.pallas_call(weight_kernel, grid=(steps,), in_specs=[whole((1, atoms)),...]
    pallas_call x1, Pallas kernels: 24.3 us -> 22.4 us  [local(): pl.pallas_call(lambda *refs: neighbour_kernel(*refs, scale=scale), grid=(...]
  transfers between devices with their start and end apart: 2 -> 2, of which waited for: 0 -> 0; matrix products, arithmetic and copies ran while one was open for 3% -> 0% of each run, Pallas kernels for 4% -> 4%
where the time goes in v2:
time: 159 us; the launch traced here: 158 us
  blocking collectives  106 us (67%)
  Pallas kernels  48.5 us (31%)
  starting transfers between devices  2.61 us (2%)
    all_to_all x2, blocking collectives, everything(): sums = lax.all_to_all(part, EVERY, 0, 0, tiled=True)  51 us
    all_to_all x2, blocking collectives, everything(): return lax.all_to_all(folded, EVERY, 0, 0, tiled=True)  39.7 us
    pallas_call x1, Pallas kernels, local(): pl.pallas_call(lambda *refs: neighbour_kernel(*refs, scale=scale), grid=(...  22.4 us
    all_to_all x1, blocking collectives, local(): v_dom = lax.all_to_all(values, 'kv', 0, 0, tiled=True)  14.9 us
    pallas_call x1, Pallas kernels, local(): pl.pallas_call(weight_kernel, grid=(steps,), in_specs=[whole((1, atoms)),...  6.88 us
    pallas_call x1, Pallas kernels, local(): pl.pallas_call(lambda *refs: table_kernel(*refs, scale=scale), out_shape=...  5.15 us
    pallas_call x1, Pallas kernels, local(): pl.pallas_call(first_project_kernel, out_shape=(shape((atoms, hid), BF16)...  3.83 us
    pallas_call x1, Pallas kernels, local(): pl.pallas_call(last_project_kernel, out_shape=(shape((atoms, hid), BF16),...  3.55 us
  transfers between devices with their start and end apart: 2, of which 0 were waited for; matrix products, arithmetic and copies ran while one was open for 0% of the time, Pallas kernels for 4%

profile of v2, /device:TPU:1, one launch (start us, length us, event | category | flops | bytes accessed | tf_op | source)
XLA Modules:
  0.0 158.2 jit_solution(12759399161593532716)
XLA Ops:
  0.6 5.1 %tables.1 = (bf16[256,2048]{1,0:T(8,128)(2,1)}, bf16[256,2048]{1,0:T(8,128)(2,1)}, bf16[512,128]{1,0:T(8,128)(2,1)}) custom-call(f32[3,256]{1,0:T(4,128)} %refs_0_.1, bf16[256,128]{1,0:T(8,128)(2,1)} %feat_ref.1, bf16[16,128]{1,0:T(8,128)(2,1)} %bitcast.56, f32[3,2048]{1,0:T(4,128)} %wave_ref.3), custom_call_target="tpu_custom_call" | custom-call | tf_op jit(solution)/shard_map/tables/pallas_call | solution.py:310
  5.8 28.6 %all_to_all.55 = bf16[256,2,128]{2,1,0:T(2,128)(2,1)} all-to-all(bf16[256,2,128]{2,1,0:T(2,128)(2,1)} %bitcast.52), channel_id=1, replica_groups=mesh['dom'=32,'kv'=8] {'dom','kv'}, dimensions={0} | all-to-all | bytes 262144 | tf_op jit(solution)/shard_map/all_to_all | solution.py:285
  34.4 1.6 %fold_first.1 = bf16[512,128]{1,0:T(8,128)(2,1)} custom-call(bf16[512,128]{1,0:T(8,128)(2,1)} %bitcast.47), custom_call_target="tpu_custom_call" | custom-call | tf_op jit(solution)/shard_map/fold_first/pallas_call | solution.py:286
  36.0 19.9 %all_to_all.56 = bf16[256,2,128]{2,1,0:T(2,128)(2,1)} all-to-all(bf16[256,2,128]{2,1,0:T(2,128)(2,1)} %bitcast.48), channel_id=1, replica_groups=mesh['dom'=32,'kv'=8] {'dom','kv'}, dimensions={0} | all-to-all | bytes 262144 | tf_op jit(solution)/shard_map/all_to_all | solution.py:287
  55.9 3.8 %project_first.1 = (bf16[256,128]{1,0:T(8,128)(2,1)}, bf16[2048,128]{1,0:T(8,128)(2,1)}, f32[3,256]{1,0:T(4,128)}) custom-call(bf16[512,128]{1,0:T(8,128)(2,1)} %bitcast.45, bf16[256,2048]{1,0:T(8,128)(2,1)} %get-tuple-element.13.cos_ref.refs_22_, bf16[256,2048]{1,0:T(8,128)(2,1)} %get-tuple-element.14.sin_ref.refs_23_, f32[3,2048]{1,0:T(4,128)} %wave_ref.3, ...), custom_call_target="tpu_custom_call" | custom-call | tf_op jit(solution)/shard_map/project_first/pallas_call | solution.py:317
  59.7 14.9 %all_to_all.57 = bf16[8,256,128]{2,1,0:T(8,128)(2,1)} all-to-all(bf16[8,256,128]{2,1,0:T(8,128)(2,1)} %bitcast.46), channel_id=1, replica_groups=mesh['dom'=32,'kv'=8] {'kv'}, dimensions={0} | all-to-all | bytes 1048576 | tf_op jit(solution)/shard_map/all_to_all | solution.py:324
  74.6 3.5 %halo_rows.1 = (bf16[1024,128]{1,0:T(8,128)(2,1)}, bf16[1024,128]{1,0:T(8,128)(2,1)}) custom-call(s32[2,1024]{1,0:T(2,128)} %bitcast.36, s32[2,1024]{1,0:T(2,128)} %bitcast.37, s32[2,1024]{1,0:T(2,128)} %bitcast.38, s32[2,1024]{1,0:T(2,128)} %bitcast.39, s32[2,1024]{1,0:T(2,128)} %bitcast.40, s32[2,1024]{1,0:T(2,128)} %bitcast.41, s32[2,1024]{1,0:T(2,128)} %bitcast.42, ...), custom_call_target="tpu_custom_call" | custom-call | tf_op jit(solution)/shard_map/halo_rows/pallas_call | solution.py:325
  78.0 2.6 %collective-permute-start = (bf16[1024,128]{1,0:T(8,128)(2,1)}, bf16[1024,128]{1,0:T(8,128)(2,1)S(1)}, u32[]{:S(2)}, u32[]{:S(2)}) collective-permute-start(bf16[1024,128]{1,0:T(8,128)(2,1)} %get-tuple-element.16), channel_id=1, source_target_pairs={{0,8},{8,16},{16,24},{24,32},{32,40},{40,48},{48,56},{56,64},{64,7... | collective-permute-start | bytes 786440 | tf_op jit(solution)/shard_map/ppermute | solution.py:336
  80.7 0.0 collective-permute-start.1
  80.7 6.9 %slot_weights.1 = f32[256,64,128]{2,1,0:T(8,128)} custom-call(s32[1,256]{1,0:T(1,128)} %bitcast.58, f32[64,256]{1,0:T(8,128)} %bitcast.53, f32[16,128]{1,0:T(8,128)} %wf_ref.1), custom_call_target="tpu_custom_call" | custom-call | flops 134217728 | bytes 8388608 | tf_op jit(solution)/shard_map/slot_weights/pallas_call | solution.py:342
  87.5 0.0 collective-permute-done.refs_18_
  87.5 0.0 copy-start
  87.5 0.0 collective-permute-done.1.refs_19_
  87.5 0.0 copy-start.1
  87.6 0.7 copy-done
  88.2 0.1 copy-done.1
  88.3 22.4 %neighbours.1 = (bf16[256,128]{1,0:T(8,128)(2,1)}, bf16[512,128]{1,0:T(8,128)(2,1)}) custom-call(s32[64,256]{1,0:T(8,128)} %bitcast.18, s32[64,256]{1,0:T(8,128)} %bitcast.19, s32[64,256]{1,0:T(8,128)} %bitcast.20, s32[64,256]{1,0:T(8,128)} %bitcast.21, s32[64,256]{1,0:T(8,128)} %bitcast.22, s32[64,256]{1,0:T(8,128)} %bitcast.23, s32[64,256]{1,0:T(8,128)} %bitcast.24, ...), custom_call_target="tpu_custom_call" | custom-call | tf_op jit(solution)/shard_map/neighbours/pallas_call | solution.py:367
  110.7 22.4 %all_to_all.58 = bf16[256,2,128]{2,1,0:T(2,128)(2,1)} all-to-all(bf16[256,2,128]{2,1,0:T(2,128)(2,1)} %bitcast.51), channel_id=1, replica_groups=mesh['dom'=32,'kv'=8] {'dom','kv'}, dimensions={0} | all-to-all | bytes 262144 | tf_op jit(solution)/shard_map/all_to_all | solution.py:285
  133.1 1.6 %fold_second.1 = bf16[512,128]{1,0:T(8,128)(2,1)} custom-call(bf16[512,128]{1,0:T(8,128)(2,1)} %bitcast.49), custom_call_target="tpu_custom_call" | custom-call | tf_op jit(solution)/shard_map/fold_second/pallas_call | solution.py:286
  134.8 19.8 %all_to_all.59 = bf16[256,2,128]{2,1,0:T(2,128)(2,1)} all-to-all(bf16[256,2,128]{2,1,0:T(2,128)(2,1)} %bitcast.50), channel_id=1, replica_groups=mesh['dom'=32,'kv'=8] {'dom','kv'}, dimensions={0} | all-to-all | bytes 262144 | tf_op jit(solution)/shard_map/all_to_all | solution.py:287
  154.6 3.6 %project_second.1 = (bf16[256,128]{1,0:T(8,128)(2,1)}, f32[3,256]{1,0:T(4,128)}) custom-call(bf16[512,128]{1,0:T(8,128)(2,1)} %bitcast.44, bf16[256,2048]{1,0:T(8,128)(2,1)} %get-tuple-element.13.cos_ref.refs_22_, bf16[256,2048]{1,0:T(8,128)(2,1)} %get-tuple-element.14.sin_ref.refs_23_, f32[3,2048]{1,0:T(4,128)} %wave_ref.3, ...), custom_call_target="tpu_custom_call" | custom-call | tf_op jit(solution)/shard_map/project_second/pallas_call | solution.py:392
Async XLA Ops:
  78.0 9.5 %collective-permute-start = (bf16[1024,128]{1,0:T(8,128)(2,1)}, bf16[1024,128]{1,0:T(8,128)(2,1)S(1)}, u32[]{:S(2)}, u32[]{:S(2)}) collective-permute-start(bf16[1024,128]{1,0:T(8,128)(2,1)} %get-tuple-element.16), channel_id=1, source_target_pairs={{0,8},{8,16},{16,24},{24,32},{32,40},{40,48},{48,56},{56,64},{64,7... | collective-permute-start | bytes 786440 | tf_op jit(solution)/shard_map/ppermute | solution.py:336
  80.7 6.9 %collective-permute-start.1 = (bf16[1024,128]{1,0:T(8,128)(2,1)}, bf16[1024,128]{1,0:T(8,128)(2,1)S(1)}, u32[]{:S(2)}, u32[]{:S(2)}) collective-permute-start(bf16[1024,128]{1,0:T(8,128)(2,1)} %get-tuple-element.17), channel_id=1, source_target_pairs={{0,248},{8,0},{16,8},{24,16},{32,24},{40,32},{48,40},{56,48},{64,5... | collective-permute-start | bytes 786440 | tf_op jit(solution)/shard_map/ppermute | solution.py:337
  87.5 0.7 copy-start
  87.5 0.8 copy-start.1

commit v3 on v2

--- a/solution.py
+++ b/solution.py
@@ -235,7 +235,7 @@
 
 
 def neighbour_kernel(*refs, scale):
-    index_refs = refs[:-13]
+    count_ref, index_refs = refs[0], refs[1:-13]
     (
         weight_ref, values_ref, below_ref, above_ref, hidden_ref, wc_ref, cos_ref, sin_ref, wave_ref,
         hidden_out, part_ref, table, sums,
@@ -256,11 +256,22 @@
 
         def one_atom(a, carry, half=half):
             lane = step * atoms + a
-            total = jnp.zeros((8, 128), F32)
-            for b in range(slots // 8):
-                rows = [index_refs[b * halves + half][s, lane] for s in range(8)]
-                total = total + row_tile(table, rows, bits) * weight_ref[half, a, 8 * b : 8 * b + 8, :]
-            sums[pl.ds(pl.multiple_of((half * 128 + lane) * 8, 8), 8), :] = total
+            at = pl.ds(pl.multiple_of((half * 128 + lane) * 8, 8), 8)
+
+            def some_slots(blocks):
+                total = jnp.zeros((8, 128), F32)
+                for b in blocks:
+                    rows = [index_refs[b * halves + half][s, lane] for s in range(8)]
+                    total = total + row_tile(table, rows, bits) * weight_ref[half, a, 8 * b : 8 * b + 8, :]
+                return total
+
+            middle = slots // 16
+            sums[at, :] = some_slots(range(middle))
+
+            @pl.when(count_ref[half * 128 + lane] > middle * 8)
+            def _():
+                sums[at, :] = sums[at, :] + some_slots(range(middle, slots // 8))
+
             return carry
 
         lax.fori_loop(0, atoms, one_atom, 0)
@@ -281,9 +292,13 @@
     return jax.ShapeDtypeStruct(dims, kind)
 
 
+def vmem(mib):
+    return pltpu.CompilerParams(vmem_limit_bytes=mib * 1024 * 1024)
+
+
 def everything(part, name):
     sums = lax.all_to_all(part, EVERY, 0, 0, tiled=True)
-    folded = pl.pallas_call(fold_kernel, out_shape=shape(part.shape, BF16), name=name)(sums)
+    folded = pl.pallas_call(fold_kernel, out_shape=shape(part.shape, BF16), compiler_params=vmem(2), name=name)(sums)
     return lax.all_to_all(folded, EVERY, 0, 0, tiled=True)
 
 
@@ -301,6 +316,7 @@
     scale = LONG_SCALE / math.sqrt(waves) / math.sqrt(total_atoms)
     part_rows = 2 * chan * waves // 128
     halo = halo_lists.shape[2]
+    smem = pl.BlockSpec(memory_space=pltpu.SMEM)
     w_charge_first = w_charge_first.T
     w_charge_second = w_charge_second.T
     lists = halo_lists[0]
@@ -311,6 +327,7 @@
         lambda *refs: table_kernel(*refs, scale=scale),
         out_shape=(shape((atoms, waves), BF16), shape((atoms, waves), BF16), shape((part_rows, 128), BF16)),
         scratch_shapes=[pltpu.VMEM((3, atoms, 128), F32), pltpu.VMEM((8, atoms), F32)],
+        compiler_params=vmem(6),
         name="tables",
     )(positions, features, w_charge_first, wave_vectors)
     sums = everything(part, "fold_first")
@@ -318,6 +335,7 @@
         first_project_kernel,
         out_shape=(shape((atoms, hid), BF16), shape((kv * atoms, hid), BF16), shape((3, atoms), F32)),
         scratch_shapes=[pltpu.VMEM((4 * chan, waves), BF16)] * 2,
+        compiler_params=vmem(6),
         name="project_first",
     )(sums, cos_table, sin_table, wave_vectors, features, w_charge_first, w_long_first, w_value)
 
@@ -331,6 +349,7 @@
         out_specs=(pl.BlockSpec((halo, hid), lambda i: (0, 0)), pl.BlockSpec((halo, hid), lambda i: (0, 0))),
         out_shape=(shape((halo, hid), BF16), shape((halo, hid), BF16)),
         scratch_shapes=[pltpu.VMEM((kv * atoms, hid), F32), pltpu.VMEM((2, halo, hid), F32)],
+        compiler_params=vmem(6),
         name="halo_rows",
     )(*[lists] * (halo // 128), v_dom)
     from_below = lax.ppermute(to_next, "dom", [(i, (i + 1) % doms) for i in range(doms)])
@@ -360,6 +379,7 @@
             bytes_accessed=atoms * slots * hid * 4,
             transcendentals=atoms * slots * 16,
         ),
+        compiler_params=vmem(6),
         name="slot_weights",
     )(nbr_count.reshape(1, atoms), dist_t, w_filter)
 
@@ -367,7 +387,7 @@
     hidden_second, part = pl.pallas_call(
         lambda *refs: neighbour_kernel(*refs, scale=scale),
         grid=(steps,),
-        in_specs=[
+        in_specs=[smem] + [
             pl.BlockSpec((8, 128), lambda i, at=at: at, memory_space=pltpu.SMEM) for at in blocks
         ] + [
             pl.BlockSpec((halves, 128 // steps, slots, hid), lambda i: (0, i, 0, 0)),
@@ -383,9 +403,10 @@
         out_specs=(whole((atoms, hid)), whole((part_rows, 128))),
         out_shape=(shape((atoms, hid), BF16), shape((part_rows, 128), BF16)),
         scratch_shapes=[pltpu.VMEM((kv * atoms + 2 * halo, hid), F32), pltpu.VMEM((8 * atoms, hid), F32)],
+        compiler_params=vmem(14),
         name="neighbours",
     )(
-        *[index_t] * len(blocks), weights.reshape(halves, 128, slots, hid), v_dom, from_below, from_above,
+        nbr_count, *[index_t] * len(blocks), weights.reshape(halves, 128, slots, hid), v_dom, from_below, from_above,
         hidden_first, w_charge_second, cos_table, sin_table, wave_vectors,
     )
     sums = everything(part, "fold_second")
@@ -393,6 +414,7 @@
         last_project_kernel,
         out_shape=(shape((atoms, hid), BF16), shape((3, atoms), F32)),
         scratch_shapes=[pltpu.VMEM((4 * chan, waves), BF16)] * 2,
+        compiler_params=vmem(6),
         name="project_second",
     )(sums, cos_table, sin_table, wave_vectors, hidden_second, w_charge_second, w_long_second, force_first)
 

time: 159 us -> 143 us (0.90)
  Pallas kernels: 48.5 us -> 30.6 us
  local copies, waits for them, and re-layouts: 0.79 us -> 8.91 us
  blocking collectives: 106 us -> 98.9 us
    unnamed x4 -> x34, local copies, waits for them, and re-layouts: 0.79 us -> 8.91 us
    pallas_call x1, Pallas kernels: 22.4 us -> 18.2 us  [local(): pl.pallas_call(lambda *refs: neighbour_kernel(*refs, scale=scale), grid=(...]
    pallas_call x1, Pallas kernels: 6.88 us -> 3.1 us  [local(): pl.pallas_call(weight_kernel, grid=(steps,), in_specs=[whole((1, atoms)),...]
    all_to_all x2, blocking collectives: 39.7 us -> 36.3 us  [everything(): return lax.all_to_all(folded, EVERY, 0, 0, tiled=True)]
    pallas_call x2, Pallas kernels: 3.28 us -> 0.16 us  [everything(): pl.pallas_call(fold_kernel, out_shape=shape(part.shape, BF16), compiler_p...]
    pallas_call x1, Pallas kernels: 3.83 us -> 1.43 us  [local(): pl.pallas_call(first_project_kernel, out_shape=(shape((atoms, hid), BF16)...]
    all_to_all x2, blocking collectives: 51 us -> 49.1 us  [everything(): sums = lax.all_to_all(part, EVERY, 0, 0, tiled=True)]
    pallas_call x1, Pallas kernels: 5.15 us -> 3.52 us  [local(): pl.pallas_call(lambda *refs: table_kernel(*refs, scale=scale), out_shape=...]
  transfers between devices with their start and end apart: 2 -> 2, of which waited for: 0 -> 1; matrix products, arithmetic and copies ran while one was open for 0% -> 0% of each run, Pallas kernels for 4% -> 2%
where the time goes in v3:
time: 143 us; the launch traced here: 142 us
  blocking collectives  98.9 us (69%)
  Pallas kernels  30.6 us (21%)
  local copies, waits for them, and re-layouts  8.91 us (6%)
  starting transfers between devices  2.54 us (2%)
    all_to_all x2, blocking collectives, everything(): sums = lax.all_to_all(part, EVERY, 0, 0, tiled=True)  49.1 us
    all_to_all x2, blocking collectives, everything(): return lax.all_to_all(folded, EVERY, 0, 0, tiled=True)  36.3 us
    pallas_call x1, Pallas kernels, local(): pl.pallas_call(lambda *refs: neighbour_kernel(*refs, scale=scale), grid=(...  18.2 us
    all_to_all x1, blocking collectives, local(): v_dom = lax.all_to_all(values, 'kv', 0, 0, tiled=True)  13.5 us
    unnamed x34, local copies, waits for them, and re-layouts  8.91 us
    pallas_call x1, Pallas kernels, local(): pl.pallas_call(lambda *refs: table_kernel(*refs, scale=scale), out_shape=...  3.52 us
    pallas_call x1, Pallas kernels, local(): pl.pallas_call(weight_kernel, grid=(steps,), in_specs=[whole((1, atoms)),...  3.1 us
  transfers between devices with their start and end apart: 2, of which 1 were waited for; matrix products, arithmetic and copies ran while one was open for 0% of the time, Pallas kernels for 2%

profile of v3, /device:TPU:1, one launch (start us, length us, event | category | flops | bytes accessed | tf_op | source)
XLA Modules:
  0.0 142.5 jit_solution(5758836993893361395)
XLA Ops:
  0.6 0.0 copy-start
  0.6 0.0 copy-start.2
  0.7 0.8 copy-done.2
  1.4 0.0 copy-start.4
  1.4 0.8 copy-done.4
  2.3 0.0 copy-start.9
  2.3 0.7 copy-done.9
  3.0 0.0 copy-start.16
  3.0 0.7 copy-done.16
  3.6 0.0 copy-start.3
  3.6 0.0 copy-start.8
  3.6 0.0 copy-start.15
  3.7 3.5 %tables.1 = (bf16[256,2048]{1,0:T(8,128)(2,1)S(1)}, bf16[256,2048]{1,0:T(8,128)(2,1)S(1)}, bf16[512,128]{1,0:T(8,128)(2,1)S(1)}) custom-call(f32[3,256]{1,0:T(4,128)S(1)} %copy-done.16, bf16[256,128]{1,0:T(8,128)(2,1)S(1)} %copy-done.4, bf16[16,128]{1,0:T(8,128)(2,1)S(1)} %bitcast.56, f32[3,2048]{1,0:T(4,128)S(1)} %copy-done.2), custom_call_target="tpu_custom_call" | custom-call | tf_op jit(solution)/shard_map/tables/pallas_call | solution.py:326
  7.2 28.5 %all_to_all.55 = bf16[256,2,128]{2,1,0:T(2,128)(2,1)S(1)} all-to-all(bf16[256,2,128]{2,1,0:T(2,128)(2,1)S(1)} %bitcast.52), channel_id=1, replica_groups=mesh['dom'=32,'kv'=8] {'dom','kv'}, dimensions={0} | all-to-all | bytes 262144 | tf_op jit(solution)/shard_map/all_to_all | solution.py:300
  35.7 0.1 fold_first.1
  35.8 18.2 %all_to_all.56 = bf16[256,2,128]{2,1,0:T(2,128)(2,1)S(1)} all-to-all(bf16[256,2,128]{2,1,0:T(2,128)(2,1)S(1)} %bitcast.48), channel_id=1, replica_groups=mesh['dom'=32,'kv'=8] {'dom','kv'}, dimensions={0} | all-to-all | bytes 262144 | tf_op jit(solution)/shard_map/all_to_all | solution.py:302
  53.9 0.0 copy-start.5
  53.9 0.8 copy-done.5
  54.8 0.0 copy-start.7
  54.8 0.8 copy-done.7
  55.5 0.0 copy-start.10
  55.5 0.7 copy-done.10
  56.2 0.0 copy-start.11
  56.2 0.7 copy-done.11
  56.9 1.4 %project_first.1 = (bf16[256,128]{1,0:T(8,128)(2,1)S(1)}, bf16[2048,128]{1,0:T(8,128)(2,1)S(1)}, f32[3,256]{1,0:T(4,128)S(1)}) custom-call(bf16[512,128]{1,0:T(8,128)(2,1)S(1)} %bitcast.45, bf16[256,2048]{1,0:T(8,128)(2,1)S(1)} %get-tuple-element.13.cos_ref.refs_23_, bf16[256,2048]{1,0:T(8,128)(2,1)S(1)} %get-tuple-element.14.sin_ref.refs_24_, ...), custom_call_target="tpu_custom_call" | custom-call | tf_op jit(solution)/shard_map/project_first/pallas_call | solution.py:334
  58.3 13.5 %all_to_all.57 = bf16[8,256,128]{2,1,0:T(8,128)(2,1)S(1)} all-to-all(bf16[8,256,128]{2,1,0:T(8,128)(2,1)S(1)} %bitcast.46), channel_id=1, replica_groups=mesh['dom'=32,'kv'=8] {'kv'}, dimensions={0} | all-to-all | bytes 1048576 | tf_op jit(solution)/shard_map/all_to_all | solution.py:342
  71.8 0.0 copy-start.1
  71.8 0.7 copy-done.1
  72.5 2.3 %halo_rows.1 = (bf16[1024,128]{1,0:T(8,128)(2,1)S(1)}, bf16[1024,128]{1,0:T(8,128)(2,1)S(1)}) custom-call(s32[2,1024]{1,0:T(2,128)S(1)} %bitcast.36, s32[2,1024]{1,0:T(2,128)S(1)} %bitcast.37, s32[2,1024]{1,0:T(2,128)S(1)} %bitcast.38, s32[2,1024]{1,0:T(2,128)S(1)} %bitcast.39, s32[2,1024]{1,0:T(2,128)S(1)} %bitcast.40, s32[2,1024]{1,0:T(2,128)S(1)} %bitcast.41, ...), custom_call_target="tpu_custom_call" | custom-call | tf_op jit(solution)/shard_map/halo_rows/pallas_call | solution.py:343
  74.8 2.5 %collective-permute-start = (bf16[1024,128]{1,0:T(8,128)(2,1)S(1)}, bf16[1024,128]{1,0:T(8,128)(2,1)S(1)}, u32[]{:S(2)}, u32[]{:S(2)}) collective-permute-start(bf16[1024,128]{1,0:T(8,128)(2,1)S(1)} %get-tuple-element.16), channel_id=1, source_target_pairs={{0,8},{8,16},{16,24},{24,32},{32,40},{40,48},{48,56},{56,64},{64,7... | collective-permute-start | bytes 786440 | tf_op jit(solution)/shard_map/ppermute | solution.py:355
  77.4 0.0 collective-permute-start.1
  77.4 0.0 copy-start.6
  77.4 0.8 copy-done.6
  78.2 0.0 copy-start.12
  78.2 0.7 copy-done.12
  78.9 0.0 copy-start.14
  78.9 0.7 copy-done.14
  79.6 3.1 %slot_weights.1 = f32[256,64,128]{2,1,0:T(8,128)S(1)} custom-call(s32[1,256]{1,0:T(1,128)S(1)} %bitcast.58, f32[64,256]{1,0:T(8,128)S(1)} %bitcast.53, f32[16,128]{1,0:T(8,128)S(1)} %copy-done.12), custom_call_target="tpu_custom_call" | custom-call | flops 134217728 | bytes 8388608 | tf_op jit(solution)/shard_map/slot_weights/pallas_call | solution.py:361
  82.7 0.0 copy-start.13
  82.7 0.0 collective-permute-done.refs_19_
  82.7 0.7 collective-permute-done.1.refs_20_
  83.5 0.0 copy-done
  83.5 0.0 copy-done.3
  83.5 0.0 copy-done.8
  83.5 0.0 copy-done.15
  83.5 18.2 %neighbours.1 = (bf16[256,128]{1,0:T(8,128)(2,1)S(1)}, bf16[512,128]{1,0:T(8,128)(2,1)S(1)}) custom-call(s32[256]{0:T(256)S(1)} %copy-done.15, s32[64,256]{1,0:T(8,128)S(1)} %bitcast.18, s32[64,256]{1,0:T(8,128)S(1)} %bitcast.19, s32[64,256]{1,0:T(8,128)S(1)} %bitcast.20, s32[64,256]{1,0:T(8,128)S(1)} %bitcast.21, s32[64,256]{1,0:T(8,128)S(1)} %bitcast.22, ...), custom_call_target="tpu_custom_call" | custom-call | tf_op jit(solution)/shard_map/neighbours/pallas_call | solution.py:387
  101.7 20.6 %all_to_all.58 = bf16[256,2,128]{2,1,0:T(2,128)(2,1)S(1)} all-to-all(bf16[256,2,128]{2,1,0:T(2,128)(2,1)S(1)} %bitcast.51), channel_id=1, replica_groups=mesh['dom'=32,'kv'=8] {'dom','kv'}, dimensions={0} | all-to-all | bytes 262144 | tf_op jit(solution)/shard_map/all_to_all | solution.py:300
  122.3 0.1 fold_second.1
  122.3 18.2 %all_to_all.59 = bf16[256,2,128]{2,1,0:T(2,128)(2,1)S(1)} all-to-all(bf16[256,2,128]{2,1,0:T(2,128)(2,1)S(1)} %bitcast.50), channel_id=1, replica_groups=mesh['dom'=32,'kv'=8] {'dom','kv'}, dimensions={0} | all-to-all | bytes 262144 | tf_op jit(solution)/shard_map/all_to_all | solution.py:302
  140.5 0.0 copy-done.13
  140.5 1.9 %project_second.1 = (bf16[256,128]{1,0:T(8,128)(2,1)}, f32[3,256]{1,0:T(4,128)}) custom-call(bf16[512,128]{1,0:T(8,128)(2,1)S(1)} %bitcast.44, bf16[256,2048]{1,0:T(8,128)(2,1)S(1)} %get-tuple-element.13.cos_ref.refs_23_, bf16[256,2048]{1,0:T(8,128)(2,1)S(1)} %get-tuple-element.14.sin_ref.refs_24_, f32[3,2048]{1,0:T(4,128)S(1)} %copy-done.3, ...), custom_call_target="tpu_custom_call" | custom-call | tf_op jit(solution)/shard_map/project_second/pallas_call | solution.py:413
Async XLA Ops:
  0.6 82.8 %copy-start = (s32[256,64]{0,1:T(8,128)S(1)}, s32[256,64]{0,1:T(8,128)}, u32[]{:S(2)}) copy-start(s32[256,64]{0,1:T(8,128)} %param.15) | copy-start | bytes 196612
  0.6 0.8 copy-start.2
  1.4 0.8 copy-start.4
  2.3 0.7 copy-start.9
  3.0 0.7 copy-start.16
  3.6 79.8 %copy-start.3 = (f32[3,2048]{1,0:T(4,128)S(1)}, f32[3,2048]{1,0:T(4,128)}, u32[]{:S(2)}) copy-start(f32[3,2048]{1,0:T(4,128)} %wave_ref.3) | copy-start | bytes 73732
  3.6 79.8 %copy-start.8 = (bf16[128,16]{0,1:T(8,128)(2,1)S(1)}, bf16[128,16]{0,1:T(8,128)(2,1)}, u32[]{:S(2)}) copy-start(bf16[128,16]{0,1:T(8,128)(2,1)} %param.24) | copy-start | bytes 12292
  3.6 79.8 %copy-start.15 = (s32[256]{0:T(256)S(1)}, s32[256]{0:T(256)}, u32[]{:S(2)}) copy-start(s32[256]{0:T(256)} %refs_0_.3) | copy-start | bytes 3076
  53.9 0.8 copy-start.5
  54.8 0.8 copy-start.7
  55.5 0.7 copy-start.10
  56.2 0.7 copy-start.11
  71.8 0.7 copy-start.1
  74.8 7.9 %collective-permute-start = (bf16[1024,128]{1,0:T(8,128)(2,1)S(1)}, bf16[1024,128]{1,0:T(8,128)(2,1)S(1)}, u32[]{:S(2)}, u32[]{:S(2)}) collective-permute-start(bf16[1024,128]{1,0:T(8,128)(2,1)S(1)} %get-tuple-element.16), channel_id=1, source_target_pairs={{0,8},{8,16},{16,24},{24,32},{32,40},{40,48},{48,56},{56,64},{64,7... | collective-permute-start | bytes 786440 | tf_op jit(solution)/shard_map/ppermute | solution.py:355
  77.4 6.1 %collective-permute-start.1 = (bf16[1024,128]{1,0:T(8,128)(2,1)S(1)}, bf16[1024,128]{1,0:T(8,128)(2,1)S(1)}, u32[]{:S(2)}, u32[]{:S(2)}) collective-permute-start(bf16[1024,128]{1,0:T(8,128)(2,1)S(1)} %get-tuple-element.17), channel_id=1, source_target_pairs={{0,248},{8,0},{16,8},{24,16},{32,24},{40,32},{48,40},{56,48},{64,5... | collective-permute-start | bytes 786440 | tf_op jit(solution)/shard_map/ppermute | solution.py:356
  77.4 0.8 copy-start.6
  78.2 0.7 copy-start.12
  78.9 0.7 copy-start.14
  82.7 57.8 %copy-start.13 = (f32[16,128]{1,0:T(8,128)S(1)}, f32[16,128]{1,0:T(8,128)}, u32[]{:S(2)}) copy-start(f32[16,128]{1,0:T(8,128)} %wl_ref.3) | copy-start | bytes 24580

commit v4 on v3

--- a/solution.py
+++ b/solution.py
@@ -12,7 +12,12 @@
 HIGHEST = lax.Precision.HIGHEST
 LONG_SCALE = 2.0
 CELL = 60.0
-EVERY = ("dom", "kv")
+PARTS = (("xlo", 2), ("z", 8), ("core", 2), ("y", 4), ("xhi", 2))
+EVERY = tuple(name for name, _ in PARTS)
+DOM = ("xlo", "z", "core")
+KV = ("y", "xhi")
+COLUMN = ("z", "core")
+PLANE = ("xlo", "y", "xhi")
 
 COS_COEF = (
     1.0,
@@ -108,12 +113,14 @@
     structure_part(charge_t, cos_ref, sin_ref, wave_ref, part_ref, scale)
 
 
-def fold_kernel(in_ref, out_ref):
-    rows = in_ref.shape[0]
-    total = jnp.sum(in_ref[...].astype(F32).reshape(rows // 8, 8, 128), axis=0)
-    total = total + pltpu.roll(total, 4, 0)
-    total = total + pltpu.roll(total, 2, 0)
-    out_ref[...] = jnp.broadcast_to(total[None], (rows // 8, 8, 128)).reshape(rows, 128).astype(BF16)
+def fold_kernel(in_ref, out_ref, *, members, copies):
+    rows = in_ref.shape[0] // members
+    total = in_ref[0:rows, :].astype(F32)
+    for m in range(1, members):
+        total = total + in_ref[m * rows : (m + 1) * rows, :].astype(F32)
+    total = total.astype(BF16)
+    for m in range(copies):
+        out_ref[m * rows : (m + 1) * rows, :] = total
 
 
 def project(sums_ref, cos_ref, sin_ref, wave_ref, charge_t, with_cos, with_sin):
@@ -292,14 +299,32 @@
     return jax.ShapeDtypeStruct(dims, kind)
 
 
+def in_hbm(*arrays):
+    return tuple(pltpu.with_memory_space_constraint(array, pltpu.HBM) for array in arrays)
+
+
 def vmem(mib):
     return pltpu.CompilerParams(vmem_limit_bytes=mib * 1024 * 1024)
 
 
+def fold(sums, members, copies, name):
+    rows = sums.shape[0] // members
+    return pl.pallas_call(
+        lambda *refs: fold_kernel(*refs, members=members, copies=copies),
+        out_shape=shape((copies * rows, sums.shape[1]), BF16),
+        compiler_params=vmem(2),
+        name=name,
+    )(sums)
+
+
 def everything(part, name):
-    sums = lax.all_to_all(part, EVERY, 0, 0, tiled=True)
-    folded = pl.pallas_call(fold_kernel, out_shape=shape(part.shape, BF16), compiler_params=vmem(2), name=name)(sums)
-    return lax.all_to_all(folded, EVERY, 0, 0, tiled=True)
+    column = lax.axis_size(COLUMN)
+    plane = lax.axis_size(PLANE)
+    share = lax.all_to_all(part, COLUMN, 0, 0, tiled=True)
+    share = fold(share, column, plane, name + "_column")
+    share = lax.all_to_all(share, PLANE, 0, 0, tiled=True)
+    share = fold(share, plane, column, name + "_plane")
+    return lax.all_to_all(share, COLUMN, 0, 0, tiled=True)
 
 
 def local(
@@ -310,8 +335,8 @@
     chan = w_charge_first.shape[1]
     waves = wave_vectors.shape[1]
     slots = nbr_index.shape[1]
-    kv = lax.axis_size("kv")
-    doms = lax.axis_size("dom")
+    kv = lax.axis_size(KV)
+    doms = lax.axis_size(DOM)
     total_atoms = atoms * doms * kv
     scale = LONG_SCALE / math.sqrt(waves) / math.sqrt(total_atoms)
     part_rows = 2 * chan * waves // 128
@@ -329,7 +354,7 @@
         scratch_shapes=[pltpu.VMEM((3, atoms, 128), F32), pltpu.VMEM((8, atoms), F32)],
         compiler_params=vmem(6),
         name="tables",
-    )(positions, features, w_charge_first, wave_vectors)
+    )(*in_hbm(positions, features, w_charge_first, wave_vectors))
     sums = everything(part, "fold_first")
     hidden_first, values, force_first = pl.pallas_call(
         first_project_kernel,
@@ -337,9 +362,9 @@
         scratch_shapes=[pltpu.VMEM((4 * chan, waves), BF16)] * 2,
         compiler_params=vmem(6),
         name="project_first",
-    )(sums, cos_table, sin_table, wave_vectors, features, w_charge_first, w_long_first, w_value)
-
-    v_dom = lax.all_to_all(values, "kv", 0, 0, tiled=True)
+    )(sums, cos_table, sin_table, *in_hbm(wave_vectors, features, w_charge_first, w_long_first, w_value))
+
+    v_dom = lax.all_to_all(values, KV, 0, 0, tiled=True)
     to_next, to_previous = pl.pallas_call(
         halo_kernel,
         grid=(1,),
@@ -351,9 +376,9 @@
         scratch_shapes=[pltpu.VMEM((kv * atoms, hid), F32), pltpu.VMEM((2, halo, hid), F32)],
         compiler_params=vmem(6),
         name="halo_rows",
-    )(*[lists] * (halo // 128), v_dom)
-    from_below = lax.ppermute(to_next, "dom", [(i, (i + 1) % doms) for i in range(doms)])
-    from_above = lax.ppermute(to_previous, "dom", [(i, (i - 1) % doms) for i in range(doms)])
+    )(*in_hbm(*[lists] * (halo // 128)), v_dom)
+    from_below = lax.ppermute(to_next, DOM, [(i, (i + 1) % doms) for i in range(doms)])
+    from_above = lax.ppermute(to_previous, DOM, [(i, (i - 1) % doms) for i in range(doms)])
 
     steps = 8
     halves = atoms // 128
@@ -381,7 +406,7 @@
         ),
         compiler_params=vmem(6),
         name="slot_weights",
-    )(nbr_count.reshape(1, atoms), dist_t, w_filter)
+    )(*in_hbm(nbr_count.reshape(1, atoms), dist_t, w_filter))
 
     blocks = [(b, h) for b in range(slots // 8) for h in range(halves)]
     hidden_second, part = pl.pallas_call(
@@ -406,8 +431,8 @@
         compiler_params=vmem(14),
         name="neighbours",
     )(
-        nbr_count, *[index_t] * len(blocks), weights.reshape(halves, 128, slots, hid), v_dom, from_below, from_above,
-        hidden_first, w_charge_second, cos_table, sin_table, wave_vectors,
+        *in_hbm(nbr_count, *[index_t] * len(blocks)), weights.reshape(halves, 128, slots, hid), v_dom, from_below, from_above,
+        hidden_first, *in_hbm(w_charge_second), cos_table, sin_table, *in_hbm(wave_vectors),
     )
     sums = everything(part, "fold_second")
     return pl.pallas_call(
@@ -416,15 +441,19 @@
         scratch_shapes=[pltpu.VMEM((4 * chan, waves), BF16)] * 2,
         compiler_params=vmem(6),
         name="project_second",
-    )(sums, cos_table, sin_table, wave_vectors, hidden_second, w_charge_second, w_long_second, force_first)
+    )(
+        sums, cos_table, sin_table, *in_hbm(wave_vectors), hidden_second,
+        *in_hbm(w_charge_second, w_long_second), force_first,
+    )
 
 
 def solution(mesh):
+    sizes = tuple(size for _, size in PARTS)
     return jax.shard_map(
         local,
-        mesh=mesh,
+        mesh=jax.sharding.Mesh(mesh.devices.reshape(sizes), EVERY),
         in_specs=(
-            P(None, EVERY), P(EVERY, None), P(EVERY, None), P(EVERY), P(EVERY, None), P("dom", None, None),
+            P(None, EVERY), P(EVERY, None), P(EVERY, None), P(EVERY), P(EVERY, None), P(DOM, None, None),
             P(), P(), P(), P(), P(), P(), P(),
         ),
         out_specs=(P(EVERY, None), P(None, EVERY)),

time: 143 us -> 136 us (0.951)
  local copies, waits for them, and re-layouts: 8.91 us -> 0 us
  Pallas kernels: 30.6 us -> 34.2 us
  blocking collectives: 98.9 us -> 97 us
    unnamed x34 -> x0, local copies, waits for them, and re-layouts: 8.91 us -> none
    all_to_all x5 -> x7, blocking collectives: 98.9 us -> 97 us  [the longest x2 33.8 us: everything(): share = lax.all_to_all(part, COLUMN, 0, 0, tiled=True)]
  transfers between devices with their start and end apart: 2 -> 2, of which waited for: 1 -> 1; matrix products, arithmetic and copies ran while one was open for 0% -> 0% of each run, Pallas kernels for 2% -> 3%
where the time goes in v4:
time: 136 us; the launch traced here: 135 us
  blocking collectives  97 us (71%)
  Pallas kernels  34.2 us (25%)
  waiting for transfers between devices  2.09 us (2%)
    all_to_all x2, blocking collectives, everything(): share = lax.all_to_all(part, COLUMN, 0, 0, tiled=True)  33.8 us
    all_to_all x2, blocking collectives, everything(): return lax.all_to_all(share, COLUMN, 0, 0, tiled=True)  25.8 us
    all_to_all x2, blocking collectives, everything(): share = lax.all_to_all(share, PLANE, 0, 0, tiled=True)  23.5 us
    pallas_call x1, Pallas kernels, local(): pl.pallas_call(lambda *refs: neighbour_kernel(*refs, scale=scale), grid=(...  18.3 us
    all_to_all x1, blocking collectives, local(): v_dom = lax.all_to_all(values, KV, 0, 0, tiled=True)  14 us
    pallas_call x1, Pallas kernels, local(): pl.pallas_call(lambda *refs: table_kernel(*refs, scale=scale), out_shape=...  4.36 us
    pallas_call x1, Pallas kernels, local(): pl.pallas_call(weight_kernel, grid=(steps,), in_specs=[whole((1, atoms)),...  3.98 us
  transfers between devices with their start and end apart: 2, of which 1 were waited for; matrix products, arithmetic and copies ran while one was open for 0% of the time, Pallas kernels for 3%

profile of v4, /device:TPU:1, one launch (start us, length us, event | category | flops | bytes accessed | tf_op | source)
XLA Modules:
  0.0 135.2 jit_solution(6291948828389696373)
XLA Ops:
  0.6 4.4 %tables.1 = (bf16[256,2048]{1,0:T(8,128)(2,1)S(1)}, bf16[256,2048]{1,0:T(8,128)(2,1)S(1)}, bf16[512,128]{1,0:T(8,128)(2,1)S(1)}) custom-call(f32[3,256]{1,0:T(4,128)} %refs_0_.2, bf16[256,128]{1,0:T(8,128)(2,1)} %feat_ref.1, bf16[16,128]{1,0:T(8,128)(2,1)} %bitcast.64, f32[3,2048]{1,0:T(4,128)} %wave_ref.3), custom_call_target="tpu_custom_call" | custom-call | tf_op jit(solution)/shard_map/tables/pallas_call | solution.py:351
  5.0 18.7 %all_to_all.77 = bf16[16,32,128]{2,1,0:T(8,128)(2,1)S(1)} all-to-all(bf16[16,32,128]{2,1,0:T(8,128)(2,1)S(1)} %bitcast.36), channel_id=1, replica_groups=mesh['xlo'=2,'z'=8,'core'=2,'y'=4,'xhi'=2] {'z','core'}, dimensions={0} | all-to-all | bytes 262144 | tf_op jit(solution)/shard_map/all_to_all | solution.py:323
  23.7 13.6 %all_to_all.78 = bf16[16,32,128]{2,1,0:T(8,128)(2,1)S(1)} all-to-all(bf16[16,32,128]{2,1,0:T(8,128)(2,1)S(1)} %bitcast.28), channel_id=1, replica_groups=mesh['xlo'=2,'z'=8,'core'=2,'y'=4,'xhi'=2] {'xlo','y','xhi'}, dimensions={0} | all-to-all | bytes 262144 | tf_op jit(solution)/shard_map/all_to_all | solution.py:325
  37.3 12.9 %all_to_all.79 = bf16[16,32,128]{2,1,0:T(8,128)(2,1)S(1)} all-to-all(bf16[16,32,128]{2,1,0:T(8,128)(2,1)S(1)} %bitcast.30), channel_id=1, replica_groups=mesh['xlo'=2,'z'=8,'core'=2,'y'=4,'xhi'=2] {'z','core'}, dimensions={0} | all-to-all | bytes 262144 | tf_op jit(solution)/shard_map/all_to_all | solution.py:327
  50.2 2.3 %project_first.1 = (bf16[256,128]{1,0:T(8,128)(2,1)S(1)}, bf16[2048,128]{1,0:T(8,128)(2,1)S(1)}, f32[3,256]{1,0:T(4,128)S(1)}) custom-call(bf16[512,128]{1,0:T(8,128)(2,1)S(1)} %bitcast.25, bf16[256,2048]{1,0:T(8,128)(2,1)S(1)} %get-tuple-element.13.cos_ref.refs_23_, bf16[256,2048]{1,0:T(8,128)(2,1)S(1)} %get-tuple-element.14.sin_ref.refs_24_, ...), custom_call_target="tpu_custom_call" | custom-call | tf_op jit(solution)/shard_map/project_first/pallas_call | solution.py:359
  52.5 14.0 %all_to_all.80 = bf16[8,256,128]{2,1,0:T(8,128)(2,1)S(1)} all-to-all(bf16[8,256,128]{2,1,0:T(8,128)(2,1)S(1)} %bitcast.26), channel_id=1, replica_groups=mesh['xlo'=2,'z'=8,'core'=2,'y'=4,'xhi'=2] {'y','xhi'}, dimensions={0} | all-to-all | bytes 1048576 | tf_op jit(solution)/shard_map/all_to_all | solution.py:367
  66.5 2.4 %halo_rows.1 = (bf16[1024,128]{1,0:T(8,128)(2,1)S(1)}, bf16[1024,128]{1,0:T(8,128)(2,1)S(1)}) custom-call(s32[2,1024]{1,0:T(2,128)} %bitcast.53, s32[2,1024]{1,0:T(2,128)} %bitcast.54, s32[2,1024]{1,0:T(2,128)} %bitcast.55, s32[2,1024]{1,0:T(2,128)} %bitcast.56, s32[2,1024]{1,0:T(2,128)} %bitcast.57, s32[2,1024]{1,0:T(2,128)} %bitcast.58, ...), custom_call_target="tpu_custom_call" | custom-call | tf_op jit(solution)/shard_map/halo_rows/pallas_call | solution.py:368
  68.9 1.2 collective-permute-start
  70.1 0.0 collective-permute-start.1
  70.1 4.0 %slot_weights.1 = f32[256,64,128]{2,1,0:T(8,128)S(1)} custom-call(s32[1,256]{1,0:T(1,128)} %bitcast.66, f32[64,256]{1,0:T(8,128)} %bitcast.61, f32[16,128]{1,0:T(8,128)} %wf_ref.1), custom_call_target="tpu_custom_call" | custom-call | flops 134217728 | bytes 8388608 | tf_op jit(solution)/shard_map/slot_weights/pallas_call | solution.py:386
  74.1 0.0 collective-permute-done.refs_19_
  74.1 2.1 %collective-permute-done.1.refs_20_ = bf16[1024,128]{1,0:T(8,128)(2,1)S(1)} collective-permute-done((bf16[1024,128]{1,0:T(8,128)(2,1)S(1)}, bf16[1024,128]{1,0:T(8,128)(2,1)S(1)}, u32[]{:S(2)}, u32[]{:S(2)}) %collective-permute-start.1) | collective-permute-done | bytes 262176 | tf_op jit(solution)/shard_map/ppermute | solution.py:381
  76.2 18.3 %neighbours.1 = (bf16[256,128]{1,0:T(8,128)(2,1)S(1)}, bf16[512,128]{1,0:T(8,128)(2,1)S(1)}) custom-call(s32[256]{0:T(256)} %refs_0_.3, s32[64,256]{1,0:T(8,128)} %bitcast.37, s32[64,256]{1,0:T(8,128)} %bitcast.38, s32[64,256]{1,0:T(8,128)} %bitcast.39, s32[64,256]{1,0:T(8,128)} %bitcast.40, s32[64,256]{1,0:T(8,128)} %bitcast.41, s32[64,256]{1,0:T(8,128)} %bitcast.42, ...), custom_call_target="tpu_custom_call" | custom-call | tf_op jit(solution)/shard_map/neighbours/pallas_call | solution.py:412
  94.5 15.1 %all_to_all.81 = bf16[16,32,128]{2,1,0:T(8,128)(2,1)S(1)} all-to-all(bf16[16,32,128]{2,1,0:T(8,128)(2,1)S(1)} %bitcast.35), channel_id=1, replica_groups=mesh['xlo'=2,'z'=8,'core'=2,'y'=4,'xhi'=2] {'z','core'}, dimensions={0} | all-to-all | bytes 262144 | tf_op jit(solution)/shard_map/all_to_all | solution.py:323
  109.7 9.9 %all_to_all.82 = bf16[16,32,128]{2,1,0:T(8,128)(2,1)S(1)} all-to-all(bf16[16,32,128]{2,1,0:T(8,128)(2,1)S(1)} %bitcast.32), channel_id=1, replica_groups=mesh['xlo'=2,'z'=8,'core'=2,'y'=4,'xhi'=2] {'xlo','y','xhi'}, dimensions={0} | all-to-all | bytes 262144 | tf_op jit(solution)/shard_map/all_to_all | solution.py:325
  119.6 12.9 %all_to_all.83 = bf16[16,32,128]{2,1,0:T(8,128)(2,1)S(1)} all-to-all(bf16[16,32,128]{2,1,0:T(8,128)(2,1)S(1)} %bitcast.34), channel_id=1, replica_groups=mesh['xlo'=2,'z'=8,'core'=2,'y'=4,'xhi'=2] {'z','core'}, dimensions={0} | all-to-all | bytes 262144 | tf_op jit(solution)/shard_map/all_to_all | solution.py:327
  132.5 2.7 %project_second.1 = (bf16[256,128]{1,0:T(8,128)(2,1)}, f32[3,256]{1,0:T(4,128)}) custom-call(bf16[512,128]{1,0:T(8,128)(2,1)S(1)} %bitcast.24, bf16[256,2048]{1,0:T(8,128)(2,1)S(1)} %get-tuple-element.13.cos_ref.refs_23_, bf16[256,2048]{1,0:T(8,128)(2,1)S(1)} %get-tuple-element.14.sin_ref.refs_24_, f32[3,2048]{1,0:T(4,128)} %wave_ref.3, ...), custom_call_target="tpu_custom_call" | custom-call | tf_op jit(solution)/shard_map/project_second/pallas_call | solution.py:438
  (4 shorter events, 0.1 us)
Async XLA Ops:
  68.9 5.2 %collective-permute-start = (bf16[1024,128]{1,0:T(8,128)(2,1)S(1)}, bf16[1024,128]{1,0:T(8,128)(2,1)S(1)}, u32[]{:S(2)}, u32[]{:S(2)}) collective-permute-start(bf16[1024,128]{1,0:T(8,128)(2,1)S(1)} %get-tuple-element.16), channel_id=1, source_target_pairs={{0,8},{8,16},{16,24},{24,32},{32,40},{40,48},{48,56},{56,64},{64,7... | collective-permute-start | bytes 786440 | tf_op jit(solution)/shard_map/ppermute | solution.py:380
  70.1 6.1 %collective-permute-start.1 = (bf16[1024,128]{1,0:T(8,128)(2,1)S(1)}, bf16[1024,128]{1,0:T(8,128)(2,1)S(1)}, u32[]{:S(2)}, u32[]{:S(2)}) collective-permute-start(bf16[1024,128]{1,0:T(8,128)(2,1)S(1)} %get-tuple-element.17), channel_id=1, source_target_pairs={{0,248},{8,0},{16,8},{24,16},{32,24},{40,32},{48,40},{56,48},{64,5... | collective-permute-start | bytes 786440 | tf_op jit(solution)/shard_map/ppermute | solution.py:381

commit v5 on v4

--- a/solution.py
+++ b/solution.py
@@ -16,8 +16,8 @@
 EVERY = tuple(name for name, _ in PARTS)
 DOM = ("xlo", "z", "core")
 KV = ("y", "xhi")
-COLUMN = ("z", "core")
-PLANE = ("xlo", "y", "xhi")
+LINE = ("z",)
+PLANE = ("xlo", "core", "y", "xhi")
 
 COS_COEF = (
     1.0,
@@ -83,8 +83,14 @@
         part_ref[t * 2 * chan + chan : (t + 1) * 2 * chan, :] = sin_sum[:, lanes].astype(BF16)
 
 
-def table_kernel(pos_ref, feat_ref, wc_ref, wave_ref, cos_ref, sin_ref, part_ref, turns, pad, *, scale):
+def table_kernel(*refs, scale):
+    later = (len(refs) - 6) // 2
+    pos_ref, kept_in, cos_ref, sin_ref, part_ref = refs[0], refs[1 : 1 + later], *refs[1 + later : 4 + later]
+    kept_out, turns, pad = refs[4 + later : -2], *refs[-2:]
+    feat_ref, wc_ref, wave_ref = kept_in[:3]
     atoms, waves = cos_ref.shape
+    for in_ref, out_ref in zip(kept_in, kept_out):
+        out_ref[...] = in_ref[...]
     pad[...] = jnp.zeros_like(pad)
     pad[0:3, :] = pos_ref[...] * (1.0 / CELL)
     columns = jnp.transpose(pad[...])
@@ -118,7 +124,7 @@
     total = in_ref[0:rows, :].astype(F32)
     for m in range(1, members):
         total = total + in_ref[m * rows : (m + 1) * rows, :].astype(F32)
-    total = total.astype(BF16)
+    total = total.astype(out_ref.dtype)
     for m in range(copies):
         out_ref[m * rows : (m + 1) * rows, :] = total
 
@@ -262,20 +268,21 @@
     for half in range(halves):
 
         def one_atom(a, carry, half=half):
-            lane = step * atoms + a
-            at = pl.ds(pl.multiple_of((half * 128 + lane) * 8, 8), 8)
+            atom = half * 128 + step * atoms + a
+            at = pl.ds(pl.multiple_of(atom * 8, 8), 8)
+            spots = [atom + q * halves * 128 for q in range(4)]
 
             def some_slots(blocks):
                 total = jnp.zeros((8, 128), F32)
                 for b in blocks:
-                    rows = [index_refs[b * halves + half][s, lane] for s in range(8)]
+                    rows = [index_refs[2 * b + s // 4][spots[s % 4]] for s in range(8)]
                     total = total + row_tile(table, rows, bits) * weight_ref[half, a, 8 * b : 8 * b + 8, :]
                 return total
 
             middle = slots // 16
             sums[at, :] = some_slots(range(middle))
 
-            @pl.when(count_ref[half * 128 + lane] > middle * 8)
+            @pl.when(count_ref[atom] > middle * 8)
             def _():
                 sums[at, :] = sums[at, :] + some_slots(range(middle, slots // 8))
 
@@ -307,24 +314,24 @@
     return pltpu.CompilerParams(vmem_limit_bytes=mib * 1024 * 1024)
 
 
-def fold(sums, members, copies, name):
+def fold(sums, members, copies, kind, name):
     rows = sums.shape[0] // members
     return pl.pallas_call(
         lambda *refs: fold_kernel(*refs, members=members, copies=copies),
-        out_shape=shape((copies * rows, sums.shape[1]), BF16),
+        out_shape=shape((copies * rows, sums.shape[1]), kind),
         compiler_params=vmem(2),
         name=name,
     )(sums)
 
 
 def everything(part, name):
-    column = lax.axis_size(COLUMN)
+    line = lax.axis_size(LINE)
     plane = lax.axis_size(PLANE)
-    share = lax.all_to_all(part, COLUMN, 0, 0, tiled=True)
-    share = fold(share, column, plane, name + "_column")
-    share = lax.all_to_all(share, PLANE, 0, 0, tiled=True)
-    share = fold(share, plane, column, name + "_plane")
-    return lax.all_to_all(share, COLUMN, 0, 0, tiled=True)
+    share = lax.all_to_all(part, PLANE, 0, 0, tiled=True)
+    share = fold(share, plane, line, F32, name + "_plane")
+    share = lax.all_to_all(share, LINE, 0, 0, tiled=True)
+    share = fold(share, line, plane, BF16, name + "_line")
+    return lax.all_to_all(share, PLANE, 0, 0, tiled=True)
 
 
 def local(
@@ -348,13 +355,24 @@
     index_t = nbr_index.T
     dist_t = nbr_dist.T
 
-    cos_table, sin_table, part = pl.pallas_call(
+    kept = (
+        features, w_charge_first, wave_vectors, w_long_first, w_value, w_charge_second, w_long_second,
+        dist_t, nbr_count.reshape(1, atoms), w_filter,
+    )
+    cos_table, sin_table, part, *kept = pl.pallas_call(
         lambda *refs: table_kernel(*refs, scale=scale),
-        out_shape=(shape((atoms, waves), BF16), shape((atoms, waves), BF16), shape((part_rows, 128), BF16)),
+        out_shape=(
+            shape((atoms, waves), BF16), shape((atoms, waves), BF16), shape((part_rows, 128), BF16),
+            *(shape(a.shape, a.dtype) for a in kept),
+        ),
         scratch_shapes=[pltpu.VMEM((3, atoms, 128), F32), pltpu.VMEM((8, atoms), F32)],
         compiler_params=vmem(6),
         name="tables",
-    )(*in_hbm(positions, features, w_charge_first, wave_vectors))
+    )(*in_hbm(positions, *kept))
+    (
+        features, w_charge_first, wave_vectors, w_long_first, w_value, w_charge_second, w_long_second,
+        dist_t, count_row, w_filter,
+    ) = kept
     sums = everything(part, "fold_first")
     hidden_first, values, force_first = pl.pallas_call(
         first_project_kernel,
@@ -362,7 +380,7 @@
         scratch_shapes=[pltpu.VMEM((4 * chan, waves), BF16)] * 2,
         compiler_params=vmem(6),
         name="project_first",
-    )(sums, cos_table, sin_table, *in_hbm(wave_vectors, features, w_charge_first, w_long_first, w_value))
+    )(sums, cos_table, sin_table, wave_vectors, features, w_charge_first, w_long_first, w_value)
 
     v_dom = lax.all_to_all(values, KV, 0, 0, tiled=True)
     to_next, to_previous = pl.pallas_call(
@@ -406,14 +424,16 @@
         ),
         compiler_params=vmem(6),
         name="slot_weights",
-    )(*in_hbm(nbr_count.reshape(1, atoms), dist_t, w_filter))
-
-    blocks = [(b, h) for b in range(slots // 8) for h in range(halves)]
+    )(count_row, dist_t, w_filter)
+
+    blocks = range(slots // 4)
+    index_t, _ = lax.optimization_barrier((index_t, to_next))
+    index_flat = index_t.reshape(slots * atoms)
     hidden_second, part = pl.pallas_call(
         lambda *refs: neighbour_kernel(*refs, scale=scale),
         grid=(steps,),
         in_specs=[smem] + [
-            pl.BlockSpec((8, 128), lambda i, at=at: at, memory_space=pltpu.SMEM) for at in blocks
+            pl.BlockSpec((4 * atoms,), lambda i, at=at: (at,), memory_space=pltpu.SMEM) for at in blocks
         ] + [
             pl.BlockSpec((halves, 128 // steps, slots, hid), lambda i: (0, i, 0, 0)),
             whole((kv * atoms, hid)),
@@ -431,8 +451,8 @@
         compiler_params=vmem(14),
         name="neighbours",
     )(
-        *in_hbm(nbr_count, *[index_t] * len(blocks)), weights.reshape(halves, 128, slots, hid), v_dom, from_below, from_above,
-        hidden_first, *in_hbm(w_charge_second), cos_table, sin_table, *in_hbm(wave_vectors),
+        *in_hbm(nbr_count), *[index_flat] * len(blocks), weights.reshape(halves, 128, slots, hid), v_dom, from_below, from_above,
+        hidden_first, w_charge_second, cos_table, sin_table, wave_vectors,
     )
     sums = everything(part, "fold_second")
     return pl.pallas_call(
@@ -442,8 +462,7 @@
         compiler_params=vmem(6),
         name="project_second",
     )(
-        sums, cos_table, sin_table, *in_hbm(wave_vectors), hidden_second,
-        *in_hbm(w_charge_second, w_long_second), force_first,
+        sums, cos_table, sin_table, wave_vectors, hidden_second, w_charge_second, w_long_second, force_first,
     )
 
 

time: 136 us -> 128 us (0.941)
  Pallas kernels: 34.2 us -> 29.5 us
  blocking collectives: 97 us -> 94.1 us
    pallas_call x1, Pallas kernels: 18.3 us -> 15.9 us  [local(): pl.pallas_call(lambda *refs: neighbour_kernel(*refs, scale=scale), grid=(...]
    all_to_all x6, blocking collectives: 83.1 us -> 80.7 us  [the longest x2 30.5 us: everything(): share = lax.all_to_all(part, PLANE, 0, 0, tiled=True)]
    ppermute x1, starting transfers between devices: 0.01 us -> 1.9 us  [local(): lax.ppermute(to_previous, DOM, [(i, (i - 1) % doms) for i in range(doms)])]
  transfers between devices with their start and end apart: 2 -> 2, of which waited for: 1 -> 1; matrix products, arithmetic and copies ran while one was open for 0% -> 0% of each run, Pallas kernels for 3% -> 2%
where the time goes in v5:
time: 128 us; the launch traced here: 127 us
  blocking collectives  94.1 us (74%)
  Pallas kernels  29.5 us (23%)
  starting transfers between devices  2.16 us (2%)
    all_to_all x2, blocking collectives, everything(): share = lax.all_to_all(part, PLANE, 0, 0, tiled=True)  30.5 us
    all_to_all x2, blocking collectives, everything(): return lax.all_to_all(share, PLANE, 0, 0, tiled=True)  25.5 us
    all_to_all x2, blocking collectives, everything(): share = lax.all_to_all(share, LINE, 0, 0, tiled=True)  24.7 us
    pallas_call x1, Pallas kernels, local(): pl.pallas_call(lambda *refs: neighbour_kernel(*refs, scale=scale), grid=(...  15.9 us
    all_to_all x1, blocking collectives, local(): v_dom = lax.all_to_all(values, KV, 0, 0, tiled=True)  13.4 us
    pallas_call x1, Pallas kernels, local(): pl.pallas_call(lambda *refs: table_kernel(*refs, scale=scale), out_shape=...  4.57 us
    pallas_call x1, Pallas kernels, local(): pl.pallas_call(weight_kernel, grid=(steps,), in_specs=[whole((1, atoms)),...  3.1 us
  transfers between devices with their start and end apart: 2, of which 1 were waited for; matrix products, arithmetic and copies ran while one was open for 0% of the time, Pallas kernels for 2%

profile of v5, /device:TPU:1, one launch (start us, length us, event | category | flops | bytes accessed | tf_op | source)
XLA Modules:
  0.0 127.3 jit_solution(11855573256416285300)
XLA Ops:
  0.6 0.0 copy-start
  0.6 4.6 %tables.1 = (bf16[256,2048]{1,0:T(8,128)(2,1)S(1)}, bf16[256,2048]{1,0:T(8,128)(2,1)S(1)}, bf16[512,128]{1,0:T(8,128)(2,1)S(1)}, bf16[256,128]{1,0:T(8,128)(2,1)...) custom-call(f32[3,256]{1,0:T(4,128)} %refs_0_.2, ...), custom_call_target="tpu_custom_call" | custom-call | tf_op jit(solution)/shard_map/tables/pallas_call | solution.py:362
  5.2 16.1 %all_to_all.77 = bf16[32,16,128]{2,1,0:T(8,128)(2,1)S(1)} all-to-all(bf16[32,16,128]{2,1,0:T(8,128)(2,1)S(1)} %bitcast.53), channel_id=1, replica_groups=mesh['xlo'=2,'z'=8,'core'=2,'y'=4,'xhi'=2] {'xlo','core','y','xhi'}, dimensions={0} | all-to-all | bytes 262144 | tf_op jit(solution)/shard_map/all_to_all | solution.py:330
  21.3 15.2 %all_to_all.78 = f32[8,16,128]{2,1,0:T(8,128)S(1)} all-to-all(f32[8,16,128]{2,1,0:T(8,128)S(1)} %bitcast.49), channel_id=1, replica_groups=mesh['xlo'=2,'z'=8,'core'=2,'y'=4,'xhi'=2] {'z'}, dimensions={0} | all-to-all | bytes 131072 | tf_op jit(solution)/shard_map/all_to_all | solution.py:332
  36.6 12.8 %all_to_all.79 = bf16[32,16,128]{2,1,0:T(8,128)(2,1)S(1)} all-to-all(bf16[32,16,128]{2,1,0:T(8,128)(2,1)S(1)} %bitcast.46), channel_id=1, replica_groups=mesh['xlo'=2,'z'=8,'core'=2,'y'=4,'xhi'=2] {'xlo','core','y','xhi'}, dimensions={0} | all-to-all | bytes 262144 | tf_op jit(solution)/shard_map/all_to_all | solution.py:334
  49.4 1.4 %project_first.1 = (bf16[256,128]{1,0:T(8,128)(2,1)S(1)}, bf16[2048,128]{1,0:T(8,128)(2,1)S(1)}, f32[3,256]{1,0:T(4,128)S(1)}) custom-call(bf16[512,128]{1,0:T(8,128)(2,1)S(1)} %bitcast.43, bf16[256,2048]{1,0:T(8,128)(2,1)S(1)} %get-tuple-element.24.cos_ref.refs_23_, bf16[256,2048]{1,0:T(8,128)(2,1)S(1)} %get-tuple-element.25.sin_ref.refs_24_, ...), custom_call_target="tpu_custom_call" | custom-call | tf_op jit(solution)/shard_map/project_first/pallas_call | solution.py:377
  50.8 13.4 %all_to_all.80 = bf16[8,256,128]{2,1,0:T(8,128)(2,1)S(1)} all-to-all(bf16[8,256,128]{2,1,0:T(8,128)(2,1)S(1)} %bitcast.44), channel_id=1, replica_groups=mesh['xlo'=2,'z'=8,'core'=2,'y'=4,'xhi'=2] {'y','xhi'}, dimensions={0} | all-to-all | bytes 1048576 | tf_op jit(solution)/shard_map/all_to_all | solution.py:385
  64.2 2.4 %halo_rows.1 = (bf16[1024,128]{1,0:T(8,128)(2,1)S(1)}, bf16[1024,128]{1,0:T(8,128)(2,1)S(1)}) custom-call(s32[2,1024]{1,0:T(2,128)} %bitcast.55, s32[2,1024]{1,0:T(2,128)} %bitcast.56, s32[2,1024]{1,0:T(2,128)} %bitcast.57, s32[2,1024]{1,0:T(2,128)} %bitcast.58, s32[2,1024]{1,0:T(2,128)} %bitcast.59, s32[2,1024]{1,0:T(2,128)} %bitcast.60, ...), custom_call_target="tpu_custom_call" | custom-call | tf_op jit(solution)/shard_map/halo_rows/pallas_call | solution.py:386
  66.6 1.9 %collective-permute-start.1 = (bf16[1024,128]{1,0:T(8,128)(2,1)S(1)}, bf16[1024,128]{1,0:T(8,128)(2,1)S(1)}, u32[]{:S(2)}, u32[]{:S(2)}) collective-permute-start(bf16[1024,128]{1,0:T(8,128)(2,1)S(1)} %get-tuple-element.37), channel_id=1, source_target_pairs={{0,248},{8,0},{16,8},{24,16},{32,24},{40,32},{48,40},{56,48},{64,5... | collective-permute-start | bytes 786440 | tf_op jit(solution)/shard_map/ppermute | solution.py:399
  68.5 0.3 collective-permute-start
  68.8 3.1 %slot_weights.1 = f32[256,64,128]{2,1,0:T(8,128)S(1)} custom-call(s32[1,256]{1,0:T(1,128)S(1)} %get-tuple-element.34.count_ref, f32[64,256]{1,0:T(8,128)S(1)} %get-tuple-element.35.dist_ref, f32[16,128]{1,0:T(8,128)S(1)} %get-tuple-element.36.wf_ref), custom_call_target="tpu_custom_call" | custom-call | flops 134217728 | bytes 8388608 | tf_op jit(solution)/shard_map/slot_weights/pallas_call | solution.py:404
  71.9 0.0 copy-done
  72.0 0.8 collective-permute-done.1.refs_20_
  72.8 0.0 collective-permute-done.refs_19_
  72.8 15.9 %neighbours.1 = (bf16[256,128]{1,0:T(8,128)(2,1)S(1)}, bf16[512,128]{1,0:T(8,128)(2,1)S(1)}) custom-call(s32[256]{0:T(256)} %refs_0_.3, s32[16384]{0:T(1024)S(1)} %bitcast.24, s32[16384]{0:T(1024)S(1)} %bitcast.25, s32[16384]{0:T(1024)S(1)} %bitcast.26, s32[16384]{0:T(1024)S(1)} %bitcast.27, s32[16384]{0:T(1024)S(1)} %bitcast.28, s32[16384]{0:T(1024)S(1)} %bitcast.29, ...), custom_call_target="tpu_custom_call" | custom-call | tf_op jit(solution)/shard_map/neighbours/pallas_call | solution.py:432
  88.7 14.4 %all_to_all.81 = bf16[32,16,128]{2,1,0:T(8,128)(2,1)S(1)} all-to-all(bf16[32,16,128]{2,1,0:T(8,128)(2,1)S(1)} %bitcast.54), channel_id=1, replica_groups=mesh['xlo'=2,'z'=8,'core'=2,'y'=4,'xhi'=2] {'xlo','core','y','xhi'}, dimensions={0} | all-to-all | bytes 262144 | tf_op jit(solution)/shard_map/all_to_all | solution.py:330
  103.1 9.5 %all_to_all.82 = f32[8,16,128]{2,1,0:T(8,128)S(1)} all-to-all(f32[8,16,128]{2,1,0:T(8,128)S(1)} %bitcast.51), channel_id=1, replica_groups=mesh['xlo'=2,'z'=8,'core'=2,'y'=4,'xhi'=2] {'z'}, dimensions={0} | all-to-all | bytes 131072 | tf_op jit(solution)/shard_map/all_to_all | solution.py:332
  112.7 12.6 %all_to_all.83 = bf16[32,16,128]{2,1,0:T(8,128)(2,1)S(1)} all-to-all(bf16[32,16,128]{2,1,0:T(8,128)(2,1)S(1)} %bitcast.48), channel_id=1, replica_groups=mesh['xlo'=2,'z'=8,'core'=2,'y'=4,'xhi'=2] {'xlo','core','y','xhi'}, dimensions={0} | all-to-all | bytes 262144 | tf_op jit(solution)/shard_map/all_to_all | solution.py:334
  125.3 1.9 %project_second.1 = (bf16[256,128]{1,0:T(8,128)(2,1)}, f32[3,256]{1,0:T(4,128)}) custom-call(bf16[512,128]{1,0:T(8,128)(2,1)S(1)} %bitcast.42, bf16[256,2048]{1,0:T(8,128)(2,1)S(1)} %get-tuple-element.24.cos_ref.refs_23_, bf16[256,2048]{1,0:T(8,128)(2,1)S(1)} %get-tuple-element.25.sin_ref.refs_24_, f32[3,2048]{1,0:T(4,128)S(1)} %get-tuple-element.26.wave_ref.refs_25_, ...), custom_call_target="tpu_custom_call" | custom-call | tf_op jit(solution)/shard_map/project_second/pallas_call | solution.py:458
  (5 shorter events, 0.1 us)
Async XLA Ops:
  0.6 71.3 %copy-start = (s32[256,64]{0,1:T(8,128)S(1)}, s32[256,64]{0,1:T(8,128)}, u32[]{:S(2)}) copy-start(s32[256,64]{0,1:T(8,128)} %param.15) | copy-start | bytes 196612
  66.6 6.1 %collective-permute-start.1 = (bf16[1024,128]{1,0:T(8,128)(2,1)S(1)}, bf16[1024,128]{1,0:T(8,128)(2,1)S(1)}, u32[]{:S(2)}, u32[]{:S(2)}) collective-permute-start(bf16[1024,128]{1,0:T(8,128)(2,1)S(1)} %get-tuple-element.37), channel_id=1, source_target_pairs={{0,248},{8,0},{16,8},{24,16},{32,24},{40,32},{48,40},{56,48},{64,5... | collective-permute-start | bytes 786440 | tf_op jit(solution)/shard_map/ppermute | solution.py:399
  68.5 4.2 %collective-permute-start = (bf16[1024,128]{1,0:T(8,128)(2,1)S(1)}, bf16[1024,128]{1,0:T(8,128)(2,1)S(1)}, u32[]{:S(2)}, u32[]{:S(2)}) collective-permute-start(bf16[1024,128]{1,0:T(8,128)(2,1)S(1)} %get-tuple-element.32), channel_id=1, source_target_pairs={{0,8},{8,16},{16,24},{24,32},{32,40},{40,48},{48,56},{56,64},{64,7... | collective-permute-start | bytes 786440 | tf_op jit(solution)/shard_map/ppermute | solution.py:398

commit v6 on v5

--- a/solution.py
+++ b/solution.py
@@ -20,22 +20,20 @@
 PLANE = ("xlo", "core", "y", "xhi")
 
 COS_COEF = (
-    1.0,
-    -19.73920440673828,
-    64.93911743164062,
-    -85.45014190673828,
-    60.16762924194336,
-    -25.967599868774414,
-    6.528658390045166,
+    0.9999992251396179,
+    -19.738981246948242,
+    64.92865753173828,
+    -85.27162170410156,
+    58.79049301147461,
+    -21.07110595703125,
 )
 SIN_COEF = (
-    6.2831854820251465,
-    -41.34170150756836,
-    81.60513305664062,
-    -76.70301818847656,
-    42.02592849731445,
-    -14.899847030639648,
-    3.2381374835968018,
+    6.283185005187988,
+    -41.341590881347656,
+    81.59994506835938,
+    -76.61447143554688,
+    41.3428840637207,
+    -12.471243858337402,
 )
 
 NN = (((1,), (0,)), ((), ()))
@@ -193,23 +191,22 @@
     return [(sub & bit) != 0 for bit in (1, 2, 4)]
 
 
-def halo_kernel(*refs):
-    lists, (values_ref, below_ref, above_ref, table, picked) = refs[:-5], refs[-5:]
-    table[...] = values_ref[...].astype(F32)
+def halo_kernel(*refs, far):
+    lists, (values_ref, out_ref, table, picked) = refs[:-4], refs[-4:]
+    core = lax.axis_index("core")
+    side = 1 - core if far else core
+    table[0 : values_ref.shape[0], :] = values_ref[...].astype(F32)
     bits = sublane_bits()
 
     def some_rows(g, carry):
         first = g * 8
-        at = [[first + j for j in range(8)] for side in (0, 1)]
         for b, list_ref in enumerate(lists):
-            for side in (0, 1):
-                rows = [list_ref[side, lane] for lane in at[side]]
-                picked[side, pl.ds(pl.multiple_of(b * 128 + first, 8), 8), :] = row_tile(table, rows, bits)
+            rows = [list_ref[side, first + j] for j in range(8)]
+            picked[pl.ds(pl.multiple_of(b * 128 + first, 8), 8), :] = row_tile(table, rows, bits)
         return carry
 
     lax.fori_loop(0, 16, some_rows, 0)
-    below_ref[...] = picked[0].astype(BF16)
-    above_ref[...] = picked[1].astype(BF16)
+    out_ref[...] = picked[...].astype(BF16)
 
 
 def weight_kernel(count_ref, dist_ref, wf_ref, out_ref, turned, near, taper, wide):
@@ -250,56 +247,46 @@
 def neighbour_kernel(*refs, scale):
     count_ref, index_refs = refs[0], refs[1:-13]
     (
-        weight_ref, values_ref, below_ref, above_ref, hidden_ref, wc_ref, cos_ref, sin_ref, wave_ref,
+        weight_ref, values_ref, far_ref, near_ref, hidden_ref, wc_ref, cos_ref, sin_ref, wave_ref,
         hidden_out, part_ref, table, sums,
     ) = refs[-13:]
-    step = pl.program_id(0)
     own = values_ref.shape[0]
-    halo = below_ref.shape[0]
-    halves, atoms, slots, _ = weight_ref.shape
-
-    @pl.when(step == 0)
-    def _():
-        table[0:own, :] = values_ref[...].astype(F32)
-        table[own : own + halo, :] = below_ref[...].astype(F32)
-        table[own + halo : own + 2 * halo, :] = above_ref[...].astype(F32)
-
+    halo = far_ref.shape[0]
+    atoms, slots, _ = weight_ref.shape
+    core = lax.axis_index("core")
+    table[0:own, :] = values_ref[...].astype(F32)
+    table[pl.ds(pl.multiple_of(own + (1 - core) * halo, 8), halo), :] = near_ref[...].astype(F32)
+    table[pl.ds(pl.multiple_of(own + core * halo, 8), halo), :] = far_ref[...].astype(F32)
     bits = sublane_bits()
-    for half in range(halves):
-
-        def one_atom(a, carry, half=half):
-            atom = half * 128 + step * atoms + a
-            at = pl.ds(pl.multiple_of(atom * 8, 8), 8)
-            spots = [atom + q * halves * 128 for q in range(4)]
-
-            def some_slots(blocks):
-                total = jnp.zeros((8, 128), F32)
-                for b in blocks:
-                    rows = [index_refs[2 * b + s // 4][spots[s % 4]] for s in range(8)]
-                    total = total + row_tile(table, rows, bits) * weight_ref[half, a, 8 * b : 8 * b + 8, :]
-                return total
-
-            middle = slots // 16
-            sums[at, :] = some_slots(range(middle))
-
-            @pl.when(count_ref[atom] > middle * 8)
-            def _():
-                sums[at, :] = sums[at, :] + some_slots(range(middle, slots // 8))
-
-            return carry
-
-        lax.fori_loop(0, atoms, one_atom, 0)
-
-    @pl.when(step == pl.num_programs(0) - 1)
-    def _():
-        count = hidden_ref.shape[0]
-        message = sums[pl.ds(0, count, stride=8), :]
-        for k in range(1, 8):
-            message = message + sums[pl.ds(k, count, stride=8), :]
-        hidden = (hidden_ref[...].astype(F32) + silu(message)).astype(BF16)
-        hidden_out[...] = hidden
-        charge_t = dot(wc_ref[...], hidden, NT)
-        structure_part(charge_t, cos_ref, sin_ref, wave_ref, part_ref, scale)
+
+    def one_atom(atom, carry):
+        at = pl.ds(pl.multiple_of(atom * 8, 8), 8)
+        spots = [atom + q * atoms for q in range(4)]
+
+        def some_slots(blocks):
+            total = jnp.zeros((8, 128), F32)
+            for b in blocks:
+                rows = [index_refs[2 * b + s // 4][spots[s % 4]] for s in range(8)]
+                total = total + row_tile(table, rows, bits) * weight_ref[atom, 8 * b : 8 * b + 8, :]
+            return total
+
+        middle = slots // 16
+        sums[at, :] = some_slots(range(middle))
+
+        @pl.when(count_ref[atom] > middle * 8)
+        def _():
+            sums[at, :] = sums[at, :] + some_slots(range(middle, slots // 8))
+
+        return carry
+
+    lax.fori_loop(0, atoms, one_atom, 0)
+    message = sums[pl.ds(0, atoms, stride=8), :]
+    for k in range(1, 8):
+        message = message + sums[pl.ds(k, atoms, stride=8), :]
+    hidden = (hidden_ref[...].astype(F32) + silu(message)).astype(BF16)
+    hidden_out[...] = hidden
+    charge_t = dot(wc_ref[...], hidden, NT)
+    structure_part(charge_t, cos_ref, sin_ref, wave_ref, part_ref, scale)
 
 
 def shape(dims, kind):
@@ -314,23 +301,22 @@
     return pltpu.CompilerParams(vmem_limit_bytes=mib * 1024 * 1024)
 
 
-def fold(sums, members, copies, kind, name):
+def fold(sums, members, copies, kind):
     rows = sums.shape[0] // members
     return pl.pallas_call(
         lambda *refs: fold_kernel(*refs, members=members, copies=copies),
         out_shape=shape((copies * rows, sums.shape[1]), kind),
         compiler_params=vmem(2),
-        name=name,
     )(sums)
 
 
-def everything(part, name):
+def everything(part):
     line = lax.axis_size(LINE)
     plane = lax.axis_size(PLANE)
     share = lax.all_to_all(part, PLANE, 0, 0, tiled=True)
-    share = fold(share, plane, line, F32, name + "_plane")
+    share = fold(share, plane, line, F32)
     share = lax.all_to_all(share, LINE, 0, 0, tiled=True)
-    share = fold(share, line, plane, BF16, name + "_line")
+    share = fold(share, line, plane, BF16)
     return lax.all_to_all(share, PLANE, 0, 0, tiled=True)
 
 
@@ -373,7 +359,7 @@
         features, w_charge_first, wave_vectors, w_long_first, w_value, w_charge_second, w_long_second,
         dist_t, count_row, w_filter,
     ) = kept
-    sums = everything(part, "fold_first")
+    sums = everything(part)
     hidden_first, values, force_first = pl.pallas_call(
         first_project_kernel,
         out_shape=(shape((atoms, hid), BF16), shape((kv * atoms, hid), BF16), shape((3, atoms), F32)),
@@ -383,23 +369,29 @@
     )(sums, cos_table, sin_table, wave_vectors, features, w_charge_first, w_long_first, w_value)
 
     v_dom = lax.all_to_all(values, KV, 0, 0, tiled=True)
-    to_next, to_previous = pl.pallas_call(
-        halo_kernel,
-        grid=(1,),
-        in_specs=[
-            pl.BlockSpec((2, 128), lambda i, b=b: (0, b), memory_space=pltpu.SMEM) for b in range(halo // 128)
-        ] + [pl.BlockSpec((kv * atoms, hid), lambda i: (0, 0))],
-        out_specs=(pl.BlockSpec((halo, hid), lambda i: (0, 0)), pl.BlockSpec((halo, hid), lambda i: (0, 0))),
-        out_shape=(shape((halo, hid), BF16), shape((halo, hid), BF16)),
-        scratch_shapes=[pltpu.VMEM((kv * atoms, hid), F32), pltpu.VMEM((2, halo, hid), F32)],
-        compiler_params=vmem(6),
-        name="halo_rows",
-    )(*in_hbm(*[lists] * (halo // 128)), v_dom)
-    from_below = lax.ppermute(to_next, DOM, [(i, (i + 1) % doms) for i in range(doms)])
-    from_above = lax.ppermute(to_previous, DOM, [(i, (i - 1) % doms) for i in range(doms)])
+
+    def halo_rows(far, source):
+        return pl.pallas_call(
+            lambda *refs: halo_kernel(*refs, far=far),
+            grid=(1,),
+            in_specs=[
+                pl.BlockSpec((2, 128), lambda i, b=b: (0, b), memory_space=pltpu.SMEM) for b in range(halo // 128)
+            ] + [pl.BlockSpec((kv * atoms, hid), lambda i: (0, 0))],
+            out_specs=pl.BlockSpec((halo, hid), lambda i: (0, 0)),
+            out_shape=shape((halo, hid), BF16),
+            scratch_shapes=[pltpu.VMEM((kv * atoms + 8, hid), F32), pltpu.VMEM((halo, hid), F32)],
+            compiler_params=vmem(6),
+            cost_estimate=pl.CostEstimate(flops=halo * hid, bytes_accessed=4 * kv * atoms * hid, transcendentals=0),
+            name="halo_far" if far else "halo_near",
+        )(*in_hbm(*[lists] * (halo // 128)), source)
+
+    to_far = halo_rows(True, v_dom)
+    to_far, source, index_t = lax.optimization_barrier((to_far, v_dom, index_t))
+    from_far = lax.ppermute(to_far, DOM, [(i, (i - 1 + 2 * (i % 2)) % doms) for i in range(doms)])
+    to_near = halo_rows(False, source)
+    from_near = lax.ppermute(to_near, DOM, [(i, i + 1 - 2 * (i % 2)) for i in range(doms)])
 
     steps = 8
-    halves = atoms // 128
     whole = lambda dims: pl.BlockSpec(dims, lambda i: (0, 0))
     weights = pl.pallas_call(
         weight_kernel,
@@ -427,15 +419,14 @@
     )(count_row, dist_t, w_filter)
 
     blocks = range(slots // 4)
-    index_t, _ = lax.optimization_barrier((index_t, to_next))
     index_flat = index_t.reshape(slots * atoms)
     hidden_second, part = pl.pallas_call(
         lambda *refs: neighbour_kernel(*refs, scale=scale),
-        grid=(steps,),
+        grid=(1,),
         in_specs=[smem] + [
             pl.BlockSpec((4 * atoms,), lambda i, at=at: (at,), memory_space=pltpu.SMEM) for at in blocks
         ] + [
-            pl.BlockSpec((halves, 128 // steps, slots, hid), lambda i: (0, i, 0, 0)),
+            pl.BlockSpec((atoms, slots, hid), lambda i: (0, 0, 0)),
             whole((kv * atoms, hid)),
             whole((halo, hid)),
             whole((halo, hid)),
@@ -447,14 +438,14 @@
         ],
         out_specs=(whole((atoms, hid)), whole((part_rows, 128))),
         out_shape=(shape((atoms, hid), BF16), shape((part_rows, 128), BF16)),
-        scratch_shapes=[pltpu.VMEM((kv * atoms + 2 * halo, hid), F32), pltpu.VMEM((8 * atoms, hid), F32)],
-        compiler_params=vmem(14),
+        scratch_shapes=[pltpu.VMEM((kv * atoms + 2 * halo + 8, hid), F32), pltpu.VMEM((8 * atoms, hid), F32)],
+        compiler_params=vmem(20),
         name="neighbours",
     )(
-        *in_hbm(nbr_count), *[index_flat] * len(blocks), weights.reshape(halves, 128, slots, hid), v_dom, from_below, from_above,
+        *in_hbm(nbr_count), *[index_flat] * len(blocks), weights, v_dom, from_far, from_near,
         hidden_first, w_charge_second, cos_table, sin_table, wave_vectors,
     )
-    sums = everything(part, "fold_second")
+    sums = everything(part)
     return pl.pallas_call(
         last_project_kernel,
         out_shape=(shape((atoms, hid), BF16), shape((3, atoms), F32)),

time: 128 us -> 127 us (level)
  blocking collectives: 94.1 us -> 92 us
  waiting for transfers between devices: 0.81 us -> 2.65 us
    all_to_all x2, blocking collectives: 30.5 us -> 28.4 us  [everything(): share = lax.all_to_all(part, PLANE, 0, 0, tiled=True)]
    ppermute x2, waiting for transfers between devices: 0.81 us -> 2.65 us  [the longest x1 2.65 us: local(): lax.ppermute(to_far, DOM, [(i, (i - 1 + 2 * (i % 2)) % doms) for i in ran...]
    pallas_call x1, Pallas kernels: 15.9 us -> 14.5 us  [local(): pl.pallas_call(lambda *refs: neighbour_kernel(*refs, scale=scale), grid=(...]
    pallas_call x1 -> x2, Pallas kernels: 2.44 us -> 3.47 us  [halo_rows(): pl.pallas_call(lambda *refs: halo_kernel(*refs, far=far), grid=(1,), in_s...]
where the time goes in v6:
time: 127 us
  blocking collectives  92 us (72%)
  Pallas kernels  28.9 us (23%)
  waiting for transfers between devices  2.65 us (2%)
  starting transfers between devices  2.18 us (2%)
    all_to_all x2, blocking collectives, everything(): share = lax.all_to_all(part, PLANE, 0, 0, tiled=True)  28.4 us
    all_to_all x2, blocking collectives, everything(): return lax.all_to_all(share, PLANE, 0, 0, tiled=True)  25.5 us
    all_to_all x2, blocking collectives, everything(): share = lax.all_to_all(share, LINE, 0, 0, tiled=True)  24.7 us
    pallas_call x1, Pallas kernels, local(): pl.pallas_call(lambda *refs: neighbour_kernel(*refs, scale=scale), grid=(...  14.5 us
    all_to_all x1, blocking collectives, local(): v_dom = lax.all_to_all(values, KV, 0, 0, tiled=True)  13.4 us
    pallas_call x1, Pallas kernels, local(): pl.pallas_call(lambda *refs: table_kernel(*refs, scale=scale), out_shape=...  4.32 us
    pallas_call x2, Pallas kernels, halo_rows(): pl.pallas_call(lambda *refs: halo_kernel(*refs, far=far), grid=(1,), in_s...  3.47 us
    pallas_call x1, Pallas kernels, local(): pl.pallas_call(weight_kernel, grid=(steps,), in_specs=[whole((1, atoms)),...  3.1 us
  transfers between devices with their start and end apart: 2, of which 1 were waited for; matrix products, arithmetic and copies ran while one was open for 0% of the time, Pallas kernels for 2%

profile of v6, /device:TPU:1, one launch (start us, length us, event | category | flops | bytes accessed | tf_op | source)
XLA Modules:
  0.0 126.5 jit_solution(7219628164845128443)
XLA Ops:
  0.6 0.0 copy-start
  0.6 4.3 %tables.1 = (bf16[256,2048]{1,0:T(8,128)(2,1)S(1)}, bf16[256,2048]{1,0:T(8,128)(2,1)S(1)}, bf16[512,128]{1,0:T(8,128)(2,1)S(1)}, bf16[256,128]{1,0:T(8,128)(2,1)...) custom-call(f32[3,256]{1,0:T(4,128)} %refs_0_.2, ...), custom_call_target="tpu_custom_call" | custom-call | tf_op jit(solution)/shard_map/tables/pallas_call | solution.py:348
  5.0 16.1 %all_to_all.77 = bf16[32,16,128]{2,1,0:T(8,128)(2,1)S(1)} all-to-all(bf16[32,16,128]{2,1,0:T(8,128)(2,1)S(1)} %bitcast.52), channel_id=1, replica_groups=mesh['xlo'=2,'z'=8,'core'=2,'y'=4,'xhi'=2] {'xlo','core','y','xhi'}, dimensions={0} | all-to-all | bytes 262144 | tf_op jit(solution)/shard_map/all_to_all | solution.py:316
  21.1 15.2 %all_to_all.78 = f32[8,16,128]{2,1,0:T(8,128)S(1)} all-to-all(f32[8,16,128]{2,1,0:T(8,128)S(1)} %bitcast.48), channel_id=1, replica_groups=mesh['xlo'=2,'z'=8,'core'=2,'y'=4,'xhi'=2] {'z'}, dimensions={0} | all-to-all | bytes 131072 | tf_op jit(solution)/shard_map/all_to_all | solution.py:318
  36.3 12.8 %all_to_all.79 = bf16[32,16,128]{2,1,0:T(8,128)(2,1)S(1)} all-to-all(bf16[32,16,128]{2,1,0:T(8,128)(2,1)S(1)} %bitcast.45), channel_id=1, replica_groups=mesh['xlo'=2,'z'=8,'core'=2,'y'=4,'xhi'=2] {'xlo','core','y','xhi'}, dimensions={0} | all-to-all | bytes 262144 | tf_op jit(solution)/shard_map/all_to_all | solution.py:320
  49.1 1.4 %project_first.1 = (bf16[256,128]{1,0:T(8,128)(2,1)S(1)}, bf16[2048,128]{1,0:T(8,128)(2,1)S(1)}, f32[3,256]{1,0:T(4,128)S(1)}) custom-call(bf16[512,128]{1,0:T(8,128)(2,1)S(1)} %bitcast.42, bf16[256,2048]{1,0:T(8,128)(2,1)S(1)} %get-tuple-element.24.cos_ref.refs_23_, bf16[256,2048]{1,0:T(8,128)(2,1)S(1)} %get-tuple-element.25.sin_ref.refs_24_, ...), custom_call_target="tpu_custom_call" | custom-call | tf_op jit(solution)/shard_map/project_first/pallas_call | solution.py:363
  50.6 13.4 %all_to_all.80 = bf16[8,256,128]{2,1,0:T(8,128)(2,1)S(1)} all-to-all(bf16[8,256,128]{2,1,0:T(8,128)(2,1)S(1)} %bitcast.43), channel_id=1, replica_groups=mesh['xlo'=2,'z'=8,'core'=2,'y'=4,'xhi'=2] {'y','xhi'}, dimensions={0} | all-to-all | bytes 1048576 | tf_op jit(solution)/shard_map/all_to_all | solution.py:371
  63.9 1.7 %halo_far.1 = bf16[1024,128]{1,0:T(8,128)(2,1)S(1)} custom-call(s32[2,1024]{1,0:T(2,128)} %bitcast.54, s32[2,1024]{1,0:T(2,128)} %bitcast.55, s32[2,1024]{1,0:T(2,128)} %bitcast.56, s32[2,1024]{1,0:T(2,128)} %bitcast.57, s32[2,1024]{1,0:T(2,128)} %bitcast.58, s32[2,1024]{1,0:T(2,128)} %bitcast.59, s32[2,1024]{1,0:T(2,128)} %bitcast.60, s32[2,1024]{1,0:T(2,128)} %bitcast.61, ...), custom_call_target="tpu_custom_call" | custom-call | flops 131072 | bytes 1048576 | tf_op jit(solution)/shard_map/halo_far/pallas_call | solution.py:374
  65.7 1.7 %halo_near.1 = bf16[1024,128]{1,0:T(8,128)(2,1)S(1)} custom-call(s32[2,1024]{1,0:T(2,128)} %bitcast.62, s32[2,1024]{1,0:T(2,128)} %bitcast.63, s32[2,1024]{1,0:T(2,128)} %bitcast.64, s32[2,1024]{1,0:T(2,128)} %bitcast.65, s32[2,1024]{1,0:T(2,128)} %bitcast.66, s32[2,1024]{1,0:T(2,128)} %bitcast.67, s32[2,1024]{1,0:T(2,128)} %bitcast.68, s32[2,1024]{1,0:T(2,128)} %bitcast.69, ...), custom_call_target="tpu_custom_call" | custom-call | flops 131072 | bytes 1048576 | tf_op jit(solution)/shard_map/halo_near/pallas_call | solution.py:374
  67.4 1.9 %collective-permute-start.1 = (bf16[1024,128]{1,0:T(8,128)(2,1)S(1)}, bf16[1024,128]{1,0:T(8,128)(2,1)S(1)}, u32[]{:S(2)}, u32[]{:S(2)}) collective-permute-start(bf16[1024,128]{1,0:T(8,128)(2,1)S(1)} %halo_near.1), channel_id=1, source_target_pairs={{0,8},{8,0},{16,24},{24,16},{32,40},{40,32},{48,56},{56,48},{64,72... | collective-permute-start | bytes 786440 | tf_op jit(solution)/shard_map/ppermute | solution.py:392
  69.3 0.3 collective-permute-start
  69.6 3.1 %slot_weights.1.refs_17_ = f32[256,64,128]{2,1,0:T(8,128)S(1)} custom-call(s32[1,256]{1,0:T(1,128)S(1)} %get-tuple-element.33.count_ref, f32[64,256]{1,0:T(8,128)S(1)} %get-tuple-element.34.dist_ref, f32[16,128]{1,0:T(8,128)S(1)} %get-tuple-element.35.wf_ref), custom_call_target="tpu_custom_call" | custom-call | flops 134217728 | bytes 8388608 | tf_op jit(solution)/shard_map/slot_weights/pallas_call | solution.py:396
  72.7 0.0 copy-done
  72.8 0.0 collective-permute-done.1.refs_20_
  72.8 2.6 %collective-permute-done.refs_19_ = bf16[1024,128]{1,0:T(8,128)(2,1)S(1)} collective-permute-done((bf16[1024,128]{1,0:T(8,128)(2,1)S(1)}, bf16[1024,128]{1,0:T(8,128)(2,1)S(1)}, u32[]{:S(2)}, u32[]{:S(2)}) %collective-permute-start) | collective-permute-done | bytes 262176 | tf_op jit(solution)/shard_map/ppermute | solution.py:390
  75.4 14.5 %neighbours.1 = (bf16[256,128]{1,0:T(8,128)(2,1)S(1)}, bf16[512,128]{1,0:T(8,128)(2,1)S(1)}) custom-call(s32[256]{0:T(256)} %refs_0_.3, s32[16384]{0:T(1024)S(1)} %bitcast.22, s32[16384]{0:T(1024)S(1)} %bitcast.23, s32[16384]{0:T(1024)S(1)} %bitcast.24, s32[16384]{0:T(1024)S(1)} %bitcast.25, s32[16384]{0:T(1024)S(1)} %bitcast.26, s32[16384]{0:T(1024)S(1)} %bitcast.27, ...), custom_call_target="tpu_custom_call" | custom-call | tf_op jit(solution)/shard_map/neighbours/pallas_call | solution.py:423
  90.0 12.3 %all_to_all.81 = bf16[32,16,128]{2,1,0:T(8,128)(2,1)S(1)} all-to-all(bf16[32,16,128]{2,1,0:T(8,128)(2,1)S(1)} %bitcast.53), channel_id=1, replica_groups=mesh['xlo'=2,'z'=8,'core'=2,'y'=4,'xhi'=2] {'xlo','core','y','xhi'}, dimensions={0} | all-to-all | bytes 262144 | tf_op jit(solution)/shard_map/all_to_all | solution.py:316
  102.4 9.5 %all_to_all.82 = f32[8,16,128]{2,1,0:T(8,128)S(1)} all-to-all(f32[8,16,128]{2,1,0:T(8,128)S(1)} %bitcast.50), channel_id=1, replica_groups=mesh['xlo'=2,'z'=8,'core'=2,'y'=4,'xhi'=2] {'z'}, dimensions={0} | all-to-all | bytes 131072 | tf_op jit(solution)/shard_map/all_to_all | solution.py:318
  111.9 12.7 %all_to_all.83 = bf16[32,16,128]{2,1,0:T(8,128)(2,1)S(1)} all-to-all(bf16[32,16,128]{2,1,0:T(8,128)(2,1)S(1)} %bitcast.47), channel_id=1, replica_groups=mesh['xlo'=2,'z'=8,'core'=2,'y'=4,'xhi'=2] {'xlo','core','y','xhi'}, dimensions={0} | all-to-all | bytes 262144 | tf_op jit(solution)/shard_map/all_to_all | solution.py:320
  124.6 1.9 %project_second.1 = (bf16[256,128]{1,0:T(8,128)(2,1)}, f32[3,256]{1,0:T(4,128)}) custom-call(bf16[512,128]{1,0:T(8,128)(2,1)S(1)} %bitcast.41, bf16[256,2048]{1,0:T(8,128)(2,1)S(1)} %get-tuple-element.24.cos_ref.refs_23_, bf16[256,2048]{1,0:T(8,128)(2,1)S(1)} %get-tuple-element.25.sin_ref.refs_24_, f32[3,2048]{1,0:T(4,128)S(1)} %get-tuple-element.26.wave_ref.refs_25_, ...), custom_call_target="tpu_custom_call" | custom-call | tf_op jit(solution)/shard_map/project_second/pallas_call | solution.py:449
  (5 shorter events, 0.1 us)
Async XLA Ops:
  0.6 72.1 %copy-start = (s32[256,64]{0,1:T(8,128)S(1)}, s32[256,64]{0,1:T(8,128)}, u32[]{:S(2)}) copy-start(s32[256,64]{0,1:T(8,128)} %param.15) | copy-start | bytes 196612
  67.4 5.4 %collective-permute-start.1 = (bf16[1024,128]{1,0:T(8,128)(2,1)S(1)}, bf16[1024,128]{1,0:T(8,128)(2,1)S(1)}, u32[]{:S(2)}, u32[]{:S(2)}) collective-permute-start(bf16[1024,128]{1,0:T(8,128)(2,1)S(1)} %halo_near.1), channel_id=1, source_target_pairs={{0,8},{8,0},{16,24},{24,16},{32,40},{40,32},{48,56},{56,48},{64,72... | collective-permute-start | bytes 786440 | tf_op jit(solution)/shard_map/ppermute | solution.py:392
  69.3 6.1 %collective-permute-start = (bf16[1024,128]{1,0:T(8,128)(2,1)S(1)}, bf16[1024,128]{1,0:T(8,128)(2,1)S(1)}, u32[]{:S(2)}, u32[]{:S(2)}) collective-permute-start(bf16[1024,128]{1,0:T(8,128)(2,1)S(1)} %halo_far.1), channel_id=1, source_target_pairs={{0,248},{8,16},{16,8},{24,32},{32,24},{40,48},{48,40},{56,64},{64,... | collective-permute-start | bytes 786440 | tf_op jit(solution)/shard_map/ppermute | solution.py:390

commit v7 on v6

--- a/solution.py
+++ b/solution.py
@@ -16,6 +16,7 @@
 EVERY = tuple(name for name, _ in PARTS)
 DOM = ("xlo", "z", "core")
 KV = ("y", "xhi")
+UNROLL = 2
 LINE = ("z",)
 PLANE = ("xlo", "core", "y", "xhi")
 
@@ -151,13 +152,14 @@
 
 
 def first_project_kernel(
-    sums_ref, cos_ref, sin_ref, wave_ref, feat_ref, wc_ref, wl_ref, wv_ref,
-    hidden_ref, values_ref, force_ref, with_cos, with_sin,
+    sums_ref, cos_ref, sin_ref, feat_ref, wl_ref, wv_ref, hidden_ref, values_ref, with_cos, with_sin,
 ):
-    charge_t = dot(wc_ref[...], feat_ref[...], NT)
-    potential_t, force = project(sums_ref, cos_ref, sin_ref, wave_ref, charge_t, with_cos, with_sin)
-    for c in range(3):
-        force_ref[c : c + 1, :] = force[c]
+    chan, waves = with_cos.shape
+    for t in range(waves // 128):
+        lanes = slice(t * 128, (t + 1) * 128)
+        with_cos[:, lanes] = sums_ref[t * 2 * chan : t * 2 * chan + chan, :]
+        with_sin[:, lanes] = sums_ref[t * 2 * chan + chan : (t + 1) * 2 * chan, :]
+    potential_t = dot(with_cos[...], cos_ref[...], NT) + dot(with_sin[...], sin_ref[...], NT)
     lifted = dot(potential_t, wl_ref[...], TN, HIGHEST)
     hidden = (feat_ref[...].astype(F32) + silu(lifted)).astype(BF16)
     hidden_ref[...] = hidden
@@ -165,6 +167,13 @@
     atoms = values.shape[0]
     for j in range(values_ref.shape[0] // atoms):
         values_ref[j * atoms : (j + 1) * atoms, :] = values
+
+
+def first_force_kernel(sums_ref, cos_ref, sin_ref, wave_ref, feat_ref, wc_ref, force_ref, with_cos, with_sin):
+    charge_t = dot(wc_ref[...], feat_ref[...], NT)
+    _, force = project(sums_ref, cos_ref, sin_ref, wave_ref, charge_t, with_cos, with_sin)
+    for c in range(3):
+        force_ref[c : c + 1, :] = force[c]
 
 
 def last_project_kernel(
@@ -259,7 +268,12 @@
     table[pl.ds(pl.multiple_of(own + core * halo, 8), halo), :] = far_ref[...].astype(F32)
     bits = sublane_bits()
 
-    def one_atom(atom, carry):
+    def some_atoms(group, carry):
+        for k in range(UNROLL):
+            one_atom(group * UNROLL + k)
+        return carry
+
+    def one_atom(atom):
         at = pl.ds(pl.multiple_of(atom * 8, 8), 8)
         spots = [atom + q * atoms for q in range(4)]
 
@@ -277,9 +291,7 @@
         def _():
             sums[at, :] = sums[at, :] + some_slots(range(middle, slots // 8))
 
-        return carry
-
-    lax.fori_loop(0, atoms, one_atom, 0)
+    lax.fori_loop(0, atoms // UNROLL, some_atoms, 0)
     message = sums[pl.ds(0, atoms, stride=8), :]
     for k in range(1, 8):
         message = message + sums[pl.ds(k, atoms, stride=8), :]
@@ -343,7 +355,7 @@
 
     kept = (
         features, w_charge_first, wave_vectors, w_long_first, w_value, w_charge_second, w_long_second,
-        dist_t, nbr_count.reshape(1, atoms), w_filter,
+        dist_t, nbr_count.reshape(1, atoms), w_filter, lists,
     )
     cos_table, sin_table, part, *kept = pl.pallas_call(
         lambda *refs: table_kernel(*refs, scale=scale),
@@ -357,16 +369,16 @@
     )(*in_hbm(positions, *kept))
     (
         features, w_charge_first, wave_vectors, w_long_first, w_value, w_charge_second, w_long_second,
-        dist_t, count_row, w_filter,
+        dist_t, count_row, w_filter, lists,
     ) = kept
     sums = everything(part)
-    hidden_first, values, force_first = pl.pallas_call(
+    hidden_first, values = pl.pallas_call(
         first_project_kernel,
-        out_shape=(shape((atoms, hid), BF16), shape((kv * atoms, hid), BF16), shape((3, atoms), F32)),
-        scratch_shapes=[pltpu.VMEM((4 * chan, waves), BF16)] * 2,
+        out_shape=(shape((atoms, hid), BF16), shape((kv * atoms, hid), BF16)),
+        scratch_shapes=[pltpu.VMEM((chan, waves), BF16)] * 2,
         compiler_params=vmem(6),
         name="project_first",
-    )(sums, cos_table, sin_table, wave_vectors, features, w_charge_first, w_long_first, w_value)
+    )(sums, cos_table, sin_table, features, w_long_first, w_value)
 
     v_dom = lax.all_to_all(values, KV, 0, 0, tiled=True)
 
@@ -383,12 +395,19 @@
             compiler_params=vmem(6),
             cost_estimate=pl.CostEstimate(flops=halo * hid, bytes_accessed=4 * kv * atoms * hid, transcendentals=0),
             name="halo_far" if far else "halo_near",
-        )(*in_hbm(*[lists] * (halo // 128)), source)
+        )(*[lists] * (halo // 128), source)
 
     to_far = halo_rows(True, v_dom)
-    to_far, source, index_t = lax.optimization_barrier((to_far, v_dom, index_t))
+    to_far, source, index_t, sums = lax.optimization_barrier((to_far, v_dom, index_t, sums))
     from_far = lax.ppermute(to_far, DOM, [(i, (i - 1 + 2 * (i % 2)) % doms) for i in range(doms)])
     to_near = halo_rows(False, source)
+    force_first = pl.pallas_call(
+        first_force_kernel,
+        out_shape=shape((3, atoms), F32),
+        scratch_shapes=[pltpu.VMEM((4 * chan, waves), BF16)] * 2,
+        compiler_params=vmem(6),
+        name="force_first",
+    )(sums, cos_table, sin_table, wave_vectors, features, w_charge_first)
     from_near = lax.ppermute(to_near, DOM, [(i, i + 1 - 2 * (i % 2)) for i in range(doms)])
 
     steps = 8

time: 127 us -> 127 us (level)
  blocking collectives: 92 us -> 79.3 us
  waiting for transfers between devices: 2.65 us -> 9.52 us
  starting transfers between devices: 2.18 us -> 7.39 us
    all_to_all x2 -> x1, blocking collectives: 25.5 us -> 12.8 us  [everything(): return lax.all_to_all(share, PLANE, 0, 0, tiled=True)]
    all_to_all x0 -> x1, waiting for transfers between devices: none -> 6.87 us  [everything(): return lax.all_to_all(share, PLANE, 0, 0, tiled=True)]
    all_to_all x0 -> x1, starting transfers between devices: none -> 5.21 us  [everything(): return lax.all_to_all(share, PLANE, 0, 0, tiled=True)]
  transfers between devices with their start and end apart: 2 -> 3, of which waited for: 1 -> 2; matrix products, arithmetic and copies ran while one was open for 0% -> 0% of each run, Pallas kernels for 2% -> 3%
where the time goes in v7:
time: 127 us; the launch traced here: 126 us
  blocking collectives  79.3 us (62%)
  Pallas kernels  29.1 us (23%)
  waiting for transfers between devices  9.52 us (7%)
  starting transfers between devices  7.39 us (6%)
    all_to_all x2, blocking collectives, everything(): share = lax.all_to_all(part, PLANE, 0, 0, tiled=True)  28.4 us
    all_to_all x2, blocking collectives, everything(): share = lax.all_to_all(share, LINE, 0, 0, tiled=True)  24.7 us
    pallas_call x1, Pallas kernels, local(): pl.pallas_call(lambda *refs: neighbour_kernel(*refs, scale=scale), grid=(...  13.6 us
    all_to_all x1, blocking collectives, local(): v_dom = lax.all_to_all(values, KV, 0, 0, tiled=True)  13.4 us
    all_to_all x1, blocking collectives, everything(): return lax.all_to_all(share, PLANE, 0, 0, tiled=True)  12.8 us
    all_to_all x1, waiting for transfers between devices, everything(): return lax.all_to_all(share, PLANE, 0, 0, tiled=True)  6.87 us
    all_to_all x1, starting transfers between devices, everything(): return lax.all_to_all(share, PLANE, 0, 0, tiled=True)  5.21 us
    pallas_call x1, Pallas kernels, local(): pl.pallas_call(lambda *refs: table_kernel(*refs, scale=scale), out_shape=...  4.32 us
  transfers between devices with their start and end apart: 3, of which 2 were waited for; matrix products, arithmetic and copies ran while one was open for 0% of the time, Pallas kernels for 3%

profile of v7, /device:TPU:1, one launch (start us, length us, event | category | flops | bytes accessed | tf_op | source)
XLA Modules:
  0.0 126.1 jit_solution(1139823115886309185)
XLA Ops:
  0.6 0.0 copy-start
  0.6 4.3 %tables.1 = (bf16[256,2048]{1,0:T(8,128)(2,1)S(1)}, bf16[256,2048]{1,0:T(8,128)(2,1)S(1)}, bf16[512,128]{1,0:T(8,128)(2,1)S(1)}, bf16[256,128]{1,0:T(8,128)(2,1)...) custom-call(f32[3,256]{1,0:T(4,128)} %refs_0_.2, ...), custom_call_target="tpu_custom_call" | custom-call | tf_op jit(solution)/shard_map/tables/pallas_call | solution.py:360
  5.0 16.0 %all_to_all.77 = bf16[32,16,128]{2,1,0:T(8,128)(2,1)S(1)} all-to-all(bf16[32,16,128]{2,1,0:T(8,128)(2,1)S(1)} %bitcast.52), channel_id=1, replica_groups=mesh['xlo'=2,'z'=8,'core'=2,'y'=4,'xhi'=2] {'xlo','core','y','xhi'}, dimensions={0} | all-to-all | bytes 262144 | tf_op jit(solution)/shard_map/all_to_all | solution.py:328
  21.1 15.2 %all_to_all.78 = f32[8,16,128]{2,1,0:T(8,128)S(1)} all-to-all(f32[8,16,128]{2,1,0:T(8,128)S(1)} %bitcast.48), channel_id=1, replica_groups=mesh['xlo'=2,'z'=8,'core'=2,'y'=4,'xhi'=2] {'z'}, dimensions={0} | all-to-all | bytes 131072 | tf_op jit(solution)/shard_map/all_to_all | solution.py:330
  36.3 12.8 %all_to_all.79 = bf16[32,16,128]{2,1,0:T(8,128)(2,1)S(1)} all-to-all(bf16[32,16,128]{2,1,0:T(8,128)(2,1)S(1)} %bitcast.46), channel_id=1, replica_groups=mesh['xlo'=2,'z'=8,'core'=2,'y'=4,'xhi'=2] {'xlo','core','y','xhi'}, dimensions={0} | all-to-all | bytes 262144 | tf_op jit(solution)/shard_map/all_to_all | solution.py:332
  49.1 1.3 %project_first.1 = (bf16[256,128]{1,0:T(8,128)(2,1)S(1)}, bf16[2048,128]{1,0:T(8,128)(2,1)S(1)}) custom-call(bf16[512,128]{1,0:T(8,128)(2,1)S(1)} %bitcast.41, bf16[256,2048]{1,0:T(8,128)(2,1)S(1)} %get-tuple-element.26.cos_ref.refs_23_, bf16[256,2048]{1,0:T(8,128)(2,1)S(1)} %get-tuple-element.27.sin_ref.refs_24_, ...), custom_call_target="tpu_custom_call" | custom-call | tf_op jit(solution)/shard_map/project_first/pallas_call | solution.py:375
  50.5 13.4 %all_to_all.80 = bf16[8,256,128]{2,1,0:T(8,128)(2,1)S(1)} all-to-all(bf16[8,256,128]{2,1,0:T(8,128)(2,1)S(1)} %bitcast.44), channel_id=1, replica_groups=mesh['xlo'=2,'z'=8,'core'=2,'y'=4,'xhi'=2] {'y','xhi'}, dimensions={0} | all-to-all | bytes 1048576 | tf_op jit(solution)/shard_map/all_to_all | solution.py:383
  63.9 1.6 %halo_far.1 = bf16[1024,128]{1,0:T(8,128)(2,1)S(1)} custom-call(s32[2,1024]{1,0:T(2,128)S(1)} %get-tuple-element.24.refs_0_.refs_1_.refs_2_.refs_3_.refs_4_.refs_5_.refs_6_.refs_7_, s32[2,1024]{1,0:T(2,128)S(1)} %get-tuple-element.24.refs_0_.refs_1_.refs_2_.refs_3_.refs_4_.refs_5_.refs_6_.refs_7_, ...), custom_call_target="tpu_custom_call" | custom-call | flops 131072 | bytes 1048576 | tf_op jit(solution)/shard_map/halo_far/pallas_call | solution.py:386
  65.5 1.6 %halo_near.1 = bf16[1024,128]{1,0:T(8,128)(2,1)S(1)} custom-call(s32[2,1024]{1,0:T(2,128)S(1)} %get-tuple-element.24.refs_0_.refs_1_.refs_2_.refs_3_.refs_4_.refs_5_.refs_6_.refs_7_, s32[2,1024]{1,0:T(2,128)S(1)} %get-tuple-element.24.refs_0_.refs_1_.refs_2_.refs_3_.refs_4_.refs_5_.refs_6_.refs_7_, ...), custom_call_target="tpu_custom_call" | custom-call | flops 131072 | bytes 1048576 | tf_op jit(solution)/shard_map/halo_near/pallas_call | solution.py:386
  67.1 1.9 %collective-permute-start.1 = (bf16[1024,128]{1,0:T(8,128)(2,1)S(1)}, bf16[1024,128]{1,0:T(8,128)(2,1)S(1)}, u32[]{:S(2)}, u32[]{:S(2)}) collective-permute-start(bf16[1024,128]{1,0:T(8,128)(2,1)S(1)} %halo_near.1), channel_id=1, source_target_pairs={{0,8},{8,0},{16,24},{24,16},{32,40},{40,32},{48,56},{56,48},{64,72... | collective-permute-start | bytes 786440 | tf_op jit(solution)/shard_map/ppermute | solution.py:411
  69.0 0.3 collective-permute-start
  69.2 3.1 %slot_weights.1.refs_17_ = f32[256,64,128]{2,1,0:T(8,128)S(1)} custom-call(s32[1,256]{1,0:T(1,128)S(1)} %get-tuple-element.33.count_ref, f32[64,256]{1,0:T(8,128)S(1)} %get-tuple-element.34.dist_ref, f32[16,128]{1,0:T(8,128)S(1)} %get-tuple-element.35.wf_ref), custom_call_target="tpu_custom_call" | custom-call | flops 134217728 | bytes 8388608 | tf_op jit(solution)/shard_map/slot_weights/pallas_call | solution.py:415
  72.3 0.0 copy-done
  72.4 0.0 collective-permute-done.1.refs_20_
  72.4 2.7 %collective-permute-done.refs_19_ = bf16[1024,128]{1,0:T(8,128)(2,1)S(1)} collective-permute-done((bf16[1024,128]{1,0:T(8,128)(2,1)S(1)}, bf16[1024,128]{1,0:T(8,128)(2,1)S(1)}, u32[]{:S(2)}, u32[]{:S(2)}) %collective-permute-start) | collective-permute-done | bytes 262176 | tf_op jit(solution)/shard_map/ppermute | solution.py:402
  75.1 13.6 %neighbours.1 = (bf16[256,128]{1,0:T(8,128)(2,1)S(1)}, bf16[512,128]{1,0:T(8,128)(2,1)S(1)}) custom-call(s32[256]{0:T(256)} %refs_0_.3, s32[16384]{0:T(1024)S(1)} %bitcast.22, s32[16384]{0:T(1024)S(1)} %bitcast.23, s32[16384]{0:T(1024)S(1)} %bitcast.24, s32[16384]{0:T(1024)S(1)} %bitcast.25, s32[16384]{0:T(1024)S(1)} %bitcast.26, s32[16384]{0:T(1024)S(1)} %bitcast.27, ...), custom_call_target="tpu_custom_call" | custom-call | tf_op jit(solution)/shard_map/neighbours/pallas_call | solution.py:442
  88.7 12.3 %all_to_all.81 = bf16[32,16,128]{2,1,0:T(8,128)(2,1)S(1)} all-to-all(bf16[32,16,128]{2,1,0:T(8,128)(2,1)S(1)} %bitcast.53), channel_id=1, replica_groups=mesh['xlo'=2,'z'=8,'core'=2,'y'=4,'xhi'=2] {'xlo','core','y','xhi'}, dimensions={0} | all-to-all | bytes 262144 | tf_op jit(solution)/shard_map/all_to_all | solution.py:328
  101.1 9.5 %all_to_all.82 = f32[8,16,128]{2,1,0:T(8,128)S(1)} all-to-all(f32[8,16,128]{2,1,0:T(8,128)S(1)} %bitcast.50), channel_id=1, replica_groups=mesh['xlo'=2,'z'=8,'core'=2,'y'=4,'xhi'=2] {'z'}, dimensions={0} | all-to-all | bytes 131072 | tf_op jit(solution)/shard_map/all_to_all | solution.py:330
  110.6 0.7 shard_map.143
  111.3 5.2 %all-to-all-start.6 = ((bf16[32,16,128]{2,1,0:T(8,128)(2,1)}), bf16[32,16,128]{2,1,0:T(8,128)(2,1)S(1)}, u32[]{:S(2)}, u32[]{:S(2)}) async-start(bf16[32,16,128]{2,1,0:T(8,128)(2,1)} %bitcast.18), calls=%async_computation.6 | async-start | bytes 262144 | tf_op jit(solution)/shard_map/all_to_all | solution.py:332
  116.5 0.8 force_first.1.force_in
  117.3 6.9 %all-to-all-done.6 = bf16[32,16,128]{2,1,0:T(8,128)(2,1)S(1)} async-done(((bf16[32,16,128]{2,1,0:T(8,128)(2,1)}), bf16[32,16,128]{2,1,0:T(8,128)(2,1)S(1)}, u32[]{:S(2)}, u32[]{:S(2)}) %all-to-all-start.6) | async-done | bytes 131104 | tf_op jit(solution)/shard_map/all_to_all | solution.py:332
  124.2 1.9 %project_second.1 = (bf16[256,128]{1,0:T(8,128)(2,1)}, f32[3,256]{1,0:T(4,128)}) custom-call(bf16[512,128]{1,0:T(8,128)(2,1)S(1)} %bitcast.43, bf16[256,2048]{1,0:T(8,128)(2,1)S(1)} %get-tuple-element.26.cos_ref.refs_23_, bf16[256,2048]{1,0:T(8,128)(2,1)S(1)} %get-tuple-element.27.sin_ref.refs_24_, f32[3,2048]{1,0:T(4,128)S(1)} %get-tuple-element.40.refs_25_.wave_ref, ...), custom_call_target="tpu_custom_call" | custom-call | tf_op jit(solution)/shard_map/project_second/pallas_call | solution.py:468
  (4 shorter events, 0.1 us)
Async XLA Ops:
  0.6 71.7 %copy-start = (s32[256,64]{0,1:T(8,128)S(1)}, s32[256,64]{0,1:T(8,128)}, u32[]{:S(2)}) copy-start(s32[256,64]{0,1:T(8,128)} %param.15) | copy-start | bytes 196612
  67.1 5.3 %collective-permute-start.1 = (bf16[1024,128]{1,0:T(8,128)(2,1)S(1)}, bf16[1024,128]{1,0:T(8,128)(2,1)S(1)}, u32[]{:S(2)}, u32[]{:S(2)}) collective-permute-start(bf16[1024,128]{1,0:T(8,128)(2,1)S(1)} %halo_near.1), channel_id=1, source_target_pairs={{0,8},{8,0},{16,24},{24,16},{32,40},{40,32},{48,56},{56,48},{64,72... | collective-permute-start | bytes 786440 | tf_op jit(solution)/shard_map/ppermute | solution.py:411
  69.0 6.1 %collective-permute-start = (bf16[1024,128]{1,0:T(8,128)(2,1)S(1)}, bf16[1024,128]{1,0:T(8,128)(2,1)S(1)}, u32[]{:S(2)}, u32[]{:S(2)}) collective-permute-start(bf16[1024,128]{1,0:T(8,128)(2,1)S(1)} %halo_far.1), channel_id=1, source_target_pairs={{0,248},{8,16},{16,8},{24,32},{32,24},{40,48},{48,40},{56,64},{64,... | collective-permute-start | bytes 786440 | tf_op jit(solution)/shard_map/ppermute | solution.py:402
  111.3 12.9 %all-to-all-start.6 = ((bf16[32,16,128]{2,1,0:T(8,128)(2,1)}), bf16[32,16,128]{2,1,0:T(8,128)(2,1)S(1)}, u32[]{:S(2)}, u32[]{:S(2)}) async-start(bf16[32,16,128]{2,1,0:T(8,128)(2,1)} %bitcast.18), calls=%async_computation.6 | async-start | bytes 262144 | tf_op jit(solution)/shard_map/all_to_all | solution.py:332

commit v8 on v7

--- a/solution.py
+++ b/solution.py
@@ -83,37 +83,48 @@
 
 
 def table_kernel(*refs, scale):
-    later = (len(refs) - 6) // 2
+    later = (len(refs) - 8) // 2
     pos_ref, kept_in, cos_ref, sin_ref, part_ref = refs[0], refs[1 : 1 + later], *refs[1 + later : 4 + later]
-    kept_out, turns, pad = refs[4 + later : -2], *refs[-2:]
+    kept_out, pieces, whole, turns_even, turns_odd = refs[4 + later : -4], *refs[-4:]
     feat_ref, wc_ref, wave_ref = kept_in[:3]
     atoms, waves = cos_ref.shape
     for in_ref, out_ref in zip(kept_in, kept_out):
         out_ref[...] = in_ref[...]
-    pad[...] = jnp.zeros_like(pad)
-    pad[0:3, :] = pos_ref[...] * (1.0 / CELL)
-    columns = jnp.transpose(pad[...])
-    for c in range(3):
-        turns[c] = jnp.broadcast_to(columns[:, c : c + 1], (atoms, 128))
+    rest = pos_ref[...] * (1.0 / CELL)
+    pieces[...] = jnp.zeros_like(pieces)
+    whole[...] = jnp.zeros_like(whole)
+    for p in range(3):
+        piece = rest.astype(BF16).astype(F32)
+        pieces[3 * p : 3 * p + 3, :] = piece
+        whole[3 * p : 3 * p + 3, :] = jnp.round(wave_ref[...] * (CELL / (2.0 * math.pi)))
+        rest = rest - piece
+    columns = jnp.transpose(pieces[...]).astype(BF16)
+    tiles = waves // 128
     rows = 64
 
-    def one_tile(t, carry):
+    def fill(t, turns):
         lanes = pl.ds(pl.multiple_of(t * 128, 128), 128)
-        whole = jnp.round(wave_ref[:, lanes] * (CELL / (2.0 * math.pi)))
+        turns[...] = dot(columns, whole[:, lanes].astype(BF16))
+
+    def finish(t, turns):
+        lanes = pl.ds(pl.multiple_of(t * 128, 128), 128)
         for b in range(atoms // rows):
             at = slice(b * rows, (b + 1) * rows)
-            u = (
-                turns[0, at, :] * whole[0:1]
-                + turns[1, at, :] * whole[1:2]
-                + turns[2, at, :] * whole[2:3]
-            )
+            u = turns[at, :]
             u = u - jnp.round(u)
             v = u * u
             cos_ref[at, lanes] = horner(COS_COEF, v).astype(BF16)
             sin_ref[at, lanes] = (u * horner(SIN_COEF, v)).astype(BF16)
+
+    def two_tiles(t, carry):
+        fill(2 * t + 1, turns_odd)
+        finish(2 * t, turns_even)
+        fill(lax.rem(2 * t + 2, tiles), turns_even)
+        finish(2 * t + 1, turns_odd)
         return carry
 
-    lax.fori_loop(0, waves // 128, one_tile, 0)
+    fill(0, turns_even)
+    lax.fori_loop(0, tiles // 2, two_tiles, 0)
     charge_t = dot(wc_ref[...], feat_ref[...], NT)
     structure_part(charge_t, cos_ref, sin_ref, wave_ref, part_ref, scale)
 
@@ -363,7 +374,7 @@
             shape((atoms, waves), BF16), shape((atoms, waves), BF16), shape((part_rows, 128), BF16),
             *(shape(a.shape, a.dtype) for a in kept),
         ),
-        scratch_shapes=[pltpu.VMEM((3, atoms, 128), F32), pltpu.VMEM((8, atoms), F32)],
+        scratch_shapes=[pltpu.VMEM((16, atoms), F32), pltpu.VMEM((16, waves), F32)] + [pltpu.VMEM((atoms, 128), F32)] * 2,
         compiler_params=vmem(6),
         name="tables",
     )(*in_hbm(positions, *kept))

time: 127 us -> 127 us (level)
  no operation moved by 1% of the time
where the time goes in v8:
time: 127 us
  blocking collectives  79.3 us (62%)
  Pallas kernels  29.5 us (23%)
  waiting for transfers between devices  9.52 us (7%)
  starting transfers between devices  7.39 us (6%)
    all_to_all x2, blocking collectives, everything(): share = lax.all_to_all(part, PLANE, 0, 0, tiled=True)  28.4 us
    all_to_all x2, blocking collectives, everything(): share = lax.all_to_all(share, LINE, 0, 0, tiled=True)  24.7 us
    pallas_call x1, Pallas kernels, local(): pl.pallas_call(lambda *refs: neighbour_kernel(*refs, scale=scale), grid=(...  13.6 us
    all_to_all x1, blocking collectives, local(): v_dom = lax.all_to_all(values, KV, 0, 0, tiled=True)  13.4 us
    all_to_all x1, blocking collectives, everything(): return lax.all_to_all(share, PLANE, 0, 0, tiled=True)  12.8 us
    all_to_all x1, waiting for transfers between devices, everything(): return lax.all_to_all(share, PLANE, 0, 0, tiled=True)  6.87 us
    all_to_all x1, starting transfers between devices, everything(): return lax.all_to_all(share, PLANE, 0, 0, tiled=True)  5.21 us
    pallas_call x1, Pallas kernels, local(): pl.pallas_call(lambda *refs: table_kernel(*refs, scale=scale), out_shape=...  4.74 us
  transfers between devices with their start and end apart: 3, of which 2 were waited for; matrix products, arithmetic and copies ran while one was open for 0% of the time, Pallas kernels for 3%

profile of v8, /device:TPU:1, one launch (start us, length us, event | category | flops | bytes accessed | tf_op | source)
XLA Modules:
  0.0 126.5 jit_solution(3208406935357725246)
XLA Ops:
  0.6 0.0 copy-start
  0.6 4.7 %tables.1 = (bf16[256,2048]{1,0:T(8,128)(2,1)S(1)}, bf16[256,2048]{1,0:T(8,128)(2,1)S(1)}, bf16[512,128]{1,0:T(8,128)(2,1)S(1)}, bf16[256,128]{1,0:T(8,128)(2,1)...) custom-call(f32[3,256]{1,0:T(4,128)} %refs_0_.2, ...), custom_call_target="tpu_custom_call" | custom-call | tf_op jit(solution)/shard_map/tables/pallas_call | solution.py:371
  5.4 16.0 %all_to_all.77 = bf16[32,16,128]{2,1,0:T(8,128)(2,1)S(1)} all-to-all(bf16[32,16,128]{2,1,0:T(8,128)(2,1)S(1)} %bitcast.52), channel_id=1, replica_groups=mesh['xlo'=2,'z'=8,'core'=2,'y'=4,'xhi'=2] {'xlo','core','y','xhi'}, dimensions={0} | all-to-all | bytes 262144 | tf_op jit(solution)/shard_map/all_to_all | solution.py:339
  21.5 15.2 %all_to_all.78 = f32[8,16,128]{2,1,0:T(8,128)S(1)} all-to-all(f32[8,16,128]{2,1,0:T(8,128)S(1)} %bitcast.48), channel_id=1, replica_groups=mesh['xlo'=2,'z'=8,'core'=2,'y'=4,'xhi'=2] {'z'}, dimensions={0} | all-to-all | bytes 131072 | tf_op jit(solution)/shard_map/all_to_all | solution.py:341
  36.7 12.8 %all_to_all.79 = bf16[32,16,128]{2,1,0:T(8,128)(2,1)S(1)} all-to-all(bf16[32,16,128]{2,1,0:T(8,128)(2,1)S(1)} %bitcast.46), channel_id=1, replica_groups=mesh['xlo'=2,'z'=8,'core'=2,'y'=4,'xhi'=2] {'xlo','core','y','xhi'}, dimensions={0} | all-to-all | bytes 262144 | tf_op jit(solution)/shard_map/all_to_all | solution.py:343
  49.6 1.3 %project_first.1 = (bf16[256,128]{1,0:T(8,128)(2,1)S(1)}, bf16[2048,128]{1,0:T(8,128)(2,1)S(1)}) custom-call(bf16[512,128]{1,0:T(8,128)(2,1)S(1)} %bitcast.41, bf16[256,2048]{1,0:T(8,128)(2,1)S(1)} %get-tuple-element.26.cos_ref.refs_23_, bf16[256,2048]{1,0:T(8,128)(2,1)S(1)} %get-tuple-element.27.sin_ref.refs_24_, ...), custom_call_target="tpu_custom_call" | custom-call | tf_op jit(solution)/shard_map/project_first/pallas_call | solution.py:386
  50.9 13.4 %all_to_all.80 = bf16[8,256,128]{2,1,0:T(8,128)(2,1)S(1)} all-to-all(bf16[8,256,128]{2,1,0:T(8,128)(2,1)S(1)} %bitcast.44), channel_id=1, replica_groups=mesh['xlo'=2,'z'=8,'core'=2,'y'=4,'xhi'=2] {'y','xhi'}, dimensions={0} | all-to-all | bytes 1048576 | tf_op jit(solution)/shard_map/all_to_all | solution.py:394
  64.3 1.6 %halo_far.1 = bf16[1024,128]{1,0:T(8,128)(2,1)S(1)} custom-call(s32[2,1024]{1,0:T(2,128)S(1)} %get-tuple-element.24.refs_0_.refs_1_.refs_2_.refs_3_.refs_4_.refs_5_.refs_6_.refs_7_, s32[2,1024]{1,0:T(2,128)S(1)} %get-tuple-element.24.refs_0_.refs_1_.refs_2_.refs_3_.refs_4_.refs_5_.refs_6_.refs_7_, ...), custom_call_target="tpu_custom_call" | custom-call | flops 131072 | bytes 1048576 | tf_op jit(solution)/shard_map/halo_far/pallas_call | solution.py:397
  65.9 1.6 %halo_near.1 = bf16[1024,128]{1,0:T(8,128)(2,1)S(1)} custom-call(s32[2,1024]{1,0:T(2,128)S(1)} %get-tuple-element.24.refs_0_.refs_1_.refs_2_.refs_3_.refs_4_.refs_5_.refs_6_.refs_7_, s32[2,1024]{1,0:T(2,128)S(1)} %get-tuple-element.24.refs_0_.refs_1_.refs_2_.refs_3_.refs_4_.refs_5_.refs_6_.refs_7_, ...), custom_call_target="tpu_custom_call" | custom-call | flops 131072 | bytes 1048576 | tf_op jit(solution)/shard_map/halo_near/pallas_call | solution.py:397
  67.5 1.9 %collective-permute-start.1 = (bf16[1024,128]{1,0:T(8,128)(2,1)S(1)}, bf16[1024,128]{1,0:T(8,128)(2,1)S(1)}, u32[]{:S(2)}, u32[]{:S(2)}) collective-permute-start(bf16[1024,128]{1,0:T(8,128)(2,1)S(1)} %halo_near.1), channel_id=1, source_target_pairs={{0,8},{8,0},{16,24},{24,16},{32,40},{40,32},{48,56},{56,48},{64,72... | collective-permute-start | bytes 786440 | tf_op jit(solution)/shard_map/ppermute | solution.py:422
  69.4 0.3 collective-permute-start
  69.7 3.1 %slot_weights.1.refs_17_ = f32[256,64,128]{2,1,0:T(8,128)S(1)} custom-call(s32[1,256]{1,0:T(1,128)S(1)} %get-tuple-element.33.count_ref, f32[64,256]{1,0:T(8,128)S(1)} %get-tuple-element.34.dist_ref, f32[16,128]{1,0:T(8,128)S(1)} %get-tuple-element.35.wf_ref), custom_call_target="tpu_custom_call" | custom-call | flops 134217728 | bytes 8388608 | tf_op jit(solution)/shard_map/slot_weights/pallas_call | solution.py:426
  72.8 0.0 copy-done
  72.8 0.0 collective-permute-done.1.refs_20_
  72.8 2.6 %collective-permute-done.refs_19_ = bf16[1024,128]{1,0:T(8,128)(2,1)S(1)} collective-permute-done((bf16[1024,128]{1,0:T(8,128)(2,1)S(1)}, bf16[1024,128]{1,0:T(8,128)(2,1)S(1)}, u32[]{:S(2)}, u32[]{:S(2)}) %collective-permute-start) | collective-permute-done | bytes 262176 | tf_op jit(solution)/shard_map/ppermute | solution.py:413
  75.5 13.6 %neighbours.1 = (bf16[256,128]{1,0:T(8,128)(2,1)S(1)}, bf16[512,128]{1,0:T(8,128)(2,1)S(1)}) custom-call(s32[256]{0:T(256)} %refs_0_.3, s32[16384]{0:T(1024)S(1)} %bitcast.22, s32[16384]{0:T(1024)S(1)} %bitcast.23, s32[16384]{0:T(1024)S(1)} %bitcast.24, s32[16384]{0:T(1024)S(1)} %bitcast.25, s32[16384]{0:T(1024)S(1)} %bitcast.26, s32[16384]{0:T(1024)S(1)} %bitcast.27, ...), custom_call_target="tpu_custom_call" | custom-call | tf_op jit(solution)/shard_map/neighbours/pallas_call | solution.py:453
  89.1 12.3 %all_to_all.81 = bf16[32,16,128]{2,1,0:T(8,128)(2,1)S(1)} all-to-all(bf16[32,16,128]{2,1,0:T(8,128)(2,1)S(1)} %bitcast.53), channel_id=1, replica_groups=mesh['xlo'=2,'z'=8,'core'=2,'y'=4,'xhi'=2] {'xlo','core','y','xhi'}, dimensions={0} | all-to-all | bytes 262144 | tf_op jit(solution)/shard_map/all_to_all | solution.py:339
  101.5 9.5 %all_to_all.82 = f32[8,16,128]{2,1,0:T(8,128)S(1)} all-to-all(f32[8,16,128]{2,1,0:T(8,128)S(1)} %bitcast.50), channel_id=1, replica_groups=mesh['xlo'=2,'z'=8,'core'=2,'y'=4,'xhi'=2] {'z'}, dimensions={0} | all-to-all | bytes 131072 | tf_op jit(solution)/shard_map/all_to_all | solution.py:341
  111.0 0.7 shard_map.143
  111.7 5.2 %all-to-all-start.6 = ((bf16[32,16,128]{2,1,0:T(8,128)(2,1)}), bf16[32,16,128]{2,1,0:T(8,128)(2,1)S(1)}, u32[]{:S(2)}, u32[]{:S(2)}) async-start(bf16[32,16,128]{2,1,0:T(8,128)(2,1)} %bitcast.18), calls=%async_computation.6 | async-start | bytes 262144 | tf_op jit(solution)/shard_map/all_to_all | solution.py:343
  116.9 0.8 force_first.1.force_in
  117.7 6.9 %all-to-all-done.6 = bf16[32,16,128]{2,1,0:T(8,128)(2,1)S(1)} async-done(((bf16[32,16,128]{2,1,0:T(8,128)(2,1)}), bf16[32,16,128]{2,1,0:T(8,128)(2,1)S(1)}, u32[]{:S(2)}, u32[]{:S(2)}) %all-to-all-start.6) | async-done | bytes 131104 | tf_op jit(solution)/shard_map/all_to_all | solution.py:343
  124.6 1.9 %project_second.1 = (bf16[256,128]{1,0:T(8,128)(2,1)}, f32[3,256]{1,0:T(4,128)}) custom-call(bf16[512,128]{1,0:T(8,128)(2,1)S(1)} %bitcast.43, bf16[256,2048]{1,0:T(8,128)(2,1)S(1)} %get-tuple-element.26.cos_ref.refs_23_, bf16[256,2048]{1,0:T(8,128)(2,1)S(1)} %get-tuple-element.27.sin_ref.refs_24_, f32[3,2048]{1,0:T(4,128)S(1)} %get-tuple-element.40.refs_25_.wave_ref, ...), custom_call_target="tpu_custom_call" | custom-call | tf_op jit(solution)/shard_map/project_second/pallas_call | solution.py:479
  (4 shorter events, 0.1 us)
Async XLA Ops:
  0.6 72.1 %copy-start = (s32[256,64]{0,1:T(8,128)S(1)}, s32[256,64]{0,1:T(8,128)}, u32[]{:S(2)}) copy-start(s32[256,64]{0,1:T(8,128)} %param.15) | copy-start | bytes 196612
  67.5 5.3 %collective-permute-start.1 = (bf16[1024,128]{1,0:T(8,128)(2,1)S(1)}, bf16[1024,128]{1,0:T(8,128)(2,1)S(1)}, u32[]{:S(2)}, u32[]{:S(2)}) collective-permute-start(bf16[1024,128]{1,0:T(8,128)(2,1)S(1)} %halo_near.1), channel_id=1, source_target_pairs={{0,8},{8,0},{16,24},{24,16},{32,40},{40,32},{48,56},{56,48},{64,72... | collective-permute-start | bytes 786440 | tf_op jit(solution)/shard_map/ppermute | solution.py:422
  69.4 6.1 %collective-permute-start = (bf16[1024,128]{1,0:T(8,128)(2,1)S(1)}, bf16[1024,128]{1,0:T(8,128)(2,1)S(1)}, u32[]{:S(2)}, u32[]{:S(2)}) collective-permute-start(bf16[1024,128]{1,0:T(8,128)(2,1)S(1)} %halo_far.1), channel_id=1, source_target_pairs={{0,248},{8,16},{16,8},{24,32},{32,24},{40,48},{48,40},{56,64},{64,... | collective-permute-start | bytes 786440 | tf_op jit(solution)/shard_map/ppermute | solution.py:413
  111.7 12.9 %all-to-all-start.6 = ((bf16[32,16,128]{2,1,0:T(8,128)(2,1)}), bf16[32,16,128]{2,1,0:T(8,128)(2,1)S(1)}, u32[]{:S(2)}, u32[]{:S(2)}) async-start(bf16[32,16,128]{2,1,0:T(8,128)(2,1)} %bitcast.18), calls=%async_computation.6 | async-start | bytes 262144 | tf_op jit(solution)/shard_map/all_to_all | solution.py:343

commit v9 on v6

--- a/solution.py
+++ b/solution.py
@@ -16,6 +16,8 @@
 EVERY = tuple(name for name, _ in PARTS)
 DOM = ("xlo", "z", "core")
 KV = ("y", "xhi")
+UNROLL = 2
+STEPS = 2
 LINE = ("z",)
 PLANE = ("xlo", "core", "y", "xhi")
 
@@ -209,11 +211,10 @@
     out_ref[...] = picked[...].astype(BF16)
 
 
-def weight_kernel(count_ref, dist_ref, wf_ref, out_ref, turned, near, taper, wide):
-    step = pl.program_id(0)
+def weight_kernel(count_ref, dist_ref, wf_ref, out_ref, turned, near, taper, wide, *, steps):
     slots, atoms = dist_ref.shape
     basis = wf_ref.shape[0]
-    pairs = out_ref.shape[0] // 2
+    pairs = atoms // 2 // steps
     sharpness = ((basis - 1) / 4.5) ** 2
 
     def paired(block):
@@ -222,26 +223,28 @@
             [turned[pl.ds(0, atoms // 2, stride=2), :], turned[pl.ds(1, atoms // 2, stride=2), :]], axis=1
         )
 
-    @pl.when(step == 0)
-    def _():
-        dist = dist_ref[...]
-        scaled = dist * 0.1
-        height = 0.5 * (horner(COS_COEF, scaled * scaled) + 1.0)
-        slot = lax.broadcasted_iota(jnp.int32, (slots, atoms), 0)
-        near[...] = paired(dist)
-        taper[...] = paired(jnp.where(slot < count_ref[...], height, 0.0))
-        wf_high = wf_ref[...].astype(BF16)
-        wide[0:basis, :] = wf_high
-        wide[basis : 2 * basis, :] = (wf_ref[...] - wf_high.astype(F32)).astype(BF16)
-
+    dist = dist_ref[...]
+    scaled = dist * 0.1
+    height = 0.5 * (horner(COS_COEF, scaled * scaled) + 1.0)
+    slot = lax.broadcasted_iota(jnp.int32, (slots, atoms), 0)
+    near[...] = paired(dist)
+    taper[...] = paired(jnp.where(slot < count_ref[...], height, 0.0))
+    wf_high = wf_ref[...].astype(BF16)
+    wide[0:basis, :] = wf_high
+    wide[basis : 2 * basis, :] = (wf_ref[...] - wf_high.astype(F32)).astype(BF16)
     centers = 0.5 + 4.5 / (basis - 1) * lax.broadcasted_iota(jnp.int32, (basis, 2 * slots), 0).astype(F32)
-    for p in range(pairs):
-        row = pl.ds(step * pairs + p, 1)
-        away = near[row, :] - centers
-        radial = (jnp.exp(-sharpness * (away * away)) * taper[row, :]).astype(BF16)
-        both = dot(jnp.concatenate([radial, radial], axis=0), wide[...], TN)
-        out_ref[2 * p] = both[:slots]
-        out_ref[2 * p + 1] = both[slots:]
+
+    def some_pairs(step, carry):
+        for p in range(pairs):
+            row = pl.ds(step * pairs + p, 1)
+            away = near[row, :] - centers
+            radial = (jnp.exp(-sharpness * (away * away)) * taper[row, :]).astype(BF16)
+            both = dot(jnp.concatenate([radial, radial], axis=0), wide[...], TN)
+            out_ref[2 * (step * pairs + p)] = both[:slots]
+            out_ref[2 * (step * pairs + p) + 1] = both[slots:]
+        return carry
+
+    lax.fori_loop(0, steps, some_pairs, 0)
 
 
 def neighbour_kernel(*refs, scale):
@@ -259,7 +262,12 @@
     table[pl.ds(pl.multiple_of(own + core * halo, 8), halo), :] = far_ref[...].astype(F32)
     bits = sublane_bits()
 
-    def one_atom(atom, carry):
+    def some_atoms(group, carry):
+        for k in range(UNROLL):
+            one_atom(group * UNROLL + k)
+        return carry
+
+    def one_atom(atom):
         at = pl.ds(pl.multiple_of(atom * 8, 8), 8)
         spots = [atom + q * atoms for q in range(4)]
 
@@ -277,9 +285,7 @@
         def _():
             sums[at, :] = sums[at, :] + some_slots(range(middle, slots // 8))
 
-        return carry
-
-    lax.fori_loop(0, atoms, one_atom, 0)
+    lax.fori_loop(0, atoms // UNROLL, some_atoms, 0)
     message = sums[pl.ds(0, atoms, stride=8), :]
     for k in range(1, 8):
         message = message + sums[pl.ds(k, atoms, stride=8), :]
@@ -343,7 +349,7 @@
 
     kept = (
         features, w_charge_first, wave_vectors, w_long_first, w_value, w_charge_second, w_long_second,
-        dist_t, nbr_count.reshape(1, atoms), w_filter,
+        dist_t, nbr_count.reshape(1, atoms), w_filter, lists,
     )
     cos_table, sin_table, part, *kept = pl.pallas_call(
         lambda *refs: table_kernel(*refs, scale=scale),
@@ -357,7 +363,7 @@
     )(*in_hbm(positions, *kept))
     (
         features, w_charge_first, wave_vectors, w_long_first, w_value, w_charge_second, w_long_second,
-        dist_t, count_row, w_filter,
+        dist_t, count_row, w_filter, lists,
     ) = kept
     sums = everything(part)
     hidden_first, values, force_first = pl.pallas_call(
@@ -383,7 +389,7 @@
             compiler_params=vmem(6),
             cost_estimate=pl.CostEstimate(flops=halo * hid, bytes_accessed=4 * kv * atoms * hid, transcendentals=0),
             name="halo_far" if far else "halo_near",
-        )(*in_hbm(*[lists] * (halo // 128)), source)
+        )(*[lists] * (halo // 128), source)
 
     to_far = halo_rows(True, v_dom)
     to_far, source, index_t = lax.optimization_barrier((to_far, v_dom, index_t))
@@ -391,17 +397,12 @@
     to_near = halo_rows(False, source)
     from_near = lax.ppermute(to_near, DOM, [(i, i + 1 - 2 * (i % 2)) for i in range(doms)])
 
-    steps = 8
-    whole = lambda dims: pl.BlockSpec(dims, lambda i: (0, 0))
+    whole = lambda dims: pl.BlockSpec(dims, lambda i: (0,) * len(dims))
     weights = pl.pallas_call(
-        weight_kernel,
-        grid=(steps,),
-        in_specs=[
-            whole((1, atoms)),
-            whole((slots, atoms)),
-            whole(w_filter.shape),
-        ],
-        out_specs=pl.BlockSpec((atoms // steps, slots, hid), lambda i: (i, 0, 0)),
+        lambda *refs: weight_kernel(*refs, steps=STEPS),
+        grid=(1,),
+        in_specs=[whole((1, atoms)), whole((slots, atoms)), whole(w_filter.shape)],
+        out_specs=whole((atoms, slots, hid)),
         out_shape=shape((atoms, slots, hid), F32),
         scratch_shapes=[
             pltpu.VMEM((atoms, slots), F32),
@@ -414,7 +415,7 @@
             bytes_accessed=atoms * slots * hid * 4,
             transcendentals=atoms * slots * 16,
         ),
-        compiler_params=vmem(6),
+        compiler_params=vmem(12),
         name="slot_weights",
     )(count_row, dist_t, w_filter)
 

time: 127 us -> 126 us (level)
  Pallas kernels: 28.9 us -> 26.4 us
  waiting for transfers between devices: 2.65 us -> 3.96 us
    ppermute x1, waiting for transfers between devices: 2.65 us -> 3.96 us  [local(): lax.ppermute(to_far, DOM, [(i, (i - 1 + 2 * (i % 2)) % doms) for i in ran...]
    pallas_call x1, Pallas kernels: 3.1 us -> 1.79 us  [local(): pl.pallas_call(lambda *refs: weight_kernel(*refs, steps=STEPS), grid=(1,)...]
  transfers between devices with their start and end apart: 2 -> 2, of which waited for: 1 -> 1; matrix products, arithmetic and copies ran while one was open for 0% -> 0% of each run, Pallas kernels for 2% -> 1%
where the time goes in v9:
time: 126 us; the launch traced here: 125 us
  blocking collectives  92 us (73%)
  Pallas kernels  26.4 us (21%)
  waiting for transfers between devices  3.96 us (3%)
  starting transfers between devices  2.18 us (2%)
    all_to_all x2, blocking collectives, everything(): share = lax.all_to_all(part, PLANE, 0, 0, tiled=True)  28.4 us
    all_to_all x2, blocking collectives, everything(): return lax.all_to_all(share, PLANE, 0, 0, tiled=True)  25.5 us
    all_to_all x2, blocking collectives, everything(): share = lax.all_to_all(share, LINE, 0, 0, tiled=True)  24.7 us
    pallas_call x1, Pallas kernels, local(): pl.pallas_call(lambda *refs: neighbour_kernel(*refs, scale=scale), grid=(...  13.6 us
    all_to_all x1, blocking collectives, local(): v_dom = lax.all_to_all(values, KV, 0, 0, tiled=True)  13.4 us
    pallas_call x1, Pallas kernels, local(): pl.pallas_call(lambda *refs: table_kernel(*refs, scale=scale), out_shape=...  4.32 us
    ppermute x1, waiting for transfers between devices, local(): lax.ppermute(to_far, DOM, [(i, (i - 1 + 2 * (i % 2)) % doms) for i in ran...  3.96 us
    pallas_call x2, Pallas kernels, halo_rows(): pl.pallas_call(lambda *refs: halo_kernel(*refs, far=far), grid=(1,), in_s...  3.17 us
  transfers between devices with their start and end apart: 2, of which 1 were waited for; matrix products, arithmetic and copies ran while one was open for 0% of the time, Pallas kernels for 1%

profile of v9, /device:TPU:1, one launch (start us, length us, event | category | flops | bytes accessed | tf_op | source)
XLA Modules:
  0.0 125.3 jit_solution(11610580560528823950)
XLA Ops:
  0.6 0.0 copy-start
  0.6 4.3 %tables.1 = (bf16[256,2048]{1,0:T(8,128)(2,1)S(1)}, bf16[256,2048]{1,0:T(8,128)(2,1)S(1)}, bf16[512,128]{1,0:T(8,128)(2,1)S(1)}, bf16[256,128]{1,0:T(8,128)(2,1)...) custom-call(f32[3,256]{1,0:T(4,128)} %refs_0_.2, ...), custom_call_target="tpu_custom_call" | custom-call | tf_op jit(solution)/shard_map/tables/pallas_call | solution.py:354
  5.0 16.0 %all_to_all.77 = bf16[32,16,128]{2,1,0:T(8,128)(2,1)S(1)} all-to-all(bf16[32,16,128]{2,1,0:T(8,128)(2,1)S(1)} %bitcast.52), channel_id=1, replica_groups=mesh['xlo'=2,'z'=8,'core'=2,'y'=4,'xhi'=2] {'xlo','core','y','xhi'}, dimensions={0} | all-to-all | bytes 262144 | tf_op jit(solution)/shard_map/all_to_all | solution.py:322
  21.1 15.2 %all_to_all.78 = f32[8,16,128]{2,1,0:T(8,128)S(1)} all-to-all(f32[8,16,128]{2,1,0:T(8,128)S(1)} %bitcast.48), channel_id=1, replica_groups=mesh['xlo'=2,'z'=8,'core'=2,'y'=4,'xhi'=2] {'z'}, dimensions={0} | all-to-all | bytes 131072 | tf_op jit(solution)/shard_map/all_to_all | solution.py:324
  36.3 12.8 %all_to_all.79 = bf16[32,16,128]{2,1,0:T(8,128)(2,1)S(1)} all-to-all(bf16[32,16,128]{2,1,0:T(8,128)(2,1)S(1)} %bitcast.45), channel_id=1, replica_groups=mesh['xlo'=2,'z'=8,'core'=2,'y'=4,'xhi'=2] {'xlo','core','y','xhi'}, dimensions={0} | all-to-all | bytes 262144 | tf_op jit(solution)/shard_map/all_to_all | solution.py:326
  49.1 1.4 %project_first.1 = (bf16[256,128]{1,0:T(8,128)(2,1)S(1)}, bf16[2048,128]{1,0:T(8,128)(2,1)S(1)}, f32[3,256]{1,0:T(4,128)S(1)}) custom-call(bf16[512,128]{1,0:T(8,128)(2,1)S(1)} %bitcast.42, bf16[256,2048]{1,0:T(8,128)(2,1)S(1)} %get-tuple-element.26.cos_ref.refs_23_, bf16[256,2048]{1,0:T(8,128)(2,1)S(1)} %get-tuple-element.27.sin_ref.refs_24_, ...), custom_call_target="tpu_custom_call" | custom-call | tf_op jit(solution)/shard_map/project_first/pallas_call | solution.py:369
  50.6 13.4 %all_to_all.80 = bf16[8,256,128]{2,1,0:T(8,128)(2,1)S(1)} all-to-all(bf16[8,256,128]{2,1,0:T(8,128)(2,1)S(1)} %bitcast.43), channel_id=1, replica_groups=mesh['xlo'=2,'z'=8,'core'=2,'y'=4,'xhi'=2] {'y','xhi'}, dimensions={0} | all-to-all | bytes 1048576 | tf_op jit(solution)/shard_map/all_to_all | solution.py:377
  63.9 1.6 %halo_far.1 = bf16[1024,128]{1,0:T(8,128)(2,1)S(1)} custom-call(s32[2,1024]{1,0:T(2,128)S(1)} %get-tuple-element.24.refs_0_.refs_1_.refs_2_.refs_3_.refs_4_.refs_5_.refs_6_.refs_7_, s32[2,1024]{1,0:T(2,128)S(1)} %get-tuple-element.24.refs_0_.refs_1_.refs_2_.refs_3_.refs_4_.refs_5_.refs_6_.refs_7_, ...), custom_call_target="tpu_custom_call" | custom-call | flops 131072 | bytes 1048576 | tf_op jit(solution)/shard_map/halo_far/pallas_call | solution.py:380
  65.5 1.6 %halo_near.1 = bf16[1024,128]{1,0:T(8,128)(2,1)S(1)} custom-call(s32[2,1024]{1,0:T(2,128)S(1)} %get-tuple-element.24.refs_0_.refs_1_.refs_2_.refs_3_.refs_4_.refs_5_.refs_6_.refs_7_, s32[2,1024]{1,0:T(2,128)S(1)} %get-tuple-element.24.refs_0_.refs_1_.refs_2_.refs_3_.refs_4_.refs_5_.refs_6_.refs_7_, ...), custom_call_target="tpu_custom_call" | custom-call | flops 131072 | bytes 1048576 | tf_op jit(solution)/shard_map/halo_near/pallas_call | solution.py:380
  67.1 1.9 %collective-permute-start.1 = (bf16[1024,128]{1,0:T(8,128)(2,1)S(1)}, bf16[1024,128]{1,0:T(8,128)(2,1)S(1)}, u32[]{:S(2)}, u32[]{:S(2)}) collective-permute-start(bf16[1024,128]{1,0:T(8,128)(2,1)S(1)} %halo_near.1), channel_id=1, source_target_pairs={{0,8},{8,0},{16,24},{24,16},{32,40},{40,32},{48,56},{56,48},{64,72... | collective-permute-start | bytes 786440 | tf_op jit(solution)/shard_map/ppermute | solution.py:398
  69.1 0.3 collective-permute-start
  69.3 1.8 %slot_weights.1.refs_17_ = f32[256,64,128]{2,1,0:T(8,128)S(1)} custom-call(s32[1,256]{1,0:T(1,128)S(1)} %get-tuple-element.35.refs_0_, f32[64,256]{1,0:T(8,128)S(1)} %get-tuple-element.36.refs_1_, f32[16,128]{1,0:T(8,128)S(1)} %get-tuple-element.37.refs_2_), custom_call_target="tpu_custom_call" | custom-call | flops 134217728 | bytes 8388608 | tf_op jit(solution)/shard_map/slot_weights/pallas_call | solution.py:401
  71.1 0.0 copy-done
  71.2 0.0 collective-permute-done.1.refs_20_
  71.2 4.0 %collective-permute-done.refs_19_ = bf16[1024,128]{1,0:T(8,128)(2,1)S(1)} collective-permute-done((bf16[1024,128]{1,0:T(8,128)(2,1)S(1)}, bf16[1024,128]{1,0:T(8,128)(2,1)S(1)}, u32[]{:S(2)}, u32[]{:S(2)}) %collective-permute-start) | collective-permute-done | bytes 262176 | tf_op jit(solution)/shard_map/ppermute | solution.py:396
  75.1 13.6 %neighbours.1 = (bf16[256,128]{1,0:T(8,128)(2,1)S(1)}, bf16[512,128]{1,0:T(8,128)(2,1)S(1)}) custom-call(s32[256]{0:T(256)} %refs_0_.3, s32[16384]{0:T(1024)S(1)} %bitcast.22, s32[16384]{0:T(1024)S(1)} %bitcast.23, s32[16384]{0:T(1024)S(1)} %bitcast.24, s32[16384]{0:T(1024)S(1)} %bitcast.25, s32[16384]{0:T(1024)S(1)} %bitcast.26, s32[16384]{0:T(1024)S(1)} %bitcast.27, ...), custom_call_target="tpu_custom_call" | custom-call | tf_op jit(solution)/shard_map/neighbours/pallas_call | solution.py:424
  88.8 12.3 %all_to_all.81 = bf16[32,16,128]{2,1,0:T(8,128)(2,1)S(1)} all-to-all(bf16[32,16,128]{2,1,0:T(8,128)(2,1)S(1)} %bitcast.53), channel_id=1, replica_groups=mesh['xlo'=2,'z'=8,'core'=2,'y'=4,'xhi'=2] {'xlo','core','y','xhi'}, dimensions={0} | all-to-all | bytes 262144 | tf_op jit(solution)/shard_map/all_to_all | solution.py:322
  101.2 9.5 %all_to_all.82 = f32[8,16,128]{2,1,0:T(8,128)S(1)} all-to-all(f32[8,16,128]{2,1,0:T(8,128)S(1)} %bitcast.50), channel_id=1, replica_groups=mesh['xlo'=2,'z'=8,'core'=2,'y'=4,'xhi'=2] {'z'}, dimensions={0} | all-to-all | bytes 131072 | tf_op jit(solution)/shard_map/all_to_all | solution.py:324
  110.7 12.7 %all_to_all.83 = bf16[32,16,128]{2,1,0:T(8,128)(2,1)S(1)} all-to-all(bf16[32,16,128]{2,1,0:T(8,128)(2,1)S(1)} %bitcast.47), channel_id=1, replica_groups=mesh['xlo'=2,'z'=8,'core'=2,'y'=4,'xhi'=2] {'xlo','core','y','xhi'}, dimensions={0} | all-to-all | bytes 262144 | tf_op jit(solution)/shard_map/all_to_all | solution.py:326
  123.4 1.9 %project_second.1 = (bf16[256,128]{1,0:T(8,128)(2,1)}, f32[3,256]{1,0:T(4,128)}) custom-call(bf16[512,128]{1,0:T(8,128)(2,1)S(1)} %bitcast.41, bf16[256,2048]{1,0:T(8,128)(2,1)S(1)} %get-tuple-element.26.cos_ref.refs_23_, bf16[256,2048]{1,0:T(8,128)(2,1)S(1)} %get-tuple-element.27.sin_ref.refs_24_, f32[3,2048]{1,0:T(4,128)S(1)} %get-tuple-element.28.wave_ref.refs_25_, ...), custom_call_target="tpu_custom_call" | custom-call | tf_op jit(solution)/shard_map/project_second/pallas_call | solution.py:450
  (5 shorter events, 0.2 us)
Async XLA Ops:
  0.6 70.5 %copy-start = (s32[256,64]{0,1:T(8,128)S(1)}, s32[256,64]{0,1:T(8,128)}, u32[]{:S(2)}) copy-start(s32[256,64]{0,1:T(8,128)} %param.15) | copy-start | bytes 196612
  67.1 4.0 %collective-permute-start.1 = (bf16[1024,128]{1,0:T(8,128)(2,1)S(1)}, bf16[1024,128]{1,0:T(8,128)(2,1)S(1)}, u32[]{:S(2)}, u32[]{:S(2)}) collective-permute-start(bf16[1024,128]{1,0:T(8,128)(2,1)S(1)} %halo_near.1), channel_id=1, source_target_pairs={{0,8},{8,0},{16,24},{24,16},{32,40},{40,32},{48,56},{56,48},{64,72... | collective-permute-start | bytes 786440 | tf_op jit(solution)/shard_map/ppermute | solution.py:398
  69.1 6.1 %collective-permute-start = (bf16[1024,128]{1,0:T(8,128)(2,1)S(1)}, bf16[1024,128]{1,0:T(8,128)(2,1)S(1)}, u32[]{:S(2)}, u32[]{:S(2)}) collective-permute-start(bf16[1024,128]{1,0:T(8,128)(2,1)S(1)} %halo_far.1), channel_id=1, source_target_pairs={{0,248},{8,16},{16,8},{24,32},{32,24},{40,48},{48,40},{56,64},{64,... | collective-permute-start | bytes 786440 | tf_op jit(solution)/shard_map/ppermute | solution.py:396

commit v10 on v9

--- a/solution.py
+++ b/solution.py
@@ -17,6 +17,7 @@
 DOM = ("xlo", "z", "core")
 KV = ("y", "xhi")
 UNROLL = 2
+TILES = 4
 STEPS = 2
 LINE = ("z",)
 PLANE = ("xlo", "core", "y", "xhi")
@@ -98,7 +99,7 @@
         turns[c] = jnp.broadcast_to(columns[:, c : c + 1], (atoms, 128))
     rows = 64
 
-    def one_tile(t, carry):
+    def one_tile(t):
         lanes = pl.ds(pl.multiple_of(t * 128, 128), 128)
         whole = jnp.round(wave_ref[:, lanes] * (CELL / (2.0 * math.pi)))
         for b in range(atoms // rows):
@@ -112,9 +113,13 @@
             v = u * u
             cos_ref[at, lanes] = horner(COS_COEF, v).astype(BF16)
             sin_ref[at, lanes] = (u * horner(SIN_COEF, v)).astype(BF16)
+
+    def some_tiles(g, carry):
+        for k in range(TILES):
+            one_tile(g * TILES + k)
         return carry
 
-    lax.fori_loop(0, waves // 128, one_tile, 0)
+    lax.fori_loop(0, waves // 128 // TILES, some_tiles, 0)
     charge_t = dot(wc_ref[...], feat_ref[...], NT)
     structure_part(charge_t, cos_ref, sin_ref, wave_ref, part_ref, scale)
 
@@ -194,16 +199,25 @@
 
 
 def halo_kernel(*refs, far):
-    lists, (values_ref, out_ref, table, picked) = refs[:-4], refs[-4:]
+    list_ref, values_ref, out_ref, table, picked, arrived = refs[:6]
+    lists = refs[6:]
+    fetches = [
+        pltpu.make_async_copy(list_ref.at[:, pl.ds(b * 128, 128)], part_ref, arrived.at[b])
+        for b, part_ref in enumerate(lists)
+    ]
+    for fetch in fetches:
+        fetch.start()
     core = lax.axis_index("core")
     side = 1 - core if far else core
     table[0 : values_ref.shape[0], :] = values_ref[...].astype(F32)
     bits = sublane_bits()
+    for fetch in fetches:
+        fetch.wait()
 
     def some_rows(g, carry):
         first = g * 8
-        for b, list_ref in enumerate(lists):
-            rows = [list_ref[side, first + j] for j in range(8)]
+        for b, part_ref in enumerate(lists):
+            rows = [part_ref[side, first + j] for j in range(8)]
             picked[pl.ds(pl.multiple_of(b * 128 + first, 8), 8), :] = row_tile(table, rows, bits)
         return carry
 
@@ -248,11 +262,18 @@
 
 
 def neighbour_kernel(*refs, scale):
-    count_ref, index_refs = refs[0], refs[1:-13]
     (
-        weight_ref, values_ref, far_ref, near_ref, hidden_ref, wc_ref, cos_ref, sin_ref, wave_ref,
-        hidden_out, part_ref, table, sums,
-    ) = refs[-13:]
+        count_ref, list_ref, weight_ref, values_ref, far_ref, near_ref, hidden_ref, wc_ref, cos_ref, sin_ref, wave_ref,
+        hidden_out, part_ref, table, sums, arrived,
+    ) = refs[:16]
+    index_refs = refs[16:]
+    size = index_refs[0].shape[0]
+    fetches = [
+        pltpu.make_async_copy(list_ref.at[pl.ds(b * size, size)], index_ref, arrived.at[b])
+        for b, index_ref in enumerate(index_refs)
+    ]
+    for fetch in fetches:
+        fetch.start()
     own = values_ref.shape[0]
     halo = far_ref.shape[0]
     atoms, slots, _ = weight_ref.shape
@@ -261,6 +282,8 @@
     table[pl.ds(pl.multiple_of(own + (1 - core) * halo, 8), halo), :] = near_ref[...].astype(F32)
     table[pl.ds(pl.multiple_of(own + core * halo, 8), halo), :] = far_ref[...].astype(F32)
     bits = sublane_bits()
+    for fetch in fetches:
+        fetch.wait()
 
     def some_atoms(group, carry):
         for k in range(UNROLL):
@@ -380,16 +403,18 @@
         return pl.pallas_call(
             lambda *refs: halo_kernel(*refs, far=far),
             grid=(1,),
-            in_specs=[
-                pl.BlockSpec((2, 128), lambda i, b=b: (0, b), memory_space=pltpu.SMEM) for b in range(halo // 128)
-            ] + [pl.BlockSpec((kv * atoms, hid), lambda i: (0, 0))],
+            in_specs=[pl.BlockSpec(memory_space=pl.ANY), pl.BlockSpec((kv * atoms, hid), lambda i: (0, 0))],
             out_specs=pl.BlockSpec((halo, hid), lambda i: (0, 0)),
             out_shape=shape((halo, hid), BF16),
-            scratch_shapes=[pltpu.VMEM((kv * atoms + 8, hid), F32), pltpu.VMEM((halo, hid), F32)],
+            scratch_shapes=[
+                pltpu.VMEM((kv * atoms + 8, hid), F32),
+                pltpu.VMEM((halo, hid), F32),
+                pltpu.SemaphoreType.DMA((halo // 128,)),
+            ] + [pltpu.SMEM((2, 128), jnp.int32)] * (halo // 128),
             compiler_params=vmem(6),
             cost_estimate=pl.CostEstimate(flops=halo * hid, bytes_accessed=4 * kv * atoms * hid, transcendentals=0),
             name="halo_far" if far else "halo_near",
-        )(*[lists] * (halo // 128), source)
+        )(lists, source)
 
     to_far = halo_rows(True, v_dom)
     to_far, source, index_t = lax.optimization_barrier((to_far, v_dom, index_t))
@@ -419,14 +444,14 @@
         name="slot_weights",
     )(count_row, dist_t, w_filter)
 
-    blocks = range(slots // 4)
+    blocks = slots // 4
     index_flat = index_t.reshape(slots * atoms)
     hidden_second, part = pl.pallas_call(
         lambda *refs: neighbour_kernel(*refs, scale=scale),
         grid=(1,),
-        in_specs=[smem] + [
-            pl.BlockSpec((4 * atoms,), lambda i, at=at: (at,), memory_space=pltpu.SMEM) for at in blocks
-        ] + [
+        in_specs=[
+            smem,
+            pl.BlockSpec(memory_space=pl.ANY),
             pl.BlockSpec((atoms, slots, hid), lambda i: (0, 0, 0)),
             whole((kv * atoms, hid)),
             whole((halo, hid)),
@@ -439,11 +464,15 @@
         ],
         out_specs=(whole((atoms, hid)), whole((part_rows, 128))),
         out_shape=(shape((atoms, hid), BF16), shape((part_rows, 128), BF16)),
-        scratch_shapes=[pltpu.VMEM((kv * atoms + 2 * halo + 8, hid), F32), pltpu.VMEM((8 * atoms, hid), F32)],
+        scratch_shapes=[
+            pltpu.VMEM((kv * atoms + 2 * halo + 8, hid), F32),
+            pltpu.VMEM((8 * atoms, hid), F32),
+            pltpu.SemaphoreType.DMA((blocks,)),
+        ] + [pltpu.SMEM((4 * atoms,), jnp.int32)] * blocks,
         compiler_params=vmem(20),
         name="neighbours",
     )(
-        *in_hbm(nbr_count), *[index_flat] * len(blocks), weights, v_dom, from_far, from_near,
+        *in_hbm(nbr_count), index_flat, weights, v_dom, from_far, from_near,
         hidden_first, w_charge_second, cos_table, sin_table, wave_vectors,
     )
     sums = everything(part)

time: 126 us -> 126 us (level)
  no operation moved by 1% of the time
where the time goes in v10:
time: 126 us
  blocking collectives  92 us (73%)
  Pallas kernels  26.7 us (21%)
  waiting for transfers between devices  3.96 us (3%)
  starting transfers between devices  2.18 us (2%)
    all_to_all x2, blocking collectives, everything(): share = lax.all_to_all(part, PLANE, 0, 0, tiled=True)  28.4 us
    all_to_all x2, blocking collectives, everything(): return lax.all_to_all(share, PLANE, 0, 0, tiled=True)  25.5 us
    all_to_all x2, blocking collectives, everything(): share = lax.all_to_all(share, LINE, 0, 0, tiled=True)  24.7 us
    pallas_call x1, Pallas kernels, local(): pl.pallas_call(lambda *refs: neighbour_kernel(*refs, scale=scale), grid=(...  14.2 us
    all_to_all x1, blocking collectives, local(): v_dom = lax.all_to_all(values, KV, 0, 0, tiled=True)  13.4 us
    pallas_call x1, Pallas kernels, local(): pl.pallas_call(lambda *refs: table_kernel(*refs, scale=scale), out_shape=...  4.14 us
    ppermute x1, waiting for transfers between devices, local(): lax.ppermute(to_far, DOM, [(i, (i - 1 + 2 * (i % 2)) % doms) for i in ran...  3.96 us
    pallas_call x2, Pallas kernels, halo_rows(): pl.pallas_call(lambda *refs: halo_kernel(*refs, far=far), grid=(1,), in_s...  3.17 us
  transfers between devices with their start and end apart: 2, of which 1 were waited for; matrix products, arithmetic and copies ran while one was open for 0% of the time, Pallas kernels for 1%

profile of v10, /device:TPU:1, one launch (start us, length us, event | category | flops | bytes accessed | tf_op | source)
XLA Modules:
  0.0 125.7 jit_solution(14640935909785651818)
XLA Ops:
  0.6 0.0 copy-start
  0.6 4.1 %tables.1 = (bf16[256,2048]{1,0:T(8,128)(2,1)S(1)}, bf16[256,2048]{1,0:T(8,128)(2,1)S(1)}, bf16[512,128]{1,0:T(8,128)(2,1)S(1)}, bf16[256,128]{1,0:T(8,128)(2,1)...) custom-call(f32[3,256]{1,0:T(4,128)} %refs_0_.2, ...), custom_call_target="tpu_custom_call" | custom-call | tf_op jit(solution)/shard_map/tables/pallas_call | solution.py:377
  4.8 16.0 %all_to_all.77 = bf16[32,16,128]{2,1,0:T(8,128)(2,1)S(1)} all-to-all(bf16[32,16,128]{2,1,0:T(8,128)(2,1)S(1)} %bitcast.37), channel_id=1, replica_groups=mesh['xlo'=2,'z'=8,'core'=2,'y'=4,'xhi'=2] {'xlo','core','y','xhi'}, dimensions={0} | all-to-all | bytes 262144 | tf_op jit(solution)/shard_map/all_to_all | solution.py:345
  20.9 15.2 %all_to_all.78 = f32[8,16,128]{2,1,0:T(8,128)S(1)} all-to-all(f32[8,16,128]{2,1,0:T(8,128)S(1)} %bitcast.33), channel_id=1, replica_groups=mesh['xlo'=2,'z'=8,'core'=2,'y'=4,'xhi'=2] {'z'}, dimensions={0} | all-to-all | bytes 131072 | tf_op jit(solution)/shard_map/all_to_all | solution.py:347
  36.1 12.8 %all_to_all.79 = bf16[32,16,128]{2,1,0:T(8,128)(2,1)S(1)} all-to-all(bf16[32,16,128]{2,1,0:T(8,128)(2,1)S(1)} %bitcast.29), channel_id=1, replica_groups=mesh['xlo'=2,'z'=8,'core'=2,'y'=4,'xhi'=2] {'xlo','core','y','xhi'}, dimensions={0} | all-to-all | bytes 262144 | tf_op jit(solution)/shard_map/all_to_all | solution.py:349
  49.0 1.4 %project_first.1 = (bf16[256,128]{1,0:T(8,128)(2,1)S(1)}, bf16[2048,128]{1,0:T(8,128)(2,1)S(1)}, f32[3,256]{1,0:T(4,128)S(1)}) custom-call(bf16[512,128]{1,0:T(8,128)(2,1)S(1)} %bitcast.26, bf16[256,2048]{1,0:T(8,128)(2,1)S(1)} %get-tuple-element.26.cos_ref.refs_8_, bf16[256,2048]{1,0:T(8,128)(2,1)S(1)} %get-tuple-element.27.sin_ref.refs_9_, ...), custom_call_target="tpu_custom_call" | custom-call | tf_op jit(solution)/shard_map/project_first/pallas_call | solution.py:392
  50.4 13.4 %all_to_all.80 = bf16[8,256,128]{2,1,0:T(8,128)(2,1)S(1)} all-to-all(bf16[8,256,128]{2,1,0:T(8,128)(2,1)S(1)} %bitcast.27), channel_id=1, replica_groups=mesh['xlo'=2,'z'=8,'core'=2,'y'=4,'xhi'=2] {'y','xhi'}, dimensions={0} | all-to-all | bytes 1048576 | tf_op jit(solution)/shard_map/all_to_all | solution.py:400
  63.8 1.6 %halo_far.1 = bf16[1024,128]{1,0:T(8,128)(2,1)S(1)} custom-call(s32[2,1024]{1,0:T(2,128)S(1)} %get-tuple-element.24.refs_0_, bf16[2048,128]{1,0:T(8,128)(2,1)S(1)} %bitcast.22), custom_call_target="tpu_custom_call" | custom-call | flops 131072 | bytes 1048576 | tf_op jit(solution)/shard_map/halo_far/pallas_call | solution.py:403
  65.4 1.6 %halo_near.1 = bf16[1024,128]{1,0:T(8,128)(2,1)S(1)} custom-call(s32[2,1024]{1,0:T(2,128)S(1)} %get-tuple-element.24.refs_0_, bf16[2048,128]{1,0:T(8,128)(2,1)S(1)} %bitcast.23), custom_call_target="tpu_custom_call" | custom-call | flops 131072 | bytes 1048576 | tf_op jit(solution)/shard_map/halo_near/pallas_call | solution.py:403
  67.0 1.9 %collective-permute-start.1 = (bf16[1024,128]{1,0:T(8,128)(2,1)S(1)}, bf16[1024,128]{1,0:T(8,128)(2,1)S(1)}, u32[]{:S(2)}, u32[]{:S(2)}) collective-permute-start(bf16[1024,128]{1,0:T(8,128)(2,1)S(1)} %halo_near.1), channel_id=1, source_target_pairs={{0,8},{8,0},{16,24},{24,16},{32,40},{40,32},{48,56},{56,48},{64,72... | collective-permute-start | bytes 786440 | tf_op jit(solution)/shard_map/ppermute | solution.py:423
  68.9 0.3 collective-permute-start
  69.1 1.8 %slot_weights.1.refs_2_ = f32[256,64,128]{2,1,0:T(8,128)S(1)} custom-call(s32[1,256]{1,0:T(1,128)S(1)} %get-tuple-element.35.refs_0_, f32[64,256]{1,0:T(8,128)S(1)} %get-tuple-element.36.refs_1_, f32[16,128]{1,0:T(8,128)S(1)} %get-tuple-element.37.refs_2_), custom_call_target="tpu_custom_call" | custom-call | flops 134217728 | bytes 8388608 | tf_op jit(solution)/shard_map/slot_weights/pallas_call | solution.py:426
  70.9 0.0 copy-done
  71.0 0.0 collective-permute-done.1.refs_5_
  71.0 4.0 %collective-permute-done.refs_4_ = bf16[1024,128]{1,0:T(8,128)(2,1)S(1)} collective-permute-done((bf16[1024,128]{1,0:T(8,128)(2,1)S(1)}, bf16[1024,128]{1,0:T(8,128)(2,1)S(1)}, u32[]{:S(2)}, u32[]{:S(2)}) %collective-permute-start) | collective-permute-done | bytes 262176 | tf_op jit(solution)/shard_map/ppermute | solution.py:421
  75.0 14.2 %neighbours.1 = (bf16[256,128]{1,0:T(8,128)(2,1)S(1)}, bf16[512,128]{1,0:T(8,128)(2,1)S(1)}) custom-call(s32[256]{0:T(256)} %refs_0_.3, s32[16384]{0:T(1024)S(1)} %bitcast.32, f32[256,64,128]{2,1,0:T(8,128)S(1)} %slot_weights.1.refs_2_, bf16[2048,128]{1,0:T(8,128)(2,1)S(1)} %bitcast.24, bf16[1024,128]{1,0:T(8,128)(2,1)S(1)} %collective-permute-done.refs_4_, ...), custom_call_target="tpu_custom_call" | custom-call | tf_op jit(solution)/shard_map/neighbours/pallas_call | solution.py:449
  89.1 12.3 %all_to_all.81 = bf16[32,16,128]{2,1,0:T(8,128)(2,1)S(1)} all-to-all(bf16[32,16,128]{2,1,0:T(8,128)(2,1)S(1)} %bitcast.38), channel_id=1, replica_groups=mesh['xlo'=2,'z'=8,'core'=2,'y'=4,'xhi'=2] {'xlo','core','y','xhi'}, dimensions={0} | all-to-all | bytes 262144 | tf_op jit(solution)/shard_map/all_to_all | solution.py:345
  101.5 9.5 %all_to_all.82 = f32[8,16,128]{2,1,0:T(8,128)S(1)} all-to-all(f32[8,16,128]{2,1,0:T(8,128)S(1)} %bitcast.35), channel_id=1, replica_groups=mesh['xlo'=2,'z'=8,'core'=2,'y'=4,'xhi'=2] {'z'}, dimensions={0} | all-to-all | bytes 131072 | tf_op jit(solution)/shard_map/all_to_all | solution.py:347
  111.0 12.7 %all_to_all.83 = bf16[32,16,128]{2,1,0:T(8,128)(2,1)S(1)} all-to-all(bf16[32,16,128]{2,1,0:T(8,128)(2,1)S(1)} %bitcast.31), channel_id=1, replica_groups=mesh['xlo'=2,'z'=8,'core'=2,'y'=4,'xhi'=2] {'xlo','core','y','xhi'}, dimensions={0} | all-to-all | bytes 262144 | tf_op jit(solution)/shard_map/all_to_all | solution.py:349
  123.7 1.9 %project_second.1 = (bf16[256,128]{1,0:T(8,128)(2,1)}, f32[3,256]{1,0:T(4,128)}) custom-call(bf16[512,128]{1,0:T(8,128)(2,1)S(1)} %bitcast.25, bf16[256,2048]{1,0:T(8,128)(2,1)S(1)} %get-tuple-element.26.cos_ref.refs_8_, bf16[256,2048]{1,0:T(8,128)(2,1)S(1)} %get-tuple-element.27.sin_ref.refs_9_, f32[3,2048]{1,0:T(4,128)S(1)} %get-tuple-element.28.wave_ref.refs_10_, ...), custom_call_target="tpu_custom_call" | custom-call | tf_op jit(solution)/shard_map/project_second/pallas_call | solution.py:479
  (5 shorter events, 0.1 us)
Async XLA Ops:
  0.6 70.3 %copy-start = (s32[256,64]{0,1:T(8,128)S(1)}, s32[256,64]{0,1:T(8,128)}, u32[]{:S(2)}) copy-start(s32[256,64]{0,1:T(8,128)} %param.15) | copy-start | bytes 196612
  67.0 4.0 %collective-permute-start.1 = (bf16[1024,128]{1,0:T(8,128)(2,1)S(1)}, bf16[1024,128]{1,0:T(8,128)(2,1)S(1)}, u32[]{:S(2)}, u32[]{:S(2)}) collective-permute-start(bf16[1024,128]{1,0:T(8,128)(2,1)S(1)} %halo_near.1), channel_id=1, source_target_pairs={{0,8},{8,0},{16,24},{24,16},{32,40},{40,32},{48,56},{56,48},{64,72... | collective-permute-start | bytes 786440 | tf_op jit(solution)/shard_map/ppermute | solution.py:423
  68.9 6.1 %collective-permute-start = (bf16[1024,128]{1,0:T(8,128)(2,1)S(1)}, bf16[1024,128]{1,0:T(8,128)(2,1)S(1)}, u32[]{:S(2)}, u32[]{:S(2)}) collective-permute-start(bf16[1024,128]{1,0:T(8,128)(2,1)S(1)} %halo_far.1), channel_id=1, source_target_pairs={{0,248},{8,16},{16,8},{24,32},{32,24},{40,48},{48,40},{56,64},{64,... | collective-permute-start | bytes 786440 | tf_op jit(solution)/shard_map/ppermute | solution.py:421

commit v11 on v10

--- a/solution.py
+++ b/solution.py
@@ -198,11 +198,11 @@
     return [(sub & bit) != 0 for bit in (1, 2, 4)]
 
 
-def halo_kernel(*refs, far):
+def halo_kernel(*refs, far, skipped):
     list_ref, values_ref, out_ref, table, picked, arrived = refs[:6]
     lists = refs[6:]
     fetches = [
-        pltpu.make_async_copy(list_ref.at[:, pl.ds(b * 128, 128)], part_ref, arrived.at[b])
+        pltpu.make_async_copy(list_ref.at[:, pl.ds(skipped + b * 128, 128)], part_ref, arrived.at[b])
         for b, part_ref in enumerate(lists)
     ]
     for fetch in fetches:
@@ -263,10 +263,10 @@
 
 def neighbour_kernel(*refs, scale):
     (
-        count_ref, list_ref, weight_ref, values_ref, far_ref, near_ref, hidden_ref, wc_ref, cos_ref, sin_ref, wave_ref,
+        count_ref, list_ref, weight_ref, values_ref, far_a_ref, far_b_ref, near_ref, hidden_ref, wc_ref, cos_ref, sin_ref, wave_ref,
         hidden_out, part_ref, table, sums, arrived,
-    ) = refs[:16]
-    index_refs = refs[16:]
+    ) = refs[:17]
+    index_refs = refs[17:]
     size = index_refs[0].shape[0]
     fetches = [
         pltpu.make_async_copy(list_ref.at[pl.ds(b * size, size)], index_ref, arrived.at[b])
@@ -275,12 +275,13 @@
     for fetch in fetches:
         fetch.start()
     own = values_ref.shape[0]
-    halo = far_ref.shape[0]
+    halo = near_ref.shape[0]
     atoms, slots, _ = weight_ref.shape
     core = lax.axis_index("core")
     table[0:own, :] = values_ref[...].astype(F32)
     table[pl.ds(pl.multiple_of(own + (1 - core) * halo, 8), halo), :] = near_ref[...].astype(F32)
-    table[pl.ds(pl.multiple_of(own + core * halo, 8), halo), :] = far_ref[...].astype(F32)
+    table[pl.ds(pl.multiple_of(own + core * halo, 8), halo // 2), :] = far_a_ref[...].astype(F32)
+    table[pl.ds(pl.multiple_of(own + core * halo + halo // 2, 8), halo // 2), :] = far_b_ref[...].astype(F32)
     bits = sublane_bits()
     for fetch in fetches:
         fetch.wait()
@@ -399,29 +400,35 @@
 
     v_dom = lax.all_to_all(values, KV, 0, 0, tiled=True)
 
-    def halo_rows(far, source):
+    def halo_rows(far, source, first, count):
         return pl.pallas_call(
-            lambda *refs: halo_kernel(*refs, far=far),
+            lambda *refs: halo_kernel(*refs, far=far, skipped=first),
             grid=(1,),
             in_specs=[pl.BlockSpec(memory_space=pl.ANY), pl.BlockSpec((kv * atoms, hid), lambda i: (0, 0))],
-            out_specs=pl.BlockSpec((halo, hid), lambda i: (0, 0)),
-            out_shape=shape((halo, hid), BF16),
+            out_specs=pl.BlockSpec((count, hid), lambda i: (0, 0)),
+            out_shape=shape((count, hid), BF16),
             scratch_shapes=[
                 pltpu.VMEM((kv * atoms + 8, hid), F32),
-                pltpu.VMEM((halo, hid), F32),
-                pltpu.SemaphoreType.DMA((halo // 128,)),
-            ] + [pltpu.SMEM((2, 128), jnp.int32)] * (halo // 128),
+                pltpu.VMEM((count, hid), F32),
+                pltpu.SemaphoreType.DMA((count // 128,)),
+            ] + [pltpu.SMEM((2, 128), jnp.int32)] * (count // 128),
             compiler_params=vmem(6),
-            cost_estimate=pl.CostEstimate(flops=halo * hid, bytes_accessed=4 * kv * atoms * hid, transcendentals=0),
-            name="halo_far" if far else "halo_near",
+            cost_estimate=pl.CostEstimate(flops=count * hid, bytes_accessed=4 * kv * atoms * hid, transcendentals=0),
         )(lists, source)
 
-    to_far = halo_rows(True, v_dom)
-    to_far, source, index_t = lax.optimization_barrier((to_far, v_dom, index_t))
-    from_far = lax.ppermute(to_far, DOM, [(i, (i - 1 + 2 * (i % 2)) % doms) for i in range(doms)])
-    to_near = halo_rows(False, source)
-    from_near = lax.ppermute(to_near, DOM, [(i, i + 1 - 2 * (i % 2)) for i in range(doms)])
-
+    part_count = halo // 2
+    to_far = [(i, (i - 1 + 2 * (i % 2)) % doms) for i in range(doms)]
+    to_near = [(i, i + 1 - 2 * (i % 2)) for i in range(doms)]
+    rows_a = halo_rows(True, v_dom, 0, part_count)
+    rows_a, source, index_t = lax.optimization_barrier((rows_a, v_dom, index_t))
+    far_a = lax.ppermute(rows_a, DOM, to_far)
+    rows_b = halo_rows(True, source, part_count, part_count)
+    rows_b, source = lax.optimization_barrier((rows_b, source))
+    far_b = lax.ppermute(rows_b, DOM, to_far)
+    rows_near = halo_rows(False, source, 0, halo)
+    from_near = lax.ppermute(rows_near, DOM, to_near)
+
+    index_flat = index_t.reshape(slots * atoms)
     whole = lambda dims: pl.BlockSpec(dims, lambda i: (0,) * len(dims))
     weights = pl.pallas_call(
         lambda *refs: weight_kernel(*refs, steps=STEPS),
@@ -445,7 +452,6 @@
     )(count_row, dist_t, w_filter)
 
     blocks = slots // 4
-    index_flat = index_t.reshape(slots * atoms)
     hidden_second, part = pl.pallas_call(
         lambda *refs: neighbour_kernel(*refs, scale=scale),
         grid=(1,),
@@ -454,7 +460,8 @@
             pl.BlockSpec(memory_space=pl.ANY),
             pl.BlockSpec((atoms, slots, hid), lambda i: (0, 0, 0)),
             whole((kv * atoms, hid)),
-            whole((halo, hid)),
+            whole((part_count, hid)),
+            whole((part_count, hid)),
             whole((halo, hid)),
             whole((atoms, hid)),
             whole((chan, hid)),
@@ -472,7 +479,7 @@
         compiler_params=vmem(20),
         name="neighbours",
     )(
-        *in_hbm(nbr_count), index_flat, weights, v_dom, from_far, from_near,
+        *in_hbm(nbr_count), index_flat, weights, v_dom, far_a, far_b, from_near,
         hidden_first, w_charge_second, cos_table, sin_table, wave_vectors,
     )
     sums = everything(part)

time: 126 us -> 128 us (1.016)
  starting transfers between devices: 2.18 us -> 3.66 us
  waiting for transfers between devices: 3.96 us -> 2.49 us
    ppermute x2 -> x3, starting transfers between devices: 2.18 us -> 3.66 us  [the longest x1 1.91 us: local(): from_near = lax.ppermute(rows_near, DOM, to_near)]
    ppermute x2 -> x3, waiting for transfers between devices: 3.96 us -> 2.49 us  [the longest x1 1.7 us: local(): far_a = lax.ppermute(rows_a, DOM, to_far)]
    pallas_call x2 -> x3, Pallas kernels: 3.17 us -> 3.98 us  [halo_rows(): pl.pallas_call(lambda *refs: halo_kernel(*refs, far=far, skipped=first),...]
  transfers between devices with their start and end apart: 2 -> 3, of which waited for: 1 -> 2; matrix products, arithmetic and copies ran while one was open for 0% -> 0% of each run, Pallas kernels for 1% -> 1%
where the time goes in v11:
time: 128 us; the launch traced here: 127 us
  blocking collectives  92.8 us (72%)
  Pallas kernels  27.6 us (22%)
  starting transfers between devices  3.66 us (3%)
  waiting for transfers between devices  2.49 us (2%)
    all_to_all x2, blocking collectives, everything(): share = lax.all_to_all(part, PLANE, 0, 0, tiled=True)  28.4 us
    all_to_all x2, blocking collectives, everything(): return lax.all_to_all(share, PLANE, 0, 0, tiled=True)  25.7 us
    all_to_all x2, blocking collectives, everything(): share = lax.all_to_all(share, LINE, 0, 0, tiled=True)  25.4 us
    pallas_call x1, Pallas kernels, local(): pl.pallas_call(lambda *refs: neighbour_kernel(*refs, scale=scale), grid=(...  14.2 us
    all_to_all x1, blocking collectives, local(): v_dom = lax.all_to_all(values, KV, 0, 0, tiled=True)  13.4 us
    pallas_call x1, Pallas kernels, local(): pl.pallas_call(lambda *refs: table_kernel(*refs, scale=scale), out_shape=...  4.14 us
    pallas_call x3, Pallas kernels, halo_rows(): pl.pallas_call(lambda *refs: halo_kernel(*refs, far=far, skipped=first),...  3.98 us
  transfers between devices with their start and end apart: 3, of which 2 were waited for; matrix products, arithmetic and copies ran while one was open for 0% of the time, Pallas kernels for 1%

profile of v11, /device:TPU:1, one launch (start us, length us, event | category | flops | bytes accessed | tf_op | source)
XLA Modules:
  0.0 127.3 jit_solution(9820432289232399550)
XLA Ops:
  0.6 0.0 copy-start
  0.6 4.1 %tables.1 = (bf16[256,2048]{1,0:T(8,128)(2,1)S(1)}, bf16[256,2048]{1,0:T(8,128)(2,1)S(1)}, bf16[512,128]{1,0:T(8,128)(2,1)S(1)}, bf16[256,128]{1,0:T(8,128)(2,1)...) custom-call(f32[3,256]{1,0:T(4,128)} %refs_0_.2, ...), custom_call_target="tpu_custom_call" | custom-call | tf_op jit(solution)/shard_map/tables/pallas_call | solution.py:378
  4.8 16.0 %all_to_all.77 = bf16[32,16,128]{2,1,0:T(8,128)(2,1)S(1)} all-to-all(bf16[32,16,128]{2,1,0:T(8,128)(2,1)S(1)} %bitcast.38), channel_id=1, replica_groups=mesh['xlo'=2,'z'=8,'core'=2,'y'=4,'xhi'=2] {'xlo','core','y','xhi'}, dimensions={0} | all-to-all | bytes 262144 | tf_op jit(solution)/shard_map/all_to_all | solution.py:346
  20.9 15.2 %all_to_all.78 = f32[8,16,128]{2,1,0:T(8,128)S(1)} all-to-all(f32[8,16,128]{2,1,0:T(8,128)S(1)} %bitcast.34), channel_id=1, replica_groups=mesh['xlo'=2,'z'=8,'core'=2,'y'=4,'xhi'=2] {'z'}, dimensions={0} | all-to-all | bytes 131072 | tf_op jit(solution)/shard_map/all_to_all | solution.py:348
  36.1 12.8 %all_to_all.79 = bf16[32,16,128]{2,1,0:T(8,128)(2,1)S(1)} all-to-all(bf16[32,16,128]{2,1,0:T(8,128)(2,1)S(1)} %bitcast.30), channel_id=1, replica_groups=mesh['xlo'=2,'z'=8,'core'=2,'y'=4,'xhi'=2] {'xlo','core','y','xhi'}, dimensions={0} | all-to-all | bytes 262144 | tf_op jit(solution)/shard_map/all_to_all | solution.py:350
  49.0 1.4 %project_first.1 = (bf16[256,128]{1,0:T(8,128)(2,1)S(1)}, bf16[2048,128]{1,0:T(8,128)(2,1)S(1)}, f32[3,256]{1,0:T(4,128)S(1)}) custom-call(bf16[512,128]{1,0:T(8,128)(2,1)S(1)} %bitcast.27, bf16[256,2048]{1,0:T(8,128)(2,1)S(1)} %get-tuple-element.28.cos_ref.refs_9_, bf16[256,2048]{1,0:T(8,128)(2,1)S(1)} %get-tuple-element.29.sin_ref.refs_10_, ...), custom_call_target="tpu_custom_call" | custom-call | tf_op jit(solution)/shard_map/project_first/pallas_call | solution.py:393
  50.4 13.4 %all_to_all.80 = bf16[8,256,128]{2,1,0:T(8,128)(2,1)S(1)} all-to-all(bf16[8,256,128]{2,1,0:T(8,128)(2,1)S(1)} %bitcast.28), channel_id=1, replica_groups=mesh['xlo'=2,'z'=8,'core'=2,'y'=4,'xhi'=2] {'y','xhi'}, dimensions={0} | all-to-all | bytes 1048576 | tf_op jit(solution)/shard_map/all_to_all | solution.py:401
  63.8 1.2 shard_map.142
  65.0 1.2 shard_map.143
  66.2 1.6 %shard_map.144 = bf16[1024,128]{1,0:T(8,128)(2,1)S(1)} custom-call(s32[2,1024]{1,0:T(2,128)S(1)} %get-tuple-element.26.refs_0_, bf16[2048,128]{1,0:T(8,128)(2,1)S(1)} %bitcast.24), custom_call_target="tpu_custom_call" | custom-call | flops 131072 | bytes 1048576 | tf_op jit(solution)/shard_map/pallas_call | solution.py:404
  67.8 1.9 %collective-permute-start.2 = (bf16[1024,128]{1,0:T(8,128)(2,1)S(1)}, bf16[1024,128]{1,0:T(8,128)(2,1)S(1)}, u32[]{:S(2)}, u32[]{:S(2)}) collective-permute-start(bf16[1024,128]{1,0:T(8,128)(2,1)S(1)} %shard_map.144), channel_id=1, source_target_pairs={{0,8},{8,0},{16,24},{24,16},{32,40},{40,32},{48,56},{56,48},{64,72... | collective-permute-start | bytes 786440 | tf_op jit(solution)/shard_map/ppermute | solution.py:429
  69.7 0.3 collective-permute-start.1
  70.0 1.5 %collective-permute-start = (bf16[512,128]{1,0:T(8,128)(2,1)S(1)}, bf16[512,128]{1,0:T(8,128)(2,1)S(1)}, u32[]{:S(2)}, u32[]{:S(2)}) collective-permute-start(bf16[512,128]{1,0:T(8,128)(2,1)S(1)} %shard_map.142), channel_id=1, source_target_pairs={{0,248},{8,16},{16,8},{24,32},{32,24},{40,48},{48,40},{56,64},{64,... | collective-permute-start | bytes 393224 | tf_op jit(solution)/shard_map/ppermute | solution.py:424
  71.4 1.8 %slot_weights.1.refs_2_ = f32[256,64,128]{2,1,0:T(8,128)S(1)} custom-call(s32[1,256]{1,0:T(1,128)S(1)} %get-tuple-element.37.refs_0_, f32[64,256]{1,0:T(8,128)S(1)} %get-tuple-element.38.refs_1_, f32[16,128]{1,0:T(8,128)S(1)} %get-tuple-element.39.refs_2_), custom_call_target="tpu_custom_call" | custom-call | flops 134217728 | bytes 8388608 | tf_op jit(solution)/shard_map/slot_weights/pallas_call | solution.py:433
  73.2 0.0 copy-done
  73.3 0.8 collective-permute-done.1.refs_5_
  74.1 1.7 %collective-permute-done.refs_4_ = bf16[512,128]{1,0:T(8,128)(2,1)S(1)} collective-permute-done((bf16[512,128]{1,0:T(8,128)(2,1)S(1)}, bf16[512,128]{1,0:T(8,128)(2,1)S(1)}, u32[]{:S(2)}, u32[]{:S(2)}) %collective-permute-start) | collective-permute-done | bytes 131104 | tf_op jit(solution)/shard_map/ppermute | solution.py:424
  75.8 0.0 collective-permute-done.2.refs_6_
  75.8 14.2 %neighbours.1 = (bf16[256,128]{1,0:T(8,128)(2,1)S(1)}, bf16[512,128]{1,0:T(8,128)(2,1)S(1)}) custom-call(s32[256]{0:T(256)} %refs_0_.3, s32[16384]{0:T(1024)S(1)} %bitcast.33, f32[256,64,128]{2,1,0:T(8,128)S(1)} %slot_weights.1.refs_2_, bf16[2048,128]{1,0:T(8,128)(2,1)S(1)} %bitcast.25, bf16[512,128]{1,0:T(8,128)(2,1)S(1)} %collective-permute-done.refs_4_, ...), custom_call_target="tpu_custom_call" | custom-call | tf_op jit(solution)/shard_map/neighbours/pallas_call | solution.py:455
  90.0 12.3 %all_to_all.81 = bf16[32,16,128]{2,1,0:T(8,128)(2,1)S(1)} all-to-all(bf16[32,16,128]{2,1,0:T(8,128)(2,1)S(1)} %bitcast.39), channel_id=1, replica_groups=mesh['xlo'=2,'z'=8,'core'=2,'y'=4,'xhi'=2] {'xlo','core','y','xhi'}, dimensions={0} | all-to-all | bytes 262144 | tf_op jit(solution)/shard_map/all_to_all | solution.py:346
  102.3 10.2 %all_to_all.82 = f32[8,16,128]{2,1,0:T(8,128)S(1)} all-to-all(f32[8,16,128]{2,1,0:T(8,128)S(1)} %bitcast.36), channel_id=1, replica_groups=mesh['xlo'=2,'z'=8,'core'=2,'y'=4,'xhi'=2] {'z'}, dimensions={0} | all-to-all | bytes 131072 | tf_op jit(solution)/shard_map/all_to_all | solution.py:348
  112.6 12.8 %all_to_all.83 = bf16[32,16,128]{2,1,0:T(8,128)(2,1)S(1)} all-to-all(bf16[32,16,128]{2,1,0:T(8,128)(2,1)S(1)} %bitcast.32), channel_id=1, replica_groups=mesh['xlo'=2,'z'=8,'core'=2,'y'=4,'xhi'=2] {'xlo','core','y','xhi'}, dimensions={0} | all-to-all | bytes 262144 | tf_op jit(solution)/shard_map/all_to_all | solution.py:350
  125.4 1.9 %project_second.1 = (bf16[256,128]{1,0:T(8,128)(2,1)}, f32[3,256]{1,0:T(4,128)}) custom-call(bf16[512,128]{1,0:T(8,128)(2,1)S(1)} %bitcast.26, bf16[256,2048]{1,0:T(8,128)(2,1)S(1)} %get-tuple-element.28.cos_ref.refs_9_, bf16[256,2048]{1,0:T(8,128)(2,1)S(1)} %get-tuple-element.29.sin_ref.refs_10_, f32[3,2048]{1,0:T(4,128)S(1)} %get-tuple-element.30.wave_ref.refs_11_, ...), custom_call_target="tpu_custom_call" | custom-call | tf_op jit(solution)/shard_map/project_second/pallas_call | solution.py:486
  (5 shorter events, 0.1 us)
Async XLA Ops:
  0.6 72.6 %copy-start = (s32[256,64]{0,1:T(8,128)S(1)}, s32[256,64]{0,1:T(8,128)}, u32[]{:S(2)}) copy-start(s32[256,64]{0,1:T(8,128)} %param.15) | copy-start | bytes 196612
  67.8 8.0 %collective-permute-start.2 = (bf16[1024,128]{1,0:T(8,128)(2,1)S(1)}, bf16[1024,128]{1,0:T(8,128)(2,1)S(1)}, u32[]{:S(2)}, u32[]{:S(2)}) collective-permute-start(bf16[1024,128]{1,0:T(8,128)(2,1)S(1)} %shard_map.144), channel_id=1, source_target_pairs={{0,8},{8,0},{16,24},{24,16},{32,40},{40,32},{48,56},{56,48},{64,72... | collective-permute-start | bytes 786440 | tf_op jit(solution)/shard_map/ppermute | solution.py:429
  69.7 4.4 %collective-permute-start.1 = (bf16[512,128]{1,0:T(8,128)(2,1)S(1)}, bf16[512,128]{1,0:T(8,128)(2,1)S(1)}, u32[]{:S(2)}, u32[]{:S(2)}) collective-permute-start(bf16[512,128]{1,0:T(8,128)(2,1)S(1)} %shard_map.143), channel_id=1, source_target_pairs={{0,248},{8,16},{16,8},{24,32},{32,24},{40,48},{48,40},{56,64},{64,... | collective-permute-start | bytes 393224 | tf_op jit(solution)/shard_map/ppermute | solution.py:427
  70.0 5.8 %collective-permute-start = (bf16[512,128]{1,0:T(8,128)(2,1)S(1)}, bf16[512,128]{1,0:T(8,128)(2,1)S(1)}, u32[]{:S(2)}, u32[]{:S(2)}) collective-permute-start(bf16[512,128]{1,0:T(8,128)(2,1)S(1)} %shard_map.142), channel_id=1, source_target_pairs={{0,248},{8,16},{16,8},{24,32},{32,24},{40,48},{48,40},{56,64},{64,... | collective-permute-start | bytes 393224 | tf_op jit(solution)/shard_map/ppermute | solution.py:424

commit v12 on v9

--- a/solution.py
+++ b/solution.py
@@ -98,7 +98,7 @@
         turns[c] = jnp.broadcast_to(columns[:, c : c + 1], (atoms, 128))
     rows = 64
 
-    def one_tile(t, carry):
+    def one_tile(t):
         lanes = pl.ds(pl.multiple_of(t * 128, 128), 128)
         whole = jnp.round(wave_ref[:, lanes] * (CELL / (2.0 * math.pi)))
         for b in range(atoms // rows):
@@ -112,9 +112,13 @@
             v = u * u
             cos_ref[at, lanes] = horner(COS_COEF, v).astype(BF16)
             sin_ref[at, lanes] = (u * horner(SIN_COEF, v)).astype(BF16)
+
+    def some_tiles(g, carry):
+        for k in range(4):
+            one_tile(g * 4 + k)
         return carry
 
-    lax.fori_loop(0, waves // 128, one_tile, 0)
+    lax.fori_loop(0, waves // 512, some_tiles, 0)
     charge_t = dot(wc_ref[...], feat_ref[...], NT)
     structure_part(charge_t, cos_ref, sin_ref, wave_ref, part_ref, scale)
 
@@ -281,9 +285,16 @@
         middle = slots // 16
         sums[at, :] = some_slots(range(middle))
 
-        @pl.when(count_ref[atom] > middle * 8)
+        most = 3 * slots // 32
+        count = count_ref[atom]
+
+        @pl.when(count > most * 8)
         def _():
             sums[at, :] = sums[at, :] + some_slots(range(middle, slots // 8))
+
+        @pl.when((count > middle * 8) & (count <= most * 8))
+        def _():
+            sums[at, :] = sums[at, :] + some_slots(range(middle, most))
 
     lax.fori_loop(0, atoms // UNROLL, some_atoms, 0)
     message = sums[pl.ds(0, atoms, stride=8), :]

time: 126 us -> 126 us (level)
  no operation moved by 1% of the time
where the time goes in v12:
time: 126 us
  blocking collectives  91.9 us (73%)
  Pallas kernels  27 us (21%)
  waiting for transfers between devices  3.96 us (3%)
  starting transfers between devices  2.18 us (2%)
    all_to_all x2, blocking collectives, everything(): share = lax.all_to_all(part, PLANE, 0, 0, tiled=True)  28.3 us
    all_to_all x2, blocking collectives, everything(): return lax.all_to_all(share, PLANE, 0, 0, tiled=True)  25.5 us
    all_to_all x2, blocking collectives, everything(): share = lax.all_to_all(share, LINE, 0, 0, tiled=True)  24.7 us
    pallas_call x1, Pallas kernels, local(): pl.pallas_call(lambda *refs: neighbour_kernel(*refs, scale=scale), grid=(...  14.4 us
    all_to_all x1, blocking collectives, local(): v_dom = lax.all_to_all(values, KV, 0, 0, tiled=True)  13.4 us
    pallas_call x1, Pallas kernels, local(): pl.pallas_call(lambda *refs: table_kernel(*refs, scale=scale), out_shape=...  4.14 us
    ppermute x1, waiting for transfers between devices, local(): lax.ppermute(to_far, DOM, [(i, (i - 1 + 2 * (i % 2)) % doms) for i in ran...  3.96 us
    pallas_call x2, Pallas kernels, halo_rows(): pl.pallas_call(lambda *refs: halo_kernel(*refs, far=far), grid=(1,), in_s...  3.17 us
  transfers between devices with their start and end apart: 2, of which 1 were waited for; matrix products, arithmetic and copies ran while one was open for 0% of the time, Pallas kernels for 1%

profile of v12, /device:TPU:1, one launch (start us, length us, event | category | flops | bytes accessed | tf_op | source)
XLA Modules:
  0.0 125.9 jit_solution(17510808873758068651)
XLA Ops:
  0.6 0.0 copy-start
  0.6 4.1 %tables.1 = (bf16[256,2048]{1,0:T(8,128)(2,1)S(1)}, bf16[256,2048]{1,0:T(8,128)(2,1)S(1)}, bf16[512,128]{1,0:T(8,128)(2,1)S(1)}, bf16[256,128]{1,0:T(8,128)(2,1)...) custom-call(f32[3,256]{1,0:T(4,128)} %refs_0_.2, ...), custom_call_target="tpu_custom_call" | custom-call | tf_op jit(solution)/shard_map/tables/pallas_call | solution.py:365
  4.8 16.0 %all_to_all.77 = bf16[32,16,128]{2,1,0:T(8,128)(2,1)S(1)} all-to-all(bf16[32,16,128]{2,1,0:T(8,128)(2,1)S(1)} %bitcast.52), channel_id=1, replica_groups=mesh['xlo'=2,'z'=8,'core'=2,'y'=4,'xhi'=2] {'xlo','core','y','xhi'}, dimensions={0} | all-to-all | bytes 262144 | tf_op jit(solution)/shard_map/all_to_all | solution.py:333
  20.9 15.2 %all_to_all.78 = f32[8,16,128]{2,1,0:T(8,128)S(1)} all-to-all(f32[8,16,128]{2,1,0:T(8,128)S(1)} %bitcast.48), channel_id=1, replica_groups=mesh['xlo'=2,'z'=8,'core'=2,'y'=4,'xhi'=2] {'z'}, dimensions={0} | all-to-all | bytes 131072 | tf_op jit(solution)/shard_map/all_to_all | solution.py:335
  36.1 12.8 %all_to_all.79 = bf16[32,16,128]{2,1,0:T(8,128)(2,1)S(1)} all-to-all(bf16[32,16,128]{2,1,0:T(8,128)(2,1)S(1)} %bitcast.45), channel_id=1, replica_groups=mesh['xlo'=2,'z'=8,'core'=2,'y'=4,'xhi'=2] {'xlo','core','y','xhi'}, dimensions={0} | all-to-all | bytes 262144 | tf_op jit(solution)/shard_map/all_to_all | solution.py:337
  49.0 1.4 %project_first.1 = (bf16[256,128]{1,0:T(8,128)(2,1)S(1)}, bf16[2048,128]{1,0:T(8,128)(2,1)S(1)}, f32[3,256]{1,0:T(4,128)S(1)}) custom-call(bf16[512,128]{1,0:T(8,128)(2,1)S(1)} %bitcast.42, bf16[256,2048]{1,0:T(8,128)(2,1)S(1)} %get-tuple-element.26.cos_ref.refs_23_, bf16[256,2048]{1,0:T(8,128)(2,1)S(1)} %get-tuple-element.27.sin_ref.refs_24_, ...), custom_call_target="tpu_custom_call" | custom-call | tf_op jit(solution)/shard_map/project_first/pallas_call | solution.py:380
  50.4 13.4 %all_to_all.80 = bf16[8,256,128]{2,1,0:T(8,128)(2,1)S(1)} all-to-all(bf16[8,256,128]{2,1,0:T(8,128)(2,1)S(1)} %bitcast.43), channel_id=1, replica_groups=mesh['xlo'=2,'z'=8,'core'=2,'y'=4,'xhi'=2] {'y','xhi'}, dimensions={0} | all-to-all | bytes 1048576 | tf_op jit(solution)/shard_map/all_to_all | solution.py:388
  63.8 1.6 %halo_far.1 = bf16[1024,128]{1,0:T(8,128)(2,1)S(1)} custom-call(s32[2,1024]{1,0:T(2,128)S(1)} %get-tuple-element.24.refs_0_.refs_1_.refs_2_.refs_3_.refs_4_.refs_5_.refs_6_.refs_7_, s32[2,1024]{1,0:T(2,128)S(1)} %get-tuple-element.24.refs_0_.refs_1_.refs_2_.refs_3_.refs_4_.refs_5_.refs_6_.refs_7_, ...), custom_call_target="tpu_custom_call" | custom-call | flops 131072 | bytes 1048576 | tf_op jit(solution)/shard_map/halo_far/pallas_call | solution.py:391
  65.4 1.6 %halo_near.1 = bf16[1024,128]{1,0:T(8,128)(2,1)S(1)} custom-call(s32[2,1024]{1,0:T(2,128)S(1)} %get-tuple-element.24.refs_0_.refs_1_.refs_2_.refs_3_.refs_4_.refs_5_.refs_6_.refs_7_, s32[2,1024]{1,0:T(2,128)S(1)} %get-tuple-element.24.refs_0_.refs_1_.refs_2_.refs_3_.refs_4_.refs_5_.refs_6_.refs_7_, ...), custom_call_target="tpu_custom_call" | custom-call | flops 131072 | bytes 1048576 | tf_op jit(solution)/shard_map/halo_near/pallas_call | solution.py:391
  67.0 1.9 %collective-permute-start.1 = (bf16[1024,128]{1,0:T(8,128)(2,1)S(1)}, bf16[1024,128]{1,0:T(8,128)(2,1)S(1)}, u32[]{:S(2)}, u32[]{:S(2)}) collective-permute-start(bf16[1024,128]{1,0:T(8,128)(2,1)S(1)} %halo_near.1), channel_id=1, source_target_pairs={{0,8},{8,0},{16,24},{24,16},{32,40},{40,32},{48,56},{56,48},{64,72... | collective-permute-start | bytes 786440 | tf_op jit(solution)/shard_map/ppermute | solution.py:409
  68.9 0.3 collective-permute-start
  69.1 1.8 %slot_weights.1.refs_17_ = f32[256,64,128]{2,1,0:T(8,128)S(1)} custom-call(s32[1,256]{1,0:T(1,128)S(1)} %get-tuple-element.35.refs_0_, f32[64,256]{1,0:T(8,128)S(1)} %get-tuple-element.36.refs_1_, f32[16,128]{1,0:T(8,128)S(1)} %get-tuple-element.37.refs_2_), custom_call_target="tpu_custom_call" | custom-call | flops 134217728 | bytes 8388608 | tf_op jit(solution)/shard_map/slot_weights/pallas_call | solution.py:412
  70.9 0.0 copy-done
  71.0 0.0 collective-permute-done.1.refs_20_
  71.0 4.0 %collective-permute-done.refs_19_ = bf16[1024,128]{1,0:T(8,128)(2,1)S(1)} collective-permute-done((bf16[1024,128]{1,0:T(8,128)(2,1)S(1)}, bf16[1024,128]{1,0:T(8,128)(2,1)S(1)}, u32[]{:S(2)}, u32[]{:S(2)}) %collective-permute-start) | collective-permute-done | bytes 262176 | tf_op jit(solution)/shard_map/ppermute | solution.py:407
  75.0 14.4 %neighbours.1 = (bf16[256,128]{1,0:T(8,128)(2,1)S(1)}, bf16[512,128]{1,0:T(8,128)(2,1)S(1)}) custom-call(s32[256]{0:T(256)} %refs_0_.3, s32[16384]{0:T(1024)S(1)} %bitcast.22, s32[16384]{0:T(1024)S(1)} %bitcast.23, s32[16384]{0:T(1024)S(1)} %bitcast.24, s32[16384]{0:T(1024)S(1)} %bitcast.25, s32[16384]{0:T(1024)S(1)} %bitcast.26, s32[16384]{0:T(1024)S(1)} %bitcast.27, ...), custom_call_target="tpu_custom_call" | custom-call | tf_op jit(solution)/shard_map/neighbours/pallas_call | solution.py:435
  89.4 12.3 %all_to_all.81 = bf16[32,16,128]{2,1,0:T(8,128)(2,1)S(1)} all-to-all(bf16[32,16,128]{2,1,0:T(8,128)(2,1)S(1)} %bitcast.53), channel_id=1, replica_groups=mesh['xlo'=2,'z'=8,'core'=2,'y'=4,'xhi'=2] {'xlo','core','y','xhi'}, dimensions={0} | all-to-all | bytes 262144 | tf_op jit(solution)/shard_map/all_to_all | solution.py:333
  101.7 9.5 %all_to_all.82 = f32[8,16,128]{2,1,0:T(8,128)S(1)} all-to-all(f32[8,16,128]{2,1,0:T(8,128)S(1)} %bitcast.50), channel_id=1, replica_groups=mesh['xlo'=2,'z'=8,'core'=2,'y'=4,'xhi'=2] {'z'}, dimensions={0} | all-to-all | bytes 131072 | tf_op jit(solution)/shard_map/all_to_all | solution.py:335
  111.3 12.7 %all_to_all.83 = bf16[32,16,128]{2,1,0:T(8,128)(2,1)S(1)} all-to-all(bf16[32,16,128]{2,1,0:T(8,128)(2,1)S(1)} %bitcast.47), channel_id=1, replica_groups=mesh['xlo'=2,'z'=8,'core'=2,'y'=4,'xhi'=2] {'xlo','core','y','xhi'}, dimensions={0} | all-to-all | bytes 262144 | tf_op jit(solution)/shard_map/all_to_all | solution.py:337
  123.9 1.9 %project_second.1 = (bf16[256,128]{1,0:T(8,128)(2,1)}, f32[3,256]{1,0:T(4,128)}) custom-call(bf16[512,128]{1,0:T(8,128)(2,1)S(1)} %bitcast.41, bf16[256,2048]{1,0:T(8,128)(2,1)S(1)} %get-tuple-element.26.cos_ref.refs_23_, bf16[256,2048]{1,0:T(8,128)(2,1)S(1)} %get-tuple-element.27.sin_ref.refs_24_, f32[3,2048]{1,0:T(4,128)S(1)} %get-tuple-element.28.wave_ref.refs_25_, ...), custom_call_target="tpu_custom_call" | custom-call | tf_op jit(solution)/shard_map/project_second/pallas_call | solution.py:461
  (5 shorter events, 0.1 us)
Async XLA Ops:
  0.6 70.3 %copy-start = (s32[256,64]{0,1:T(8,128)S(1)}, s32[256,64]{0,1:T(8,128)}, u32[]{:S(2)}) copy-start(s32[256,64]{0,1:T(8,128)} %param.15) | copy-start | bytes 196612
  67.0 4.0 %collective-permute-start.1 = (bf16[1024,128]{1,0:T(8,128)(2,1)S(1)}, bf16[1024,128]{1,0:T(8,128)(2,1)S(1)}, u32[]{:S(2)}, u32[]{:S(2)}) collective-permute-start(bf16[1024,128]{1,0:T(8,128)(2,1)S(1)} %halo_near.1), channel_id=1, source_target_pairs={{0,8},{8,0},{16,24},{24,16},{32,40},{40,32},{48,56},{56,48},{64,72... | collective-permute-start | bytes 786440 | tf_op jit(solution)/shard_map/ppermute | solution.py:409
  68.9 6.1 %collective-permute-start = (bf16[1024,128]{1,0:T(8,128)(2,1)S(1)}, bf16[1024,128]{1,0:T(8,128)(2,1)S(1)}, u32[]{:S(2)}, u32[]{:S(2)}) collective-permute-start(bf16[1024,128]{1,0:T(8,128)(2,1)S(1)} %halo_far.1), channel_id=1, source_target_pairs={{0,248},{8,16},{16,8},{24,32},{32,24},{40,48},{48,40},{56,64},{64,... | collective-permute-start | bytes 786440 | tf_op jit(solution)/shard_map/ppermute | solution.py:407
